TPU v7x, 128 devices: a whole 4x4x4 slice. The times are simulated.
128 devices in a mesh: tm: 8 (over y, z_lo), dp: 16 (over x, z_hi, core).
Axes of the slice: x: 4, y: 4, z: 4 (z_hi: 2, z_lo: 2; z = z_hi * 2 + z_lo), core: 2. Of those that a mesh axis runs over, the one named last changes fastest.
Arguments:
- features: bfloat16 [16, 16, 16, 24, 384], P('dp', 'tm'), may hold values from -60 to 60
- conv_weight: bfloat16 [10368, 384], replicated, may hold values from -0.0625 to 0.0625
- up_weight: bfloat16 [1152, 768], replicated, may hold values from -0.1875 to 0.1875
- cotangent: bfloat16 [16, 32, 16, 24, 384], P('dp', 'tm'), may hold values from -6 to 6
Outputs:
- features_grad: bfloat16 [16, 16, 16, 24, 384], P('dp', 'tm')
- grad_conv: float32 [10368, 384], P('dp', 'tm')
- grad_up: float32 [1152, 768], P('dp', 'tm')
All inputs are finite; a program needn't handle non-finite values.
Results may differ from a plain program's by a relative error of at most 0.0049.
Values may be sent and summed in bfloat16 or wider, within the bound.
No kernel may reach another device: no remote copies, remote signals or barrier semaphores. Data moves between devices by JAX's collectives and lax.ppermute only.
A program may use at most 128 MiB of HBM per device.

v0:
```python
import math

import jax
import jax.numpy as jnp
from jax import lax
from jax.sharding import PartitionSpec as P

G = 32


EPSILON = 1e-06


def from_behind(value, axis, steps):
    count = lax.axis_size(axis)
    first, last = (max(0, -steps), min(count, count - steps))
    return lax.ppermute(value, axis, [(source, source + steps) for source in range(first, last)])


def norm_act(field):
    shape = field.shape
    grouped = field.reshape(shape[:-3] + (shape[-3] * shape[-2], G, shape[-1] // G))
    center = grouped - jnp.mean(grouped, axis=(-3, -1), keepdims=True)
    spread = jnp.mean(center * center, axis=(-3, -1), keepdims=True)
    normed = center * lax.rsqrt(spread + EPSILON)
    return jax.nn.silu(normed).reshape(shape)


def space_pad(field):
    return jnp.pad(field, ((0, 0), (0, 0), (1, 1), (1, 1), (0, 0)))


def stack_taps(padded, frames, height, breadth):
    pieces = [
        padded[
            :,
            time_tap : time_tap + frames,
            high_tap : high_tap + height,
            wide_tap : wide_tap + breadth,
            :,
        ]
        for time_tap in range(3)
        for high_tap in range(3)
        for wide_tap in range(3)
    ]
    joined = jnp.concatenate(pieces, axis=-1)
    return joined.reshape(-1, joined.shape[-1])


def stack_times(padded, frames):
    pieces = [padded[:, time_tap : time_tap + frames] for time_tap in range(3)]
    joined = jnp.concatenate(pieces, axis=-1)
    return joined.reshape(-1, joined.shape[-1])


def contract_rows(left, right):
    return lax.dot_general(
        left, right, (((0,), (0,)), ((), ())), preferred_element_type=jnp.float32
    )


def shards(features, conv_weight, up_weight, cotangent):
    crop_count, frames, height, breadth, channels = features.shape
    block_shape = features.shape
    feature_field = features.astype(jnp.float32)
    act_float, pullback = jax.vjp(norm_act, feature_field)
    act = act_float.astype(jnp.bfloat16)
    act_prior = from_behind(act, "tm", 1)
    act_cols = stack_taps(
        space_pad(jnp.concatenate([act_prior, act], axis=1)), frames, height, breadth
    )
    conv_out = jnp.dot(act_cols, conv_weight, preferred_element_type=jnp.float32)
    hidden = (
        (feature_field.reshape(-1, channels) + conv_out).astype(jnp.bfloat16).reshape(block_shape)
    )
    hidden_prior = from_behind(hidden, "tm", 1)
    hidden_cols = stack_times(jnp.concatenate([hidden_prior, hidden], axis=1), frames)
    up_grad = cotangent.reshape(crop_count, frames, 2, height, breadth, channels)
    up_grad = up_grad.transpose(0, 1, 3, 4, 2, 5).reshape(
        crop_count, frames, height, breadth, 2 * channels
    )
    up_next = from_behind(up_grad, "tm", -1)
    up_cols = stack_times(jnp.concatenate([up_grad, up_next], axis=1), frames)
    up_flip = (
        up_weight.reshape(3, channels, 2 * channels)[::-1]
        .transpose(0, 2, 1)
        .reshape(6 * channels, channels)
    )
    hidden_grad = jnp.dot(up_cols, up_flip, preferred_element_type=jnp.float32)
    conv_grad = hidden_grad.astype(jnp.bfloat16)
    up_flat = up_grad.reshape(-1, 2 * channels)
    conv_field = conv_grad.reshape(block_shape)
    conv_next = from_behind(conv_field, "tm", -1)
    conv_cols = stack_taps(
        space_pad(jnp.concatenate([conv_field, conv_next], axis=1)), frames, height, breadth
    )
    conv_flip = (
        conv_weight.reshape(3, 3, 3, channels, channels)[::-1, ::-1, ::-1]
        .transpose(0, 1, 2, 4, 3)
        .reshape(27 * channels, channels)
    )
    act_grad = jnp.dot(conv_cols, conv_flip, preferred_element_type=jnp.float32)
    (norm_grad,) = pullback(act_grad.reshape(block_shape))
    features_grad = (hidden_grad.reshape(block_shape) + norm_grad).astype(jnp.bfloat16)
    data_count = lax.axis_size("dp")
    time_count = lax.axis_size("tm")
    scale = 1.0 / math.sqrt(crop_count * frames * height * breadth * data_count * time_count)
    up_part = lax.psum_scatter(
        contract_rows(hidden_cols, up_flat), "dp", scatter_dimension=0, tiled=True
    )
    grad_up = lax.psum_scatter(up_part, "tm", scatter_dimension=1, tiled=True) * scale
    conv_part = lax.psum_scatter(
        contract_rows(act_cols, conv_grad), "dp", scatter_dimension=0, tiled=True
    )
    grad_conv = lax.psum_scatter(conv_part, "tm", scatter_dimension=1, tiled=True) * scale
    return (features_grad, grad_conv, grad_up)


def solution(mesh):
    in_specs = (P("dp", "tm", None, None, None), P(), P(), P("dp", "tm", None, None, None))
    out_specs = (P("dp", "tm", None, None, None), P("dp", "tm"), P("dp", "tm"))
    return jax.shard_map(shards, mesh=mesh, in_specs=in_specs, out_specs=out_specs, check_vma=False)
```

profile of v0, /device:TPU:0, one launch (start us, length us, event | category | flops | bytes accessed | tf_op | source)
XLA Modules:
  0.0 496.2 jit_solution(12018478470615032043)
XLA Ops:
  7.2 2.5 copy.68
  10.5 1.4 collective-permute-start
  13.3 2.3 copy.46
  15.6 7.6 %reverse_bitcast_fusion = bf16[3,3,3,384,384]{3,4,2,1,0:T(8,128)(2,1)} fusion(bf16[3,3,3,384,384]{4,3,2,1,0:T(8,128)(2,1)} %bitcast.73), kind=kLoop, calls=%fused_computation | loop fusion | bytes 15925248 | tf_op jit(solution)/shard_map/transpose | solution.py:99
  23.2 15.1 %copy.47 = bf16[3,3,3,384,384]{4,3,2,1,0:T(8,128)(2,1)} copy(bf16[3,3,3,384,384]{3,4,2,1,0:T(8,128)(2,1)} %reverse_bitcast_fusion) | data formatting | bytes 15925248 | tf_op jit(solution)/shard_map/transpose | solution.py:99
  38.4 5.0 %copy.49 = f32[1,2,16,24,384]{3,2,1,4,0:T(8,128)} copy(bf16[1,2,16,24,384]{4,3,2,1,0:T(8,128)(2,1)S(1)} %copy-done) | data formatting | bytes 1769472 | tf_op jit(solution)/shard_map/convert_element_type | solution.py:65
  43.7 1.3 pad_maximum_fusion.2
  45.7 4.3 fusion.53
  50.0 1.5 collective-permute-start.1
  52.7 5.9 %reshape.274 = f32[1,2,384,32,12]{2,1,4,3,0:T(2,128)S(1)} reshape(f32[1,2,16,24,384]{3,2,1,4,0:T(8,128)} %copy.49) | data formatting | bytes 2359296 | tf_op jit(solution)/shard_map/jvp()/reshape | solution.py:22
  58.7 9.2 %collective-permute-done.1 = bf16[1,2,16,24,384]{4,3,2,1,0:T(8,128)(2,1)S(1)} collective-permute-done((bf16[1,2,16,24,384]{4,3,2,1,0:T(8,128)(2,1)S(1)}, bf16[1,2,16,24,384]{4,3,2,1,0:T(8,128)(2,1)S(1)}, u32[]{:S(2)}, u32[]{:S(2)}) %collective-permute-start.1) | collective-permute-done | bytes 589856 | tf_op jit(solution)/shard_map/ppermute | solution.py:17
  68.0 3.3 pad_slice_fusion.24
  97.5 11.3 %fusion.54 = f32[768,384]{1,0:T(8,128)S(1)} fusion(bf16[768,10368]{1,0:T(8,128)(2,1)} %constant_dynamic-update-slice_fusion, bf16[10368,384]{1,0:T(8,128)(2,1)S(1)} %bitcast.78), kind=kOutput, calls=%fused_computation.159 | convolution fusion | flops 6115295232 | bytes 25067520 | tf_op jit(solution)/shard_map/dot_general | solution.py:102
  108.9 1.4 copy.48
  110.2 2.9 reshape_reshape.7
  114.5 1.4 reduce_sum.73
  116.6 2.2 fusion.21
  119.1 2.9 multiply_convert_fusion
  122.0 4.6 collective-permute-start.2
  126.7 11.6 %collective-permute-done.2 = bf16[1,2,16,24,384]{4,3,2,1,0:T(8,128)(2,1)S(1)} collective-permute-done((bf16[1,2,16,24,384]{4,3,2,1,0:T(8,128)(2,1)S(1)}, bf16[1,2,16,24,384]{4,3,2,1,0:T(8,128)(2,1)S(1)}, u32[]{:S(2)}, u32[]{:S(2)}) %collective-permute-start.2) | collective-permute-done | bytes 589856 | tf_op jit(solution)/shard_map/ppermute | solution.py:17
  143.5 6.0 %copy-done.5 = bf16[1,2,16,24,10368]{4,3,2,1,0:T(8,128)(2,1)} copy-done((bf16[1,2,16,24,10368]{4,3,2,1,0:T(8,128)(2,1)}, bf16[1,2,16,24,10368]{4,3,2,1,0:T(8,128)(2,1)S(1)}, u32[]{:S(2)}) %copy-start.5) | copy-done | bytes 15925272
  149.5 11.8 %fusion.12 = bf16[768,384]{1,0:T(8,128)(2,1)S(1)} fusion(f32[768,384]{1,0:T(8,128)S(1)} %bitcast.117, bf16[768,10368]{1,0:T(8,128)(2,1)} %bitcast.124, bf16[10368,384]{1,0:T(8,128)(2,1)S(1)} %bitcast.75), kind=kOutput, calls=%fused_computation.73 | convolution fusion | flops 6115885056 | bytes 25657344 | tf_op jit(solution)/shard_map/dot_general | solution.py:72
  161.3 4.8 collective-permute-start.3
  166.1 10.6 %collective-permute-done.3 = bf16[1,2,16,24,384]{4,3,2,1,0:T(8,128)(2,1)S(1)} collective-permute-done((bf16[1,2,16,24,384]{4,3,2,1,0:T(8,128)(2,1)S(1)}, bf16[1,2,16,24,384]{4,3,2,1,0:T(8,128)(2,1)S(1)}, u32[]{:S(2)}, u32[]{:S(2)}) %collective-permute-start.3) | collective-permute-done | bytes 589856 | tf_op jit(solution)/shard_map/ppermute | solution.py:17
  176.8 3.3 fusion.6
  180.2 15.2 %fusion.55 = f32[10368,384]{1,0:T(8,128)} fusion(bf16[768,10368]{1,0:T(8,128)(2,1)} %bitcast.125, bf16[768,384]{1,0:T(8,128)(2,1)S(1)} %get-tuple-element.49), kind=kOutput, calls=%fused_computation.160 | convolution fusion | flops 6115295232 | bytes 32440320 | tf_op jit(solution)/shard_map/dot_general | solution.py:57
  195.5 66.3 %reduce-scatter.11.cloned.1.call-done = f32[72,768]{1,0:T(8,128)} async-done(((f32[1152,768]{1,0:T(8,128)}), f32[72,768]{1,0:T(8,128)}) %reduce-scatter.11.cloned.1.call-update) | async-done | bytes 221200 | tf_op jit(solution)/shard_map/reduce_scatter | solution.py:108
  261.8 1.9 copy.58
  263.7 143.6 %reduce-scatter.17.cloned.1.call-done = f32[648,384]{1,0:T(8,128)} async-done(((f32[10368,384]{1,0:T(8,128)}), f32[648,384]{1,0:T(8,128)}) %reduce-scatter.17.cloned.1.call-update) | async-done | bytes 995344
  407.4 2.6 copy.56
  410.0 35.9 %reduce-scatter.15.cloned.1.call-done = f32[96,72]{1,0:T(8,128)} async-done(((f32[768,72]{1,0:T(8,128)}), f32[96,72]{1,0:T(8,128)}) %reduce-scatter.15.cloned.1.call-update) | async-done | bytes 27664
  447.4 40.4 %reduce-scatter.13.cloned.1.call-done = f32[48,648]{1,0:T(8,128)} async-done(((f32[384,648]{1,0:T(8,128)}), f32[48,648]{1,0:T(8,128)}) %reduce-scatter.13.cloned.1.call-update) | async-done | bytes 124432
  (122 shorter events, 41.9 us)
Async XLA Ops:
  7.2 254.7 %reduce-scatter.11.cloned.1.call-start = ((), (), s32[]{:S(2)}) async-start(), calls=%async_computation.4 | async-start | bytes 3760128 | tf_op jit(solution)/shard_map/reduce_scatter | solution.py:108
  10.5 2.7 copy-start.1
  10.5 33.2 %collective-permute-start = (bf16[1,2,16,24,768]{4,3,2,1,0:T(8,128)(2,1)S(1)}, bf16[1,2,16,24,768]{4,3,2,1,0:T(8,128)(2,1)}, u32[]{:S(2)}, u32[]{:S(2)}) collective-permute-start(bf16[1,2,16,24,768]{4,3,2,1,0:T(8,128)(2,1)S(1)} %reshape.267), channel_id=1, source_target_pairs={{16,0},{32,16},{48,32},{64,48},{80,64},{96,80},{112,96},{17,1},{33... | collective-permute-start | bytes 3538952 | tf_op jit(solution)/shard_map/ppermute | solution.py:17
  23.2 15.1 %copy-start = (bf16[1,2,16,24,384]{4,3,2,1,0:T(8,128)(2,1)S(1)}, bf16[1,2,16,24,384]{4,3,2,1,0:T(8,128)(2,1)}, u32[]{:S(2)}) copy-start(bf16[1,2,16,24,384]{4,3,2,1,0:T(8,128)(2,1)} %param.4) | copy-start | bytes 1769476
  43.7 1.7 copy-start.2
  43.7 2.0 copy-start.3
  50.0 17.9 %collective-permute-start.1 = (bf16[1,2,16,24,384]{4,3,2,1,0:T(8,128)(2,1)S(1)}, bf16[1,2,16,24,384]{4,3,2,1,0:T(8,128)(2,1)S(1)}, u32[]{:S(2)}, u32[]{:S(2)}) collective-permute-start(bf16[1,2,16,24,384]{4,3,2,1,0:T(8,128)(2,1)S(1)} %bitcast.79), channel_id=1, source_target_pairs={{16,0},{32,16},{48,32},{64,48},{80,64},{96,80},{112,96},{17,1},{33... | collective-permute-start | bytes 1769480 | tf_op jit(solution)/shard_map/ppermute | solution.py:17
  52.0 6.7 %copy-start.7 = (f32[2,32]{1,0:T(2,128)}, f32[2,32]{1,0:T(2,128)S(1)}, u32[]{:S(2)}) copy-start(f32[2,32]{1,0:T(2,128)S(1)} %reduce_sum.70) | copy-start | bytes 772
  52.0 0.5 copy-start.6
  85.2 12.3 %slice-start.2 = ((s8[7962624]{0:T(1024)(128)(4,1)}), s8[4194304]{0:T(1024)(128)(4,1)S(1)}, s32[]{:S(2)}) async-start(s8[7962624]{0:T(1024)(128)(4,1)} %bitcast.76), calls=%async_computation.10 | async-start | bytes 8388608
  90.7 6.8 %slice-start.3 = ((s8[7962624]{0:T(1024)(128)(4,1)}), s8[3768320]{0:T(1024)(128)(4,1)S(1)}, s32[]{:S(2)}) async-start(s8[7962624]{0:T(1024)(128)(4,1)} %bitcast.76), calls=%async_computation.11 | async-start | bytes 7536640
  122.0 16.2 %collective-permute-start.2 = (bf16[1,2,16,24,384]{4,3,2,1,0:T(8,128)(2,1)S(1)}, bf16[1,2,16,24,384]{4,3,2,1,0:T(8,128)(2,1)S(1)}, u32[]{:S(2)}, u32[]{:S(2)}) collective-permute-start(bf16[1,2,16,24,384]{4,3,2,1,0:T(8,128)(2,1)S(1)} %get-tuple-element.47), channel_id=1, source_target_pairs={{0,16},{16,32},{32,48},{48,64},{64,80},{80,96},{96,112},{1,17},{17... | collective-permute-start | bytes 1769480 | tf_op jit(solution)/shard_map/ppermute | solution.py:17
  141.7 7.7 %slice-start = ((s8[7962624]{0:T(1024)(128)(4,1)}), s8[4194304]{0:T(1024)(128)(4,1)S(1)}, s32[]{:S(2)}) async-start(s8[7962624]{0:T(1024)(128)(4,1)} %bitcast.74), calls=%async_computation.8 | async-start | bytes 8388608
  142.5 6.9 %slice-start.1 = ((s8[7962624]{0:T(1024)(128)(4,1)}), s8[3768320]{0:T(1024)(128)(4,1)S(1)}, s32[]{:S(2)}) async-start(s8[7962624]{0:T(1024)(128)(4,1)} %bitcast.74), calls=%async_computation.9 | async-start | bytes 7536640
  143.4 6.0 %copy-start.5 = (bf16[1,2,16,24,10368]{4,3,2,1,0:T(8,128)(2,1)}, bf16[1,2,16,24,10368]{4,3,2,1,0:T(8,128)(2,1)S(1)}, u32[]{:S(2)}) copy-start(bf16[1,2,16,24,10368]{4,3,2,1,0:T(8,128)(2,1)S(1)} %fusion.48) | copy-start | bytes 47775748
  161.3 15.5 %copy-start.4 = (bf16[96,8,2,384]{3,1,2,0:T(8,128)(2,1)S(1)}, bf16[96,8,2,384]{3,1,2,0:T(8,128)(2,1)}, u32[]{:S(2)}) copy-start(bf16[96,8,2,384]{3,1,2,0:T(8,128)(2,1)} %copy.61) | copy-start | bytes 3538948
  161.3 15.4 %collective-permute-start.3 = (bf16[1,2,16,24,384]{4,3,2,1,0:T(8,128)(2,1)S(1)}, bf16[1,2,16,24,384]{4,3,2,1,0:T(8,128)(2,1)S(1)}, u32[]{:S(2)}, u32[]{:S(2)}) collective-permute-start(bf16[1,2,16,24,384]{4,3,2,1,0:T(8,128)(2,1)S(1)} %bitcast.118), channel_id=1, source_target_pairs={{0,16},{16,32},{32,48},{48,64},{64,80},{80,96},{96,112},{1,17},{17... | collective-permute-start | bytes 1769480 | tf_op jit(solution)/shard_map/ppermute | solution.py:17
  180.2 227.2 %reduce-scatter.17.cloned.1.call-start = ((), (), s32[]{:S(2)}) async-start(), calls=%async_computation.7 | async-start | bytes 16920576
  195.5 250.4 %reduce-scatter.15.cloned.1.call-start = ((), (), s32[]{:S(2)}) async-start(), calls=%async_computation.6 | async-start | bytes 442368
  263.7 224.1 %reduce-scatter.13.cloned.1.call-start = ((), (), s32[]{:S(2)}) async-start(), calls=%async_computation.5 | async-start | bytes 1327104
Sparse Core Ops, SparseCore 0:
  180.3 81.4 reduce-scatter.10
  266.3 141.0 reduce-scatter.16
  409.7 36.0 reduce-scatter.14
  448.1 39.6 reduce-scatter.12
where the time goes:
time: 497 us; the launch traced here: 496 us
  waiting for transfers between devices  318 us (64%)
  local copies, waits for them, and re-layouts  95.1 us (19%)
  matrix products  46.1 us (9%)
  between operations  14.2 us (3%)
  starting transfers between devices  12.4 us (2%)
  other arithmetic  10.8 us (2%)
    unnamed x7, waiting for transfers between devices  220 us
    reduce_scatter x1, waiting for transfers between devices, shards(): lax.psum_scatter(contract_rows(hidden_cols, up_flat), 'dp', scatter_dimen...  66.3 us
    unnamed x81, local copies, waits for them, and re-layouts  44.6 us
    ppermute x4, waiting for transfers between devices, from_behind(): lax.ppermute(value, axis, [(source, source + steps) for source in range(f...  31.3 us
    transpose x2, local copies, waits for them, and re-layouts, shards(): conv_flip = conv_weight.reshape(3, 3, 3, channels, channels)[::-1, ::-1,...  22.7 us
    dot_general x2, matrix products, contract_rows(): lax.dot_general(left, right, (((0,), (0,)), ((), ())), preferred_element_...  18.6 us
    ppermute x4, starting transfers between devices, from_behind(): lax.ppermute(value, axis, [(source, source + steps) for source in range(f...  12.3 us
    dot_general x1, matrix products, shards(): jnp.dot(act_cols, conv_weight, preferred_element_type=jnp.float32)  11.8 us
  transfers between devices with their start and end apart: 8, of which 7 were waited for; matrix products, arithmetic and copies ran while one was open for 12% of the time, Pallas kernels for 0%

commit v1 on v0

--- a/solution.py
+++ b/solution.py
@@ -59,6 +59,24 @@
     )
 
 
+def reduce_blocks(partial):
+    rows, cols = partial.shape
+    data, times = lax.axis_size("dp"), lax.axis_size("tm")
+    chips = data // 2
+    core = lax.axis_index("dp") % 2
+    halves = partial.reshape(chips, 2, rows // data, cols)
+    send = lax.dynamic_index_in_dim(halves, 1 - core, 1, keepdims=False).astype(jnp.bfloat16)
+    keep = lax.dynamic_index_in_dim(halves, core, 1, keepdims=False)
+    swapped = lax.ppermute(send, "dp", [(d, d ^ 1) for d in range(data)])
+    pair = (keep + swapped.astype(jnp.float32)).astype(jnp.bfloat16)
+    groups = [[2 * chip + side for chip in range(chips)] for side in range(2)]
+    spread = lax.all_to_all(pair, "dp", 0, 0, axis_index_groups=groups, tiled=True)
+    rowsum = jnp.sum(spread.astype(jnp.float32), axis=0).astype(jnp.bfloat16)
+    blocks = rowsum.reshape(rows // data, times, cols // times).transpose(1, 0, 2)
+    final = lax.all_to_all(blocks, "tm", 0, 0, tiled=True)
+    return jnp.sum(final.astype(jnp.float32), axis=0)
+
+
 def shards(features, conv_weight, up_weight, cotangent):
     crop_count, frames, height, breadth, channels = features.shape
     block_shape = features.shape
@@ -73,8 +91,6 @@
     hidden = (
         (feature_field.reshape(-1, channels) + conv_out).astype(jnp.bfloat16).reshape(block_shape)
     )
-    hidden_prior = from_behind(hidden, "tm", 1)
-    hidden_cols = stack_times(jnp.concatenate([hidden_prior, hidden], axis=1), frames)
     up_grad = cotangent.reshape(crop_count, frames, 2, height, breadth, channels)
     up_grad = up_grad.transpose(0, 1, 3, 4, 2, 5).reshape(
         crop_count, frames, height, breadth, 2 * channels
@@ -88,7 +104,6 @@
     )
     hidden_grad = jnp.dot(up_cols, up_flip, preferred_element_type=jnp.float32)
     conv_grad = hidden_grad.astype(jnp.bfloat16)
-    up_flat = up_grad.reshape(-1, 2 * channels)
     conv_field = conv_grad.reshape(block_shape)
     conv_next = from_behind(conv_field, "tm", -1)
     conv_cols = stack_taps(
@@ -105,14 +120,17 @@
     data_count = lax.axis_size("dp")
     time_count = lax.axis_size("tm")
     scale = 1.0 / math.sqrt(crop_count * frames * height * breadth * data_count * time_count)
-    up_part = lax.psum_scatter(
-        contract_rows(hidden_cols, up_flat), "dp", scatter_dimension=0, tiled=True
+    grad_conv = reduce_blocks(contract_rows(act_cols, conv_grad)) * scale
+    hidden_flat = hidden.reshape(-1, channels)
+    up_ext = jnp.concatenate([up_grad, up_next], axis=1)
+    up_part = jnp.concatenate(
+        [
+            contract_rows(hidden_flat, up_ext[:, 2 - k : 2 - k + frames].reshape(-1, 2 * channels))
+            for k in range(3)
+        ],
+        axis=0,
     )
-    grad_up = lax.psum_scatter(up_part, "tm", scatter_dimension=1, tiled=True) * scale
-    conv_part = lax.psum_scatter(
-        contract_rows(act_cols, conv_grad), "dp", scatter_dimension=0, tiled=True
-    )
-    grad_conv = lax.psum_scatter(conv_part, "tm", scatter_dimension=1, tiled=True) * scale
+    grad_up = reduce_blocks(up_part) * scale
     return (features_grad, grad_conv, grad_up)
 
 

time: 497 us -> 321 us (0.65); the launches traced: 496 us -> 314 us
  waiting for transfers between devices: 318 us -> 94.9 us
  local copies, waits for them, and re-layouts: 95.1 us -> 118 us
  starting transfers between devices: 12.4 us -> 29.8 us
  other arithmetic: 10.8 us -> 24 us
  between operations: 14.2 us -> 1.58 us
    unnamed x7 -> x0, waiting for transfers between devices: 220 us -> none
    all_to_all x0 -> x4, waiting for transfers between devices: none -> 73.4 us  [the longest x2 63.1 us: reduce_blocks(): lax.all_to_all(pair, 'dp', 0, 0, axis_index_groups=groups, tiled=True)]
    reduce_scatter x1 -> x0, waiting for transfers between devices: 66.3 us -> none  [shards(): lax.psum_scatter(contract_rows(hidden_cols, up_flat), 'dp', scatter_dimen...]
    reshape x0 -> x2, local copies, waits for them, and re-layouts: none -> 21.9 us  [the longest x1 21.7 us: stack_taps(): return joined.reshape(-1, joined.shape[-1])]
    all_to_all x0 -> x4, starting transfers between devices: none -> 21.8 us  [the longest x2 11.7 us: reduce_blocks(): lax.all_to_all(pair, 'dp', 0, 0, axis_index_groups=groups, tiled=True)]
    ppermute x4 -> x3, waiting for transfers between devices: 31.3 us -> 19.4 us  [from_behind(): lax.ppermute(value, axis, [(source, source + steps) for source in range(f...]
    convert_element_type x0 -> x2, other arithmetic: none -> 9.83 us  [reduce_blocks(): pair = (keep + swapped.astype(jnp.float32)).astype(jnp.bfloat16)]
    unnamed x81 -> x78, local copies, waits for them, and re-layouts: 44.6 us -> 38.1 us
  transfers between devices with their start and end apart: 8 -> 9, of which waited for: 7 -> 7; matrix products, arithmetic and copies ran while one was open for 12% -> 23% of each run, Pallas kernels for 0% -> 0%
where the time goes in v1:
time: 321 us; the launch traced here: 314 us
  local copies, waits for them, and re-layouts  118 us (37%)
  waiting for transfers between devices  94.9 us (30%)
  matrix products  45.6 us (14%)
  starting transfers between devices  29.8 us (9%)
  other arithmetic  24 us (7%)
    all_to_all x2, waiting for transfers between devices, reduce_blocks(): lax.all_to_all(pair, 'dp', 0, 0, axis_index_groups=groups, tiled=True)  63.1 us
    unnamed x78, local copies, waits for them, and re-layouts  38.1 us
    transpose x2, local copies, waits for them, and re-layouts, shards(): conv_flip = conv_weight.reshape(3, 3, 3, channels, channels)[::-1, ::-1,...  22.8 us
    reshape x1, local copies, waits for them, and re-layouts, stack_taps(): return joined.reshape(-1, joined.shape[-1])  21.7 us
    ppermute x3, waiting for transfers between devices, from_behind(): lax.ppermute(value, axis, [(source, source + steps) for source in range(f...  19.4 us
    dot_general x4, matrix products, contract_rows(): lax.dot_general(left, right, (((0,), (0,)), ((), ())), preferred_element_...  18.6 us
    all_to_all x2, starting transfers between devices, reduce_blocks(): lax.all_to_all(pair, 'dp', 0, 0, axis_index_groups=groups, tiled=True)  11.7 us
    dot_general x1, matrix products, shards(): act_grad = jnp.dot(conv_cols, conv_flip, preferred_element_type=jnp.float32)  11.3 us
  transfers between devices with their start and end apart: 9, of which 7 were waited for; matrix products, arithmetic and copies ran while one was open for 23% of the time, Pallas kernels for 0%

profile of v1, /device:TPU:0, one launch (start us, length us, event | category | flops | bytes accessed | tf_op | source)
XLA Modules:
  0.0 314.3 jit_solution(12640907682848138316)
XLA Ops:
  0.6 2.5 copy.81
  6.8 2.3 copy.60
  9.1 7.6 %reverse_bitcast_fusion = bf16[3,3,3,384,384]{3,4,2,1,0:T(8,128)(2,1)} fusion(bf16[3,3,3,384,384]{4,3,2,1,0:T(8,128)(2,1)} %bitcast.99), kind=kLoop, calls=%fused_computation.3 | loop fusion | bytes 15925248 | tf_op jit(solution)/shard_map/transpose | solution.py:114
  16.7 15.1 %copy.61 = bf16[3,3,3,384,384]{4,3,2,1,0:T(8,128)(2,1)} copy(bf16[3,3,3,384,384]{3,4,2,1,0:T(8,128)(2,1)} %reverse_bitcast_fusion) | data formatting | bytes 15925248 | tf_op jit(solution)/shard_map/transpose | solution.py:114
  31.8 5.1 %copy.63 = f32[1,2,16,24,384]{3,2,1,4,0:T(8,128)} copy(bf16[1,2,16,24,384]{4,3,2,1,0:T(8,128)(2,1)S(1)} %copy-done) | data formatting | bytes 1769472 | tf_op jit(solution)/shard_map/convert_element_type | solution.py:83
  39.2 4.3 %fusion.52 = (bf16[768,384]{1,0:T(8,128)(2,1)S(1)}, f32[768,384]{1,0:T(8,128)}) fusion(bf16[2304,384]{1,0:T(8,128)(2,1)S(1)} %bitcast.137, bf16[768,768]{1,0:T(8,128)(2,1)} %bitcast.3, bf16[768,768]{1,0:T(8,128)(2,1)S(1)} %bitcast.107, bf16[768,768]{1,0:T(8,128)(2,1)S(1)} %bitcast.109), kind=kOutput, calls=%fused_computation.163 | convolution fusion | flops 1369866240 | bytes 7077888 | tf_op jit(solution)/shard_map/dot_general | solution.py:105
  45.8 6.7 %reshape.281 = f32[1,2,384,32,12]{2,1,4,3,0:T(2,128)} reshape(f32[1,2,16,24,384]{3,2,1,4,0:T(8,128)} %copy.63) | data formatting | bytes 2359296 | tf_op jit(solution)/shard_map/jvp()/reshape | solution.py:22
  52.5 8.9 %collective-permute-done.1 = bf16[1,2,16,24,384]{4,3,2,1,0:T(8,128)(2,1)S(1)} collective-permute-done((bf16[1,2,16,24,384]{4,3,2,1,0:T(8,128)(2,1)S(1)}, bf16[1,2,16,24,384]{4,3,2,1,0:T(8,128)(2,1)S(1)}, u32[]{:S(2)}, u32[]{:S(2)}) %collective-permute-start.1) | collective-permute-done | bytes 589856 | tf_op jit(solution)/shard_map/ppermute | solution.py:17
  61.5 3.3 %pad_slice_fusion.24 = (bf16[1,2,16,24,384]{4,3,2,1,0:T(8,128)(2,1)S(1)}, bf16[1,2,16,24,384]{4,3,2,1,0:T(8,128)(2,1)S(1)}, bf16[1,2,16,24,384]{4,3,2,1,0:T(8,12...) fusion(bf16[1,4,16,24,384]{4,3,2,1,0:T(8,128)(2,1)S(1)} %pad_ma, ...), kind=kLoop, calls=%fused_computation.29 | loop fusion | bytes 12386304 | tf_op jit(solution)/shard_map/slice | solution.py:35
  91.0 11.3 %fusion.53 = f32[768,384]{1,0:T(8,128)S(1)} fusion(bf16[768,10368]{1,0:T(8,128)(2,1)} %constant_dynamic-update-slice_fusion, bf16[10368,384]{1,0:T(8,128)(2,1)S(1)} %bitcast.102), kind=kOutput, calls=%fused_computation.164 | convolution fusion | flops 6115295232 | bytes 25067520 | tf_op jit(solution)/shard_map/dot_general | solution.py:117
  103.7 3.0 reshape_reshape.7
  107.5 2.5 fusion.18
  110.4 2.9 multiply_convert_fusion
  113.4 4.6 %collective-permute-start.2 = (bf16[1,2,16,24,384]{4,3,2,1,0:T(8,128)(2,1)S(1)}, bf16[1,2,16,24,384]{4,3,2,1,0:T(8,128)(2,1)S(1)}, u32[]{:S(2)}, u32[]{:S(2)}) collective-permute-start(bf16[1,2,16,24,384]{4,3,2,1,0:T(8,128)(2,1)S(1)} %get-tuple-element.29), channel_id=1, source_target_pairs={{0,16},{16,32},{32,48},{48,64},{64,80},{80,96},{96,112},{1,17},{17... | collective-permute-start | bytes 1769480 | tf_op jit(solution)/shard_map/ppermute | solution.py:17
  119.1 10.6 %collective-permute-done.2 = bf16[1,2,16,24,384]{4,3,2,1,0:T(8,128)(2,1)S(1)} collective-permute-done((bf16[1,2,16,24,384]{4,3,2,1,0:T(8,128)(2,1)S(1)}, bf16[1,2,16,24,384]{4,3,2,1,0:T(8,128)(2,1)S(1)}, u32[]{:S(2)}, u32[]{:S(2)}) %collective-permute-start.2) | collective-permute-done | bytes 589856 | tf_op jit(solution)/shard_map/ppermute | solution.py:17
  134.7 5.6 %copy-done.1 = bf16[1,2,16,24,10368]{4,3,2,1,0:T(8,128)(2,1)} copy-done((bf16[1,2,16,24,10368]{4,3,2,1,0:T(8,128)(2,1)}, bf16[1,2,16,24,10368]{4,3,2,1,0:T(8,128)(2,1)S(1)}, u32[]{:S(2)}) %copy-start.1) | copy-done | bytes 15925272
  140.3 21.7 %copy.69 = bf16[768,10368]{0,1:T(8,128)(2,1)} copy(bf16[768,10368]{1,0:T(8,128)(2,1)} %bitcast.90) | data formatting | bytes 31850496 | tf_op jit(solution)/shard_map/reshape | solution.py:47
  162.0 15.3 %fusion.47 = f32[8,2,648,384]{3,2,1,0:T(8,128)} fusion(bf16[8,2,648,768]{3,2,1,0:T(8,128)(2,1)} %bitcast.92, bf16[768,384]{1,0:T(8,128)(2,1)S(1)} %get-tuple-element.31), kind=kOutput, calls=%fused_computation.121 | convolution fusion | flops 6115295232 | bytes 32440320 | tf_op jit(solution)/shard_map/dot_general | solution.py:57
  177.3 5.7 %fusion.1 = bf16[8,648,384]{2,1,0:T(8,128)(2,1)} fusion(f32[8,2,648,384]{3,2,1,0:T(8,128)} %fusion.47, s32[]{:T(128)S(6)} %select_n.21), kind=kLoop, calls=%fused_computation.4 | loop fusion | bytes 7962628 | tf_op jit(solution)/shard_map/convert_element_type | solution.py:68
  183.0 11.3 %fusion.9 = bf16[768,384]{1,0:T(8,128)(2,1)S(1)} fusion(f32[768,384]{1,0:T(8,128)S(1)} %bitcast.140, bf16[768,10368]{1,0:T(8,128)(2,1)S(1)} %bitcast.91, bf16[10368,384]{1,0:T(8,128)(2,1)} %param.5), kind=kOutput, calls=%fused_computation.75 | convolution fusion | flops 6115885056 | bytes 25657344 | tf_op jit(solution)/shard_map/dot_general | solution.py:90
  200.3 2.1 collective-permute-done.4
  202.4 2.6 fusion.8
  205.0 7.1 %all-to-all-start.2 = ((bf16[8,72,768]{2,1,0:T(8,128)(2,1)}), bf16[8,72,768]{2,1,0:T(8,128)(2,1)S(1)}, u32[]{:S(2)}, u32[]{:S(2)}) async-start(bf16[8,72,768]{2,1,0:T(8,128)(2,1)} %fusion.8), calls=%async_computation.2 | async-start | bytes 1769472 | tf_op jit(solution)/shard_map/all_to_all | solution.py:73
  212.1 7.3 %fusion = bf16[8,648,384]{2,1,0:T(8,128)(2,1)} fusion(bf16[8,648,384]{2,1,0:T(8,128)(2,1)} %collective-permute-done.3, f32[8,2,648,384]{3,2,1,0:T(8,128)} %fusion.47, s32[]{:T(128)S(6)} %select_n.20), kind=kLoop, calls=%fused_computation.1 | loop fusion | flops 5971968 | bytes 15925252 | tf_op jit(solution)/shard_map/convert_element_type | solution.py:71
  219.4 7.5 %all-to-all-done.2 = bf16[8,72,768]{2,1,0:T(8,128)(2,1)S(1)} async-done(((bf16[8,72,768]{2,1,0:T(8,128)(2,1)}), bf16[8,72,768]{2,1,0:T(8,128)(2,1)S(1)}, u32[]{:S(2)}, u32[]{:S(2)}) %all-to-all-start.2) | async-done | bytes 884768 | tf_op jit(solution)/shard_map/all_to_all | solution.py:73
  226.9 4.5 %all-to-all-start = ((bf16[8,648,384]{2,1,0:T(8,128)(2,1)}), bf16[8,648,384]{2,1,0:T(8,128)(2,1)}, u32[]{:S(2)}, u32[]{:S(2)}) async-start(bf16[8,648,384]{2,1,0:T(8,128)(2,1)} %fusion), calls=%async_computation | async-start | bytes 7962624 | tf_op jit(solution)/shard_map/all_to_all | solution.py:73
  232.4 55.6 %all-to-all-done = bf16[8,648,384]{2,1,0:T(8,128)(2,1)} async-done(((bf16[8,648,384]{2,1,0:T(8,128)(2,1)}), bf16[8,648,384]{2,1,0:T(8,128)(2,1)}, u32[]{:S(2)}, u32[]{:S(2)}) %all-to-all-start) | async-done | bytes 3981344 | tf_op jit(solution)/shard_map/all_to_all | solution.py:73
  288.0 6.5 %all-to-all-start.3 = ((bf16[8,72,96]{2,1,0:T(8,128)(2,1)}), bf16[8,72,96]{2,1,0:T(8,128)(2,1)S(1)}, u32[]{:S(2)}, u32[]{:S(2)}) async-start(bf16[8,72,96]{2,1,0:T(8,128)(2,1)} %copy.71), calls=%async_computation.3 | async-start | bytes 294912 | tf_op jit(solution)/shard_map/all_to_all | solution.py:76
  294.5 2.9 reduce_sum.117
  298.5 2.5 all-to-all-done.3
  301.0 3.5 %all-to-all-start.1 = ((bf16[8,648,48]{1,2,0:T(8,128)(2,1)}), bf16[8,648,48]{1,2,0:T(8,128)(2,1)S(1)}, u32[]{:S(2)}, u32[]{:S(2)}) async-start(bf16[8,648,48]{1,2,0:T(8,128)(2,1)} %bitcast.47), calls=%async_computation.1 | async-start | bytes 1179648 | tf_op jit(solution)/shard_map/all_to_all | solution.py:76
  305.2 7.9 %all-to-all-done.1 = bf16[8,648,48]{1,2,0:T(8,128)(2,1)S(1)} async-done(((bf16[8,648,48]{1,2,0:T(8,128)(2,1)}), bf16[8,648,48]{1,2,0:T(8,128)(2,1)S(1)}, u32[]{:S(2)}, u32[]{:S(2)}) %all-to-all-start.1) | async-done | bytes 497696 | tf_op jit(solution)/shard_map/all_to_all | solution.py:76
  (130 shorter events, 52.5 us)
Async XLA Ops:
  3.9 2.7 copy-start.8
  3.9 33.3 %collective-permute-start = (bf16[1,2,16,24,768]{4,3,2,1,0:T(8,128)(2,1)S(1)}, bf16[1,2,16,24,768]{4,3,2,1,0:T(8,128)(2,1)}, u32[]{:S(2)}, u32[]{:S(2)}) collective-permute-start(bf16[1,2,16,24,768]{4,3,2,1,0:T(8,128)(2,1)S(1)} %reshape.274), channel_id=1, source_target_pairs={{16,0},{32,16},{48,32},{64,48},{80,64},{96,80},{112,96},{17,1},{33... | collective-permute-start | bytes 3538952 | tf_op jit(solution)/shard_map/ppermute | solution.py:17
  16.7 15.1 %copy-start = (bf16[1,2,16,24,384]{4,3,2,1,0:T(8,128)(2,1)S(1)}, bf16[1,2,16,24,384]{4,3,2,1,0:T(8,128)(2,1)}, u32[]{:S(2)}) copy-start(bf16[1,2,16,24,384]{4,3,2,1,0:T(8,128)(2,1)} %param.4) | copy-start | bytes 1769476
  37.2 1.5 copy-start.6
  37.2 2.0 copy-start.9
  38.5 5.0 %copy-start.4 = (bf16[1,2,16,24,768]{4,3,2,1,0:T(8,128)(2,1)}, bf16[1,2,16,24,768]{4,3,2,1,0:T(8,128)(2,1)S(1)}, u32[]{:S(2)}) copy-start(bf16[1,2,16,24,768]{4,3,2,1,0:T(8,128)(2,1)S(1)} %pad_maximum_fusion.3) | copy-start | bytes 3538948
  43.5 17.9 %collective-permute-start.1 = (bf16[1,2,16,24,384]{4,3,2,1,0:T(8,128)(2,1)S(1)}, bf16[1,2,16,24,384]{4,3,2,1,0:T(8,128)(2,1)S(1)}, u32[]{:S(2)}, u32[]{:S(2)}) collective-permute-start(bf16[1,2,16,24,384]{4,3,2,1,0:T(8,128)(2,1)S(1)} %bitcast.103), channel_id=1, source_target_pairs={{16,0},{32,16},{48,32},{64,48},{80,64},{96,80},{112,96},{17,1},{33... | collective-permute-start | bytes 1769480 | tf_op jit(solution)/shard_map/ppermute | solution.py:17
  78.9 12.0 %slice-start = ((s8[7962624]{0:T(1024)(128)(4,1)}), s8[4194304]{0:T(1024)(128)(4,1)S(1)}, s32[]{:S(2)}) async-start(s8[7962624]{0:T(1024)(128)(4,1)} %bitcast.100), calls=%async_computation.4 | async-start | bytes 8388608
  84.5 6.5 %slice-start.1 = ((s8[7962624]{0:T(1024)(128)(4,1)}), s8[3768320]{0:T(1024)(128)(4,1)S(1)}, s32[]{:S(2)}) async-start(s8[7962624]{0:T(1024)(128)(4,1)} %bitcast.100), calls=%async_computation.5 | async-start | bytes 7536640
  113.4 16.2 %collective-permute-start.2 = (bf16[1,2,16,24,384]{4,3,2,1,0:T(8,128)(2,1)S(1)}, bf16[1,2,16,24,384]{4,3,2,1,0:T(8,128)(2,1)S(1)}, u32[]{:S(2)}, u32[]{:S(2)}) collective-permute-start(bf16[1,2,16,24,384]{4,3,2,1,0:T(8,128)(2,1)S(1)} %get-tuple-element.29), channel_id=1, source_target_pairs={{0,16},{16,32},{32,48},{48,64},{64,80},{80,96},{96,112},{1,17},{17... | collective-permute-start | bytes 1769480 | tf_op jit(solution)/shard_map/ppermute | solution.py:17
  134.7 5.6 %copy-start.1 = (bf16[1,2,16,24,10368]{4,3,2,1,0:T(8,128)(2,1)}, bf16[1,2,16,24,10368]{4,3,2,1,0:T(8,128)(2,1)S(1)}, u32[]{:S(2)}) copy-start(bf16[1,2,16,24,10368]{4,3,2,1,0:T(8,128)(2,1)S(1)} %fusion.46) | copy-start | bytes 47775748
  162.0 21.0 %copy-start.2 = (bf16[1,2,16,24,10368]{4,3,2,1,0:T(8,128)(2,1)S(1)}, bf16[1,2,16,24,10368]{4,3,2,1,0:T(8,128)(2,1)}, u32[]{:S(2)}) copy-start(bf16[1,2,16,24,10368]{4,3,2,1,0:T(8,128)(2,1)} %copy-done.1) | copy-start | bytes 47775748
  177.3 5.7 %copy-start.10 = (f32[1,2,16,24,384]{4,3,2,1,0:T(8,128)S(1)}, f32[1,2,16,24,384]{4,3,2,1,0:T(8,128)}, u32[]{:S(2)}) copy-start(f32[1,2,16,24,384]{4,3,2,1,0:T(8,128)} %convert_element_type.57) | copy-start | bytes 3538948
  182.9 29.2 %collective-permute-start.3 = (bf16[8,648,384]{2,1,0:T(8,128)(2,1)}, bf16[8,648,384]{2,1,0:T(8,128)(2,1)}, u32[]{:S(2)}, u32[]{:S(2)}) collective-permute-start(bf16[8,648,384]{2,1,0:T(8,128)(2,1)} %fusion.1), channel_id=1, source_target_pairs={{0,1},{1,0},{2,3},{3,2},{4,5},{5,4},{6,7},{7,6},{8,9},{9,8},{10,11... | collective-permute-start | bytes 11943944 | tf_op jit(solution)/shard_map/ppermute | solution.py:70
  182.9 11.3 %copy-start.5 = (bf16[1,2,16,24,768]{4,3,2,1,0:T(8,128)(2,1)S(1)}, bf16[1,2,16,24,768]{4,3,2,1,0:T(8,128)(2,1)}, u32[]{:S(2)}) copy-start(bf16[1,2,16,24,768]{4,3,2,1,0:T(8,128)(2,1)} %copy-done.4) | copy-start | bytes 3538948
  194.9 2.0 copy-start.7
  197.9 1.8 copy-start.3
  199.8 2.6 collective-permute-start.4
  205.0 21.9 %all-to-all-start.2 = ((bf16[8,72,768]{2,1,0:T(8,128)(2,1)}), bf16[8,72,768]{2,1,0:T(8,128)(2,1)S(1)}, u32[]{:S(2)}, u32[]{:S(2)}) async-start(bf16[8,72,768]{2,1,0:T(8,128)(2,1)} %fusion.8), calls=%async_computation.2 | async-start | bytes 1769472 | tf_op jit(solution)/shard_map/all_to_all | solution.py:73
  226.9 61.1 %all-to-all-start = ((bf16[8,648,384]{2,1,0:T(8,128)(2,1)}), bf16[8,648,384]{2,1,0:T(8,128)(2,1)}, u32[]{:S(2)}, u32[]{:S(2)}) async-start(bf16[8,648,384]{2,1,0:T(8,128)(2,1)} %fusion), calls=%async_computation | async-start | bytes 7962624 | tf_op jit(solution)/shard_map/all_to_all | solution.py:73
  288.0 13.0 %all-to-all-start.3 = ((bf16[8,72,96]{2,1,0:T(8,128)(2,1)}), bf16[8,72,96]{2,1,0:T(8,128)(2,1)S(1)}, u32[]{:S(2)}, u32[]{:S(2)}) async-start(bf16[8,72,96]{2,1,0:T(8,128)(2,1)} %copy.71), calls=%async_computation.3 | async-start | bytes 294912 | tf_op jit(solution)/shard_map/all_to_all | solution.py:76
  301.0 12.1 %all-to-all-start.1 = ((bf16[8,648,48]{1,2,0:T(8,128)(2,1)}), bf16[8,648,48]{1,2,0:T(8,128)(2,1)S(1)}, u32[]{:S(2)}, u32[]{:S(2)}) async-start(bf16[8,648,48]{1,2,0:T(8,128)(2,1)} %bitcast.47), calls=%async_computation.1 | async-start | bytes 1179648 | tf_op jit(solution)/shard_map/all_to_all | solution.py:76

commit v2 on v0

v2 whole, which is shorter than its diff:
```python
import math

import jax
import jax.numpy as jnp
from jax import lax
from jax.experimental import pallas as pl
from jax.experimental.pallas import tpu as pltpu
from jax.sharding import PartitionSpec as P


G = 32
EPSILON = 1e-06
F32 = jnp.float32
BF16 = jnp.bfloat16
ROW_ROW = (((1,), (1,)), ((), ()))


def call(body, grid, ins, outs, shapes, scratch=(), flops=0, nbytes=0):
    return pl.pallas_call(
        body,
        grid=grid,
        in_specs=ins,
        out_specs=outs,
        out_shape=shapes,
        scratch_shapes=list(scratch),
        cost_estimate=pl.CostEstimate(flops=flops, bytes_accessed=nbytes, transcendentals=0),
        compiler_params=pltpu.CompilerParams(
            dimension_semantics=("arbitrary",) * len(grid), vmem_limit_bytes=56 * 2**20
        ),
    )


def whole(*shape):
    return pl.BlockSpec(shape, lambda *at: (0,) * len(shape))


def from_behind(value, axis, steps):
    count = lax.axis_size(axis)
    first, last = (max(0, -steps), min(count, count - steps))
    return lax.ppermute(value, axis, [(source, source + steps) for source in range(first, last)])


def group_mean(value):
    rows, channels = value.shape
    width = channels // G
    sums = jnp.broadcast_to(jnp.sum(value, axis=0, keepdims=True), (8, channels))
    left = lax.broadcasted_iota(jnp.int32, (channels, channels), 0) // width
    right = lax.broadcasted_iota(jnp.int32, (channels, channels), 1) // width
    mix = jnp.where(left == right, 1.0, 0.0).astype(F32)
    total = jnp.dot(sums, mix, precision=lax.Precision.HIGHEST, preferred_element_type=F32)
    return total[0:1] * (1.0 / (rows * width))


def normalize(value):
    center = value - group_mean(value)
    scale = lax.rsqrt(group_mean(center * center) + EPSILON)
    return center * scale, scale


def act_body(field_ref, act_ref):
    normed, _ = normalize(field_ref[0].astype(F32))
    act_ref[0] = (normed / (1.0 + jnp.exp(-normed))).astype(BF16)


def up_body(cot_ref, weight_ref, local_ref, prior_ref):
    channels = cot_ref.shape[-1]
    weight = weight_ref[...]
    parts = []
    for frame in range(2):
        pair = jnp.concatenate([cot_ref[2 * frame], cot_ref[2 * frame + 1]], axis=1)
        parts.append(lax.dot_general(pair, weight, ROW_ROW, preferred_element_type=F32))
    first, second = parts
    low, mid, high = (slice(k * channels, (k + 1) * channels) for k in range(3))
    local_ref[0] = first[:, high] + second[:, mid]
    local_ref[1] = second[:, high]
    prior_ref[0] = first[:, low].astype(BF16)
    prior_ref[1] = (first[:, mid] + second[:, low]).astype(BF16)


def turn_body(weight_ref, out_ref):
    for tap in range(3):
        out_ref[tap] = weight_ref[2 - tap].astype(F32).T.astype(BF16)


def fill_shifts(frames, cols_ref, breadth):
    rows, channels = frames[0].shape
    place = lax.broadcasted_iota(jnp.int32, (rows, channels), 0)
    wide = place % breadth
    for at, frame in enumerate(frames):
        value = frame.astype(F32)
        for wide_tap in range(3):
            moved = value
            if wide_tap != 1:
                moved = pltpu.roll(value, (1 - wide_tap) % rows, 0)
                edge = 0 if wide_tap == 0 else breadth - 1
                moved = jnp.where(wide == edge, 0.0, moved)
            for high_tap in range(3):
                shifted = moved
                if high_tap == 0:
                    shifted = jnp.concatenate(
                        [jnp.zeros((breadth, channels), F32), moved[: rows - breadth]], axis=0
                    )
                elif high_tap == 2:
                    shifted = jnp.concatenate(
                        [moved[breadth:], jnp.zeros((breadth, channels), F32)], axis=0
                    )
                tap = high_tap * 3 + wide_tap
                cols_ref[at * rows : (at + 1) * rows, tap * channels : (tap + 1) * channels] = (
                    shifted.astype(BF16)
                )


def accumulate(step, weight_ref, cols_ref, acc_ref):
    rows = acc_ref.shape[0]
    part = jnp.dot(
        cols_ref[pl.ds(pl.multiple_of(step * (rows // 2), rows // 2), rows), :],
        weight_ref[0],
        preferred_element_type=F32,
    )

    @pl.when(step == 0)
    def _():
        acc_ref[...] = part

    @pl.when(step > 0)
    def _():
        acc_ref[...] += part


def make_conv(breadth):
    def body(early_ref, late_ref, weight_ref, field_ref, hidden_ref, cols_ref, acc_ref):
        step = pl.program_id(0)

        @pl.when(step == 0)
        def _():
            frames = [early_ref[0], early_ref[1], late_ref[0], late_ref[1]]
            fill_shifts(frames, cols_ref, breadth)

        accumulate(step, weight_ref, cols_ref, acc_ref)

        @pl.when(step == 2)
        def _():
            rows = acc_ref.shape[0] // 2
            for frame in range(2):
                total = field_ref[frame].astype(F32) + acc_ref[frame * rows : (frame + 1) * rows]
                hidden_ref[frame] = total.astype(BF16)

    return body


def make_back(breadth):
    def body(
        early_ref, late_ref, weight_ref, field_ref, local_ref, next_ref, out_ref, cols_ref, acc_ref
    ):
        step = pl.program_id(0)

        @pl.when(step == 0)
        def _():
            frames = [early_ref[0], early_ref[1], late_ref[0], late_ref[1]]
            fill_shifts(frames, cols_ref, breadth)

        accumulate(step, weight_ref, cols_ref, acc_ref)

        @pl.when(step == 2)
        def _():
            rows = acc_ref.shape[0] // 2
            for frame in range(2):
                normed, scale = normalize(field_ref[frame].astype(F32))
                gate = 1.0 / (1.0 + jnp.exp(-normed))
                slope = gate * (1.0 + normed * (1.0 - gate))
                grad = acc_ref[frame * rows : (frame + 1) * rows] * slope
                inner = grad - group_mean(grad) - normed * group_mean(grad * normed)
                hidden_grad = local_ref[frame] + next_ref[frame].astype(F32)
                out_ref[frame] = (hidden_grad + scale * inner).astype(BF16)

    return body


def split_store(part, side, send_ref, keep_ref, times, at):
    rows, width = part.shape
    halves = part.reshape(times, rows // times, width)
    low = halves[:, : rows // times // 2]
    high = halves[:, rows // times // 2 :]
    send_ref[:, :, at : at + width] = jnp.where(side == 0, high, low).astype(BF16)
    keep_ref[:, :, at : at + width] = jnp.where(side == 0, low, high).astype(BF16)


def make_weight_grad(breadth, times):
    def body(side_ref, early_ref, late_ref, grad_ref, send_ref, keep_ref, cols_ref, turned_ref):
        step = pl.program_id(0)
        rows, channels = early_ref.shape[1:]

        @pl.when(step == 0)
        def _():
            frames = [early_ref[0], early_ref[1], late_ref[0], late_ref[1]]
            fill_shifts(frames, cols_ref, breadth)
            for frame in range(2):
                turned_ref[:, frame * rows : (frame + 1) * rows] = (
                    grad_ref[frame].astype(F32).T.astype(BF16)
                )

        start = pl.multiple_of(step * rows, rows)
        turned = turned_ref[...]
        total = cols_ref.shape[1]
        for at in range(0, total, 2 * channels):
            width = min(2 * channels, total - at)
            part = jnp.dot(
                turned,
                cols_ref[pl.ds(start, 2 * rows), at : at + width],
                preferred_element_type=F32,
            )
            split_store(part, side_ref[0], send_ref, keep_ref, times, at)

    return body


def make_up_grad(times):
    def body(side_ref, early_ref, late_ref, cot_ref, send_ref, keep_ref, cols_ref, turned_ref):
        rows, channels = early_ref.shape[1:]
        frames = [early_ref[0], early_ref[1], late_ref[0], late_ref[1]]
        for tap in range(3):
            for frame in range(2):
                cols_ref[
                    frame * rows : (frame + 1) * rows, tap * channels : (tap + 1) * channels
                ] = frames[frame + tap]
        for frame in range(2):
            for half in range(2):
                turned_ref[
                    half * channels : (half + 1) * channels, frame * rows : (frame + 1) * rows
                ] = cot_ref[2 * frame + half].astype(F32).T.astype(BF16)
        part = jnp.dot(turned_ref[...], cols_ref[...], preferred_element_type=F32)
        split_store(part, side_ref[0], send_ref, keep_ref, times, 0)

    return body


def swap_sides(value):
    return lax.ppermute(value, "dp", [(d, d ^ 1) for d in range(lax.axis_size("dp"))])


def place_of(device):
    time, data = divmod(device, 16)
    return [data // 4, time // 2, (data // 2 % 2) * 2 + time % 2, data % 2]


def device_at(x, y, z, core):
    return (y * 2 + z % 2) * 16 + x * 4 + z // 2 * 2 + core


def exchange(pieces, ring):
    got = [pieces[0]]
    for step in (1, 2, 3):
        pairs = []
        for device in range(128):
            place = place_of(device)
            place[ring] = (place[ring] + step) % 4
            pairs.append((device, device_at(*place)))
        got.append(lax.ppermute(pieces[step], ("tm", "dp"), pairs))
    return got


def added(refs):
    total = refs[0][...].astype(F32)
    for ref in refs[1:]:
        total = total + ref[...].astype(F32)
    return total


def join_body(place_ref, got_ref, keep_ref, *refs):
    row_refs, col_refs, hold_ref = refs[:4], refs[4:8], refs[8]
    step = pl.program_id(0)
    quarter = got_ref.shape[-1] // 4
    total = (got_ref[0].astype(F32) + keep_ref[0].astype(F32)).astype(BF16)
    for at in range(4):
        hold_ref[at] = total[0][:, at * quarter : (at + 1) * quarter]
    for slot in range(4):
        row_refs[slot][0] = hold_ref[lax.rem(place_ref[0] + slot, 4)]

        @pl.when(lax.rem(step - place_ref[1] + 4, 4) == slot)
        def _():
            col_refs[slot][...] = total[1]


def mid_body(place_ref, *refs):
    row_in, col_in, row_out, col_out = refs[:4], refs[4:8], refs[8:12], refs[12:16]
    row_hold, col_hold = refs[16:]
    quarter = col_in[0].shape[-1] // 4
    row_hold[...] = added(row_in).astype(BF16)
    total = added(col_in).astype(BF16)
    for at in range(4):
        col_hold[at] = total[:, at * quarter : (at + 1) * quarter]
    for slot in range(4):
        row_out[slot][...] = row_hold[lax.rem(place_ref[1] + slot, 4)]
        col_out[slot][...] = col_hold[lax.rem(place_ref[0] + slot, 4)]


def end_body(place_ref, *refs):
    outs, hold_ref = refs[8:12], refs[12]
    width = outs[0].shape[-1]
    for low in range(2):
        total = added(refs[4 * low : 4 * low + 4]).astype(BF16)
        for high in range(2):
            hold_ref[high * 2 + low] = total[:, high * width : (high + 1) * width]
    for slot in range(4):
        outs[slot][...] = hold_ref[lax.rem(place_ref[2] + slot, 4)]


def last_body(place_ref, *refs):
    total = added(refs[:4])
    width = total.shape[1] // 2
    low, high = total[:, :width], total[:, width:]
    refs[4][...] = jnp.where(place_ref[3] == 0, low, high)
    refs[5][...] = jnp.where(place_ref[3] == 0, high, low)


def reduce_blocks(send, keep):
    times, cols, rows = send.shape
    data, time = lax.axis_index("dp"), lax.axis_index("tm")
    place = jnp.stack([data // 4, time // 2, (data // 2 % 2) * 2 + time % 2, data % 2])
    place = place.astype(jnp.int32)
    scalars = pl.BlockSpec(memory_space=pltpu.SMEM)

    def small(body, arrays, shapes, scratch):
        return call(
            body,
            (1,),
            [scalars] + [whole(*array.shape) for array in arrays],
            [whole(*shape.shape) for shape in shapes],
            shapes,
            scratch,
            flops=1000,
            nbytes=2 * times * cols * rows,
        )(place, *arrays)

    def shape(*dims):
        return jax.ShapeDtypeStruct(dims, BF16)

    got = swap_sides(send)
    blocks = (4, 2, cols, rows)
    pair_spec = pl.BlockSpec((1, 2, cols, rows), lambda k: (k, 0, 0, 0))
    row_spec = pl.BlockSpec((1, cols, rows // 4), lambda k: (k, 0, 0))
    out = call(
        join_body,
        (4,),
        [scalars, pair_spec, pair_spec],
        [row_spec] * 4 + [whole(cols, rows)] * 4,
        [shape(4, cols, rows // 4)] * 4 + [shape(cols, rows)] * 4,
        [pltpu.VMEM((4, cols, rows // 4), BF16)],
        flops=1000,
        nbytes=6 * times * cols * rows,
    )(place, got.reshape(blocks), keep.reshape(blocks))
    first = exchange(out[4:], 1)
    second = exchange(out[:4], 0)
    hold = pltpu.VMEM((4, cols, rows // 4), BF16)
    out = small(mid_body, second + first, [shape(cols, rows // 4)] * 8, [hold, hold])
    first = exchange(out[:4], 1)
    second = exchange(out[4:], 0)
    hold = pltpu.VMEM((4, cols, rows // 8), BF16)
    out = small(end_body, first + second, [shape(cols, rows // 8)] * 4, [hold])
    out = exchange(out, 2)
    half = jax.ShapeDtypeStruct((cols, rows // 16), F32)
    mine, other = small(last_body, out, [half, half], [])
    got = swap_sides(other)
    side = data % 2
    full = jnp.where(
        side == 0, jnp.concatenate([mine, got], axis=0), jnp.concatenate([got, mine], axis=0)
    )
    return full.T


def join_pair(send, keep):
    swapped = swap_sides(send)
    return (keep.astype(F32) + swapped.astype(F32)).astype(BF16)


def over_times(pair):
    spread = lax.all_to_all(pair, "tm", 0, 0, tiled=True)
    return jnp.sum(spread.astype(F32), axis=0).astype(BF16)


def over_data(rowsum):
    cols, rows = rowsum.shape
    chips = lax.axis_size("dp") // 2
    side = lax.axis_index("dp") % 2
    blocks = rowsum.reshape(cols, chips, rows // chips).transpose(1, 0, 2)
    groups = [[2 * chip + own for chip in range(chips)] for own in range(2)]
    spread = lax.all_to_all(blocks, "dp", 0, 0, axis_index_groups=groups, tiled=True)
    total = jnp.sum(spread.astype(F32), axis=0).reshape(cols, 2, rows // chips // 2)
    mine = lax.dynamic_index_in_dim(total, side, 1, keepdims=False)
    other = lax.dynamic_index_in_dim(total, 1 - side, 1, keepdims=False)
    got = swap_sides(other)
    both = jnp.where(
        side == 0, jnp.concatenate([mine, got], axis=0), jnp.concatenate([got, mine], axis=0)
    )
    return both.T


def step(features, conv_weight, up_weight, cotangent):
    crops, frames, height, breadth, channels = features.shape
    rows = height * breadth
    times = lax.axis_size("tm")
    data = lax.axis_size("dp")
    scale = 1.0 / math.sqrt(crops * frames * rows * times * data)
    field = features.reshape(frames, rows, channels)
    cot = cotangent.reshape(2 * frames, rows, channels)
    side = (lax.axis_index("dp") % 2).astype(jnp.int32).reshape(1)
    block = (frames, rows, channels)
    square = 2 * channels * channels
    act = call(
        act_body,
        (frames,),
        [pl.BlockSpec((1, rows, channels), lambda f: (f, 0, 0))],
        pl.BlockSpec((1, rows, channels), lambda f: (f, 0, 0)),
        jax.ShapeDtypeStruct(block, BF16),
        flops=20 * frames * rows * channels,
        nbytes=4 * frames * rows * channels,
    )(field)
    act_prior = from_behind(act, "tm", 1)
    local, prior_part = call(
        up_body,
        (1,),
        [whole(*cot.shape), whole(*up_weight.shape)],
        [whole(*block), whole(*block)],
        [jax.ShapeDtypeStruct(block, F32), jax.ShapeDtypeStruct(block, BF16)],
        flops=6 * frames * rows * square,
        nbytes=10 * frames * rows * channels,
    )(cot, up_weight)
    next_part = from_behind(prior_part, "tm", -1)
    taps = conv_weight.reshape(27, channels, channels)
    turned = call(
        turn_body,
        (9,),
        [pl.BlockSpec((3, channels, channels), lambda n: (8 - n, 0, 0))],
        pl.BlockSpec((3, channels, channels), lambda n: (n, 0, 0)),
        jax.ShapeDtypeStruct(taps.shape, BF16),
        flops=27 * square,
        nbytes=4 * 27 * channels * channels,
    )(taps)
    turned = turned.reshape(3, 9 * channels, channels)
    conv_grad = (local + next_part.astype(F32)).astype(BF16)
    conv_next = from_behind(conv_grad, "tm", -1)
    columns = pltpu.VMEM((4 * rows, 9 * channels), BF16)
    sums = pltpu.VMEM((frames * rows, channels), F32)
    kernel_spec = pl.BlockSpec((1, 9 * channels, channels), lambda k: (k, 0, 0))
    act_prior, turned = lax.optimization_barrier((act_prior, turned))
    hidden = call(
        make_conv(breadth),
        (3,),
        [whole(*block), whole(*block), kernel_spec, whole(*block)],
        whole(*block),
        jax.ShapeDtypeStruct(block, BF16),
        [columns, sums],
        flops=27 * frames * rows * square,
        nbytes=2 * 27 * channels * channels,
    )(act_prior, act, conv_weight.reshape(3, 9 * channels, channels), field)
    hidden_prior = from_behind(hidden, "tm", 1)
    cut = channels // times // 2
    half = jax.ShapeDtypeStruct((times, cut, 27 * channels), BF16)
    half_spec = pl.BlockSpec((times, cut, 9 * channels), lambda k: (0, 0, k))
    send, keep = call(
        make_weight_grad(breadth, times),
        (3,),
        [pl.BlockSpec(memory_space=pltpu.SMEM), whole(*block), whole(*block), whole(*block)],
        [half_spec, half_spec],
        [half, half],
        [columns, pltpu.VMEM((channels, frames * rows), BF16)],
        flops=27 * frames * rows * square,
        nbytes=4 * 27 * channels * channels,
    )(side, act_prior, act, conv_grad)
    grad_conv = reduce_blocks(send, keep) * scale
    up_half = jax.ShapeDtypeStruct((times, channels // times, 3 * channels), BF16)
    up_send, up_keep = call(
        make_up_grad(times),
        (1,),
        [pl.BlockSpec(memory_space=pltpu.SMEM), whole(*block), whole(*block), whole(*cot.shape)],
        [whole(*up_half.shape), whole(*up_half.shape)],
        [up_half, up_half],
        [
            pltpu.VMEM((frames * rows, 3 * channels), BF16),
            pltpu.VMEM((2 * channels, frames * rows), BF16),
        ],
        flops=6 * frames * rows * square,
        nbytes=12 * channels * channels,
    )(side, hidden_prior, hidden, cot)
    grad_up = over_data(over_times(join_pair(up_send, up_keep))) * scale
    features_grad = call(
        make_back(breadth),
        (3,),
        [whole(*block), whole(*block), kernel_spec] + [whole(*block)] * 3,
        whole(*block),
        jax.ShapeDtypeStruct(block, BF16),
        [columns, sums],
        flops=27 * frames * rows * square,
        nbytes=2 * 27 * channels * channels,
    )(conv_grad, conv_next, turned, field, local, next_part)
    return (features_grad.reshape(features.shape), grad_conv, grad_up)


def solution(mesh):
    in_specs = (P("dp", "tm", None, None, None), P(), P(), P("dp", "tm", None, None, None))
    out_specs = (P("dp", "tm", None, None, None), P("dp", "tm"), P("dp", "tm"))
    return jax.shard_map(step, mesh=mesh, in_specs=in_specs, out_specs=out_specs, check_vma=False)
```

time: 497 us -> 199 us (0.40)
  waiting for transfers between devices: 318 us -> 47.9 us
  local copies, waits for them, and re-layouts: 95.1 us -> 5.65 us
  Pallas kernels: 0 us -> 82.2 us
  matrix products: 46.1 us -> 0 us
  starting transfers between devices: 12.4 us -> 55.2 us
  between operations: 14.2 us -> 0.95 us
  other arithmetic: 10.8 us -> 5.37 us
    unnamed x7 -> x0, waiting for transfers between devices: 220 us -> none
    pallas_call x0 -> x11, Pallas kernels: none -> 82.2 us  [the longest x1 17.6 us: step(): call(make_back(breadth), (3,), [whole(*block), whole(*block), kernel_spec...]
    reduce_scatter x1 -> x0, waiting for transfers between devices: 66.3 us -> none  [shards(): lax.psum_scatter(contract_rows(hidden_cols, up_flat), 'dp', scatter_dimen...]
    dot_general x5 -> x0, matrix products: 46.1 us -> none  [the longest x2 18.6 us: contract_rows(): lax.dot_general(left, right, (((0,), (0,)), ((), ())), preferred_element_...]
    unnamed x81 -> x56, local copies, waits for them, and re-layouts: 44.6 us -> 4.36 us
    ppermute x0 -> x19, starting transfers between devices: none -> 32.3 us  [the longest x15 32.2 us: exchange(): got.append(lax.ppermute(pieces[step], ('tm', 'dp'), pairs))]
    ppermute x0 -> x19, waiting for transfers between devices: none -> 26.1 us  [the longest x15 25.3 us: exchange(): got.append(lax.ppermute(pieces[step], ('tm', 'dp'), pairs))]
    transpose x4 -> x1, local copies, waits for them, and re-layouts: 25.1 us -> 0.71 us  [over_data(): blocks = rowsum.reshape(cols, chips, rows // chips).transpose(1, 0, 2)]
  transfers between devices with their start and end apart: 8 -> 25, of which waited for: 7 -> 8; matrix products, arithmetic and copies ran while one was open for 12% -> 2% of each run, Pallas kernels for 0% -> 33%
where the time goes in v2:
time: 199 us; the launch traced here: 197 us
  Pallas kernels  82.2 us (41%)
  starting transfers between devices  55.2 us (28%)
  waiting for transfers between devices  47.9 us (24%)
  local copies, waits for them, and re-layouts  5.65 us (3%)
  other arithmetic  5.37 us (3%)
    ppermute x15, starting transfers between devices, exchange(): got.append(lax.ppermute(pieces[step], ('tm', 'dp'), pairs))  32.2 us
    ppermute x15, waiting for transfers between devices, exchange(): got.append(lax.ppermute(pieces[step], ('tm', 'dp'), pairs))  25.3 us
    ppermute x4, waiting for transfers between devices, from_behind(): lax.ppermute(value, axis, [(source, source + steps) for source in range(f...  21.8 us
    pallas_call x1, Pallas kernels, step(): call(make_back(breadth), (3,), [whole(*block), whole(*block), kernel_spec...  17.6 us
    pallas_call x1, Pallas kernels, step(): call(make_conv(breadth), (3,), [whole(*block), whole(*block), kernel_spec...  13.6 us
    pallas_call x1, Pallas kernels, step(): call(make_weight_grad(breadth, times), (3,), [pl.BlockSpec(memory_space=p...  12.2 us
    pallas_call x1, Pallas kernels, step(): call(turn_body, (9,), [pl.BlockSpec((3, channels, channels), lambda n: (8...  11.1 us
    ppermute x4, starting transfers between devices, from_behind(): lax.ppermute(value, axis, [(source, source + steps) for source in range(f...  11 us
  transfers between devices with their start and end apart: 25, of which 8 were waited for; matrix products, arithmetic and copies ran while one was open for 2% of the time, Pallas kernels for 33%

profile of v2, /device:TPU:0, one launch (start us, length us, event | category | flops | bytes accessed | tf_op | source)
XLA Modules:
  0.0 197.3 jit_solution(14653211473187101433)
XLA Ops:
  0.6 4.0 %shard_map.68.late_ref = bf16[2,384,384]{2,1,0:T(8,128)(2,1)} custom-call(bf16[2,384,384]{2,1,0:T(8,128)(2,1)} %bitcast.24), custom_call_target="tpu_custom_call" | custom-call | flops 5898240 | bytes 1179648 | tf_op jit(solution)/shard_map/pallas_call | solution.py:409
  4.6 4.0 %collective-permute-start.2 = (bf16[2,384,384]{2,1,0:T(8,128)(2,1)}, bf16[2,384,384]{2,1,0:T(8,128)(2,1)S(1)}, u32[]{:S(2)}, u32[]{:S(2)}) collective-permute-start(bf16[2,384,384]{2,1,0:T(8,128)(2,1)} %shard_map.68.late_ref), channel_id=1, source_target_pairs={{0,16},{16,32},{32,48},{48,64},{64,80},{80,96},{96,112},{1,17},{17... | collective-permute-start | bytes 1769480 | tf_op jit(solution)/shard_map/ppermute | solution.py:40
  8.6 4.6 %shard_map.67 = (f32[2,384,384]{2,1,0:T(8,128)}, bf16[2,384,384]{2,1,0:T(8,128)(2,1)}) custom-call(bf16[4,384,384]{2,1,0:T(8,128)(2,1)} %bitcast.29, bf16[1152,768]{1,0:T(8,128)(2,1)} %weight_ref.1), custom_call_target="tpu_custom_call" | custom-call | flops 1358954496 | bytes 2949120 | tf_op jit(solution)/shard_map/pallas_call | solution.py:419
  14.5 11.1 %shard_map.69 = bf16[27,384,384]{2,1,0:T(8,128)(2,1)} custom-call(bf16[27,384,384]{2,1,0:T(8,128)(2,1)} %bitcast.19), custom_call_target="tpu_custom_call" | custom-call | flops 7962624 | bytes 15925248 | tf_op jit(solution)/shard_map/pallas_call | solution.py:430
  25.6 8.5 %collective-permute-done.2.early_ref = bf16[2,384,384]{2,1,0:T(8,128)(2,1)S(1)} collective-permute-done((bf16[2,384,384]{2,1,0:T(8,128)(2,1)}, bf16[2,384,384]{2,1,0:T(8,128)(2,1)S(1)}, u32[]{:S(2)}, u32[]{:S(2)}) %collective-permute-start.2) | collective-permute-done | bytes 589856 | tf_op jit(solution)/shard_map/ppermute | solution.py:40
  35.1 12.2 %shard_map.71 = (bf16[8,24,10368]{2,1,0:T(8,128)(2,1)}, bf16[8,24,10368]{2,1,0:T(8,128)(2,1)}) custom-call(s32[1]{0:T(128)} %bitcast.8.side_ref, bf16[2,384,384]{2,1,0:T(8,128)(2,1)} %copy-done.20, bf16[2,384,384]{2,1,0:T(8,128)(2,1)} %shard_map.68.late_ref, bf16[2,384,384]{2,1,0:T(8,128)(2,1)} %add_convert_fusion.1.early_ref.grad_ref), custom_call_target="tpu_custom_call" | custom-call | flops 6115295232 | bytes 15925248 | tf_op jit(solution)/shard_map/pallas_call | solution.py:460
  47.3 13.6 %shard_map.76.late_ref = bf16[2,384,384]{2,1,0:T(8,128)(2,1)} custom-call(bf16[2,384,384]{2,1,0:T(8,128)(2,1)} %copy-done.20, bf16[2,384,384]{2,1,0:T(8,128)(2,1)} %shard_map.68.late_ref, bf16[3,3456,384]{2,1,0:T(8,128)(2,1)} %bitcast.20, bf16[2,384,384]{2,1,0:T(8,128)(2,1)} %bitcast.25), custom_call_target="tpu_custom_call" | custom-call | flops 6115295232 | bytes 7962624 | tf_op jit(solution)/shard_map/pallas_call | solution.py:446
  60.9 4.5 %collective-permute-start.20 = (bf16[2,384,384]{2,1,0:T(8,128)(2,1)}, bf16[2,384,384]{2,1,0:T(8,128)(2,1)S(1)}, u32[]{:S(2)}, u32[]{:S(2)}) collective-permute-start(bf16[2,384,384]{2,1,0:T(8,128)(2,1)} %shard_map.76.late_ref), channel_id=1, source_target_pairs={{0,16},{16,32},{32,48},{48,64},{64,80},{80,96},{96,112},{1,17},{17... | collective-permute-start | bytes 1769480 | tf_op jit(solution)/shard_map/ppermute | solution.py:40
  65.4 13.3 %collective-permute-done.20.early_ref = bf16[2,384,384]{2,1,0:T(8,128)(2,1)S(1)} collective-permute-done((bf16[2,384,384]{2,1,0:T(8,128)(2,1)}, bf16[2,384,384]{2,1,0:T(8,128)(2,1)S(1)}, u32[]{:S(2)}, u32[]{:S(2)}) %collective-permute-start.20) | collective-permute-done | bytes 589856 | tf_op jit(solution)/shard_map/ppermute | solution.py:40
  79.6 4.8 %shard_map.77 = (bf16[8,48,1152]{2,1,0:T(8,128)(2,1)}, bf16[8,48,1152]{2,1,0:T(8,128)(2,1)}) custom-call(s32[1]{0:T(128)} %bitcast.8.side_ref, bf16[2,384,384]{2,1,0:T(8,128)(2,1)} %copy-done.21, bf16[2,384,384]{2,1,0:T(8,128)(2,1)} %shard_map.76.late_ref, bf16[4,384,384]{2,1,0:T(8,128)(2,1)} %bitcast.30), custom_call_target="tpu_custom_call" | custom-call | flops 1358954496 | bytes 1769472 | tf_op jit(solution)/shard_map/pallas_call | solution.py:472
  85.0 6.6 %shard_map.72 = (bf16[4,24,2592]{2,1,0:T(8,128)(2,1)}, bf16[4,24,2592]{2,1,0:T(8,128)(2,1)}, bf16[4,24,2592]{2,1,0:T(8,128)(2,1)}, bf16[4,24,2592]{2,1,0:T(8,128...) custom-call(s32[4]{0:T(128)} %pad_add_fusion.place_ref, ...), custom_call_target="tpu_custom_call" | custom-call | flops 1000 | bytes 11943936 | tf_op jit(solution)/shard_map/pallas_call | solution.py:342
  91.6 3.9 %collective-permute-start.7 = (bf16[24,10368]{1,0:T(8,128)(2,1)}, bf16[24,10368]{1,0:T(8,128)(2,1)S(1)}, u32[]{:S(2)}, u32[]{:S(2)}) collective-permute-start(bf16[24,10368]{1,0:T(8,128)(2,1)} %get-tuple-element.44), channel_id=1, source_target_pairs={{0,32},{1,33},{2,34},{3,35},{4,36},{5,37},{6,38},{7,39},{8,40},{9,... | collective-permute-start | bytes 1493000 | tf_op jit(solution)/shard_map/ppermute | solution.py:258
  96.6 4.3 %all-to-all-start = ((bf16[8,48,1152]{2,1,0:T(8,128)(2,1)}), bf16[8,48,1152]{2,1,0:T(8,128)(2,1)S(1)}, u32[]{:S(2)}, u32[]{:S(2)}) async-start(bf16[8,48,1152]{2,1,0:T(8,128)(2,1)} %add_convert_fusion), calls=%async_computation | async-start | bytes 1769472 | tf_op jit(solution)/shard_map/all_to_all | solution.py:377
  100.9 3.5 %collective-permute-start.8 = (bf16[24,10368]{1,0:T(8,128)(2,1)S(1)}, bf16[24,10368]{1,0:T(8,128)(2,1)S(1)}, u32[]{:S(2)}, u32[]{:S(2)}) collective-permute-start(bf16[24,10368]{1,0:T(8,128)(2,1)S(1)} %copy-done.23), channel_id=1, source_target_pairs={{0,64},{1,65},{2,66},{3,67},{4,68},{5,69},{6,70},{7,71},{8,72},{9,... | collective-permute-start | bytes 1493000 | tf_op jit(solution)/shard_map/ppermute | solution.py:258
  105.6 1.5 collective-permute-start.4
  107.1 2.7 %collective-permute-start.5 = (bf16[4,24,2592]{2,1,0:T(8,128)(2,1)}, bf16[4,24,2592]{2,1,0:T(8,128)(2,1)S(1)}, u32[]{:S(2)}, u32[]{:S(2)}) collective-permute-start(bf16[4,24,2592]{2,1,0:T(8,128)(2,1)} %get-tuple-element.41), channel_id=1, source_target_pairs={{0,8},{1,9},{2,10},{3,11},{4,12},{5,13},{6,14},{7,15},{8,0},{9,1},... | collective-permute-start | bytes 1493000 | tf_op jit(solution)/shard_map/ppermute | solution.py:258
  109.9 2.2 %collective-permute-start.6 = (bf16[4,24,2592]{2,1,0:T(8,128)(2,1)S(1)}, bf16[4,24,2592]{2,1,0:T(8,128)(2,1)S(1)}, u32[]{:S(2)}, u32[]{:S(2)}) collective-permute-start(bf16[4,24,2592]{2,1,0:T(8,128)(2,1)S(1)} %copy-done.22), channel_id=1, source_target_pairs={{0,12},{1,13},{2,14},{3,15},{4,0},{5,1},{6,2},{7,3},{8,4},{9,5},{1... | collective-permute-start | bytes 1493000 | tf_op jit(solution)/shard_map/ppermute | solution.py:258
  112.0 18.6 %collective-permute-done.8.refs_6_ = bf16[24,10368]{1,0:T(8,128)(2,1)S(1)} collective-permute-done((bf16[24,10368]{1,0:T(8,128)(2,1)S(1)}, bf16[24,10368]{1,0:T(8,128)(2,1)S(1)}, u32[]{:S(2)}, u32[]{:S(2)}) %collective-permute-start.8) | collective-permute-done | bytes 497696 | tf_op jit(solution)/shard_map/ppermute | solution.py:258
  131.9 3.7 %collective-permute-done.9.refs_7_ = bf16[24,10368]{1,0:T(8,128)(2,1)S(1)} collective-permute-done((bf16[24,10368]{1,0:T(8,128)(2,1)}, bf16[24,10368]{1,0:T(8,128)(2,1)S(1)}, u32[]{:S(2)}, u32[]{:S(2)}) %collective-permute-start.9) | collective-permute-done | bytes 497696 | tf_op jit(solution)/shard_map/ppermute | solution.py:258
  137.0 3.8 %shard_map.73 = (bf16[24,2592]{1,0:T(8,128)(2,1)}, bf16[24,2592]{1,0:T(8,128)(2,1)}, bf16[24,2592]{1,0:T(8,128)(2,1)}, bf16[24,2592]{1,0:T(8,128)(2,1)}, bf16[24...) custom-call(s32[4]{0:T(128)} %pad_add_fusion.place_ref, ...), custom_call_target="tpu_custom_call" | custom-call | flops 1000 | bytes 3981312 | tf_op jit(solution)/shard_map/pallas_call | solution.py:324
  144.7 7.6 %all-to-all-start.1 = ((bf16[8,48,144]{2,1,0:T(8,128)(2,1)}), bf16[8,48,144]{2,1,0:T(8,128)(2,1)S(1)}, u32[]{:S(2)}, u32[]{:S(2)}) async-start(bf16[8,48,144]{2,1,0:T(8,128)(2,1)} %copy.8), calls=%async_computation.1 | async-start | bytes 393216 | tf_op jit(solution)/shard_map/all_to_all | solution.py:387
  152.4 2.6 %collective-permute-start.12 = (bf16[24,2592]{1,0:T(8,128)(2,1)S(1)}, bf16[24,2592]{1,0:T(8,128)(2,1)S(1)}, u32[]{:S(2)}, u32[]{:S(2)}) collective-permute-start(bf16[24,2592]{1,0:T(8,128)(2,1)S(1)} %copy-done.27), channel_id=1, source_target_pairs={{0,96},{1,97},{2,98},{3,99},{4,100},{5,101},{6,102},{7,103},{8,104... | collective-permute-start | bytes 373256 | tf_op jit(solution)/shard_map/ppermute | solution.py:258
  155.0 1.9 collective-permute-start.13
  156.9 2.8 %collective-permute-start.14 = (bf16[24,2592]{1,0:T(8,128)(2,1)S(1)}, bf16[24,2592]{1,0:T(8,128)(2,1)S(1)}, u32[]{:S(2)}, u32[]{:S(2)}) collective-permute-start(bf16[24,2592]{1,0:T(8,128)(2,1)S(1)} %copy-done.25), channel_id=1, source_target_pairs={{0,8},{1,9},{2,10},{3,11},{4,12},{5,13},{6,14},{7,15},{8,0},{9,1},... | collective-permute-start | bytes 373256 | tf_op jit(solution)/shard_map/ppermute | solution.py:258
  159.7 1.5 collective-permute-start.15
  162.1 1.8 collective-permute-done.14.refs_6_
  165.3 2.2 %shard_map.74 = (bf16[24,1296]{1,0:T(8,128)(2,1)}, bf16[24,1296]{1,0:T(8,128)(2,1)}, bf16[24,1296]{1,0:T(8,128)(2,1)}, bf16[24,1296]{1,0:T(8,128)(2,1)}) custom-call(s32[4]{0:T(128)} %pad_add_fusion.place_ref, bf16[24,2592]{1,0:T(8,128)(2,1)} %get-tuple-element.47.refs_0_, bf16[24,2592]{1,0:T(8,128)(2,1)} %copy-done.10, bf16[24,2592]{1,0:T(8,128)(2,1)} %copy-done.11, ...), custom_call_target="tpu_custom_call" | custom-call | flops 1000 | bytes 3981312 | tf_op jit(solution)/shard_map/pallas_call | solution.py:324
  167.6 3.5 %collective-permute-start.17 = (bf16[24,1296]{1,0:T(8,128)(2,1)}, bf16[24,1296]{1,0:T(8,128)(2,1)S(1)}, u32[]{:S(2)}, u32[]{:S(2)}) collective-permute-start(bf16[24,1296]{1,0:T(8,128)(2,1)} %get-tuple-element.57), channel_id=1, source_target_pairs={{0,2},{1,3},{2,0},{3,1},{4,6},{5,7},{6,4},{7,5},{8,10},{9,11},{10,... | collective-permute-start | bytes 186632 | tf_op jit(solution)/shard_map/ppermute | solution.py:258
  171.0 2.1 %collective-permute-start.18 = (bf16[24,1296]{1,0:T(8,128)(2,1)}, bf16[24,1296]{1,0:T(8,128)(2,1)S(1)}, u32[]{:S(2)}, u32[]{:S(2)}) collective-permute-start(bf16[24,1296]{1,0:T(8,128)(2,1)} %get-tuple-element.58), channel_id=1, source_target_pairs={{0,18},{1,19},{2,16},{3,17},{4,22},{5,23},{6,20},{7,21},{8,26},{9,... | collective-permute-start | bytes 186632 | tf_op jit(solution)/shard_map/ppermute | solution.py:258
  174.0 17.6 %shard_map.70 = bf16[2,384,384]{2,1,0:T(8,128)(2,1)} custom-call(bf16[2,384,384]{2,1,0:T(8,128)(2,1)} %add_convert_fusion.1.early_ref.grad_ref, bf16[2,384,384]{2,1,0:T(8,128)(2,1)} %copy-done.19, bf16[3,3456,384]{2,1,0:T(8,128)(2,1)} %bitcast.21, bf16[2,384,384]{2,1,0:T(8,128)(2,1)} %bitcast.26, f32[2,384,384]{2,1,0:T(8,128)} %get-tuple-element.33.local_ref, ...), custom_call_target="tpu_custom_call" | custom-call | flops 6115295232 | bytes 7962624 | tf_op jit(solution)/shard_map/pallas_call | solution.py:486
  192.4 1.8 shard_map.75
  195.6 1.6 fusion.1
  (98 shorter events, 18.2 us)
Async XLA Ops:
  4.6 29.5 %collective-permute-start.2 = (bf16[2,384,384]{2,1,0:T(8,128)(2,1)}, bf16[2,384,384]{2,1,0:T(8,128)(2,1)S(1)}, u32[]{:S(2)}, u32[]{:S(2)}) collective-permute-start(bf16[2,384,384]{2,1,0:T(8,128)(2,1)} %shard_map.68.late_ref), channel_id=1, source_target_pairs={{0,16},{16,32},{32,48},{48,64},{64,80},{80,96},{96,112},{1,17},{17... | collective-permute-start | bytes 1769480 | tf_op jit(solution)/shard_map/ppermute | solution.py:40
  13.2 20.9 %collective-permute-start = (bf16[2,384,384]{2,1,0:T(8,128)(2,1)}, bf16[2,384,384]{2,1,0:T(8,128)(2,1)S(1)}, u32[]{:S(2)}, u32[]{:S(2)}) collective-permute-start(bf16[2,384,384]{2,1,0:T(8,128)(2,1)} %get-tuple-element.34), channel_id=1, source_target_pairs={{16,0},{32,16},{48,32},{64,48},{80,64},{96,80},{112,96},{17,1},{33... | collective-permute-start | bytes 1769480 | tf_op jit(solution)/shard_map/ppermute | solution.py:40
  14.5 19.6 %copy-start = (f32[2,384,384]{2,1,0:T(8,128)S(1)}, f32[2,384,384]{2,1,0:T(8,128)}, u32[]{:S(2)}) copy-start(f32[2,384,384]{2,1,0:T(8,128)} %get-tuple-element.33.local_ref) | copy-start | bytes 3538948
  47.3 37.6 %collective-permute-start.3 = (bf16[8,24,10368]{2,1,0:T(8,128)(2,1)}, bf16[8,24,10368]{2,1,0:T(8,128)(2,1)}, u32[]{:S(2)}, u32[]{:S(2)}) collective-permute-start(bf16[8,24,10368]{2,1,0:T(8,128)(2,1)} %get-tuple-element.37), channel_id=1, source_target_pairs={{0,1},{1,0},{2,3},{3,2},{4,5},{5,4},{6,7},{7,6},{8,9},{9,8},{10,11... | collective-permute-start | bytes 11943944 | tf_op jit(solution)/shard_map/ppermute | solution.py:238
  60.9 17.8 %collective-permute-start.20 = (bf16[2,384,384]{2,1,0:T(8,128)(2,1)}, bf16[2,384,384]{2,1,0:T(8,128)(2,1)S(1)}, u32[]{:S(2)}, u32[]{:S(2)}) collective-permute-start(bf16[2,384,384]{2,1,0:T(8,128)(2,1)} %shard_map.76.late_ref), channel_id=1, source_target_pairs={{0,16},{16,32},{32,48},{48,64},{64,80},{80,96},{96,112},{1,17},{17... | collective-permute-start | bytes 1769480 | tf_op jit(solution)/shard_map/ppermute | solution.py:40
  84.4 11.1 %collective-permute-start.21 = (bf16[8,48,1152]{2,1,0:T(8,128)(2,1)}, bf16[8,48,1152]{2,1,0:T(8,128)(2,1)S(1)}, u32[]{:S(2)}, u32[]{:S(2)}) collective-permute-start(bf16[8,48,1152]{2,1,0:T(8,128)(2,1)} %get-tuple-element.62), channel_id=1, source_target_pairs={{0,1},{1,0},{2,3},{3,2},{4,5},{5,4},{6,7},{7,6},{8,9},{9,8},{10,11... | collective-permute-start | bytes 2654216 | tf_op jit(solution)/shard_map/ppermute | solution.py:238
  91.6 18.3 %collective-permute-start.7 = (bf16[24,10368]{1,0:T(8,128)(2,1)}, bf16[24,10368]{1,0:T(8,128)(2,1)S(1)}, u32[]{:S(2)}, u32[]{:S(2)}) collective-permute-start(bf16[24,10368]{1,0:T(8,128)(2,1)} %get-tuple-element.44), channel_id=1, source_target_pairs={{0,32},{1,33},{2,34},{3,35},{4,36},{5,37},{6,38},{7,39},{8,40},{9,... | collective-permute-start | bytes 1493000 | tf_op jit(solution)/shard_map/ppermute | solution.py:258
  95.4 14.4 %copy-start.22 = (bf16[4,24,2592]{2,1,0:T(8,128)(2,1)S(1)}, bf16[4,24,2592]{2,1,0:T(8,128)(2,1)}, u32[]{:S(2)}) copy-start(bf16[4,24,2592]{2,1,0:T(8,128)(2,1)} %get-tuple-element.42) | copy-start | bytes 1492996
  95.4 35.2 %copy-start.3 = (bf16[2,384,384]{2,1,0:T(8,128)(2,1)S(1)}, bf16[2,384,384]{2,1,0:T(8,128)(2,1)}, u32[]{:S(2)}) copy-start(bf16[2,384,384]{2,1,0:T(8,128)(2,1)} %add_convert_fusion.1.early_ref.grad_ref) | copy-start | bytes 1769476
  96.6 47.0 %all-to-all-start = ((bf16[8,48,1152]{2,1,0:T(8,128)(2,1)}), bf16[8,48,1152]{2,1,0:T(8,128)(2,1)S(1)}, u32[]{:S(2)}, u32[]{:S(2)}) async-start(bf16[8,48,1152]{2,1,0:T(8,128)(2,1)} %add_convert_fusion), calls=%async_computation | async-start | bytes 1769472 | tf_op jit(solution)/shard_map/all_to_all | solution.py:377
  100.9 29.7 %collective-permute-start.8 = (bf16[24,10368]{1,0:T(8,128)(2,1)S(1)}, bf16[24,10368]{1,0:T(8,128)(2,1)S(1)}, u32[]{:S(2)}, u32[]{:S(2)}) collective-permute-start(bf16[24,10368]{1,0:T(8,128)(2,1)S(1)} %copy-done.23), channel_id=1, source_target_pairs={{0,64},{1,65},{2,66},{3,67},{4,68},{5,69},{6,70},{7,71},{8,72},{9,... | collective-permute-start | bytes 1493000 | tf_op jit(solution)/shard_map/ppermute | solution.py:258
  104.5 31.1 %collective-permute-start.9 = (bf16[24,10368]{1,0:T(8,128)(2,1)}, bf16[24,10368]{1,0:T(8,128)(2,1)S(1)}, u32[]{:S(2)}, u32[]{:S(2)}) collective-permute-start(bf16[24,10368]{1,0:T(8,128)(2,1)} %get-tuple-element.46), channel_id=1, source_target_pairs={{0,96},{1,97},{2,98},{3,99},{4,100},{5,101},{6,102},{7,103},{8,104... | collective-permute-start | bytes 1493000 | tf_op jit(solution)/shard_map/ppermute | solution.py:258
  105.6 29.9 %collective-permute-start.4 = (bf16[4,24,2592]{2,1,0:T(8,128)(2,1)}, bf16[4,24,2592]{2,1,0:T(8,128)(2,1)S(1)}, u32[]{:S(2)}, u32[]{:S(2)}) collective-permute-start(bf16[4,24,2592]{2,1,0:T(8,128)(2,1)} %get-tuple-element.40), channel_id=1, source_target_pairs={{0,4},{1,5},{2,6},{3,7},{4,8},{5,9},{6,10},{7,11},{8,12},{9,13},{1... | collective-permute-start | bytes 1493000 | tf_op jit(solution)/shard_map/ppermute | solution.py:258
  107.1 28.4 %collective-permute-start.5 = (bf16[4,24,2592]{2,1,0:T(8,128)(2,1)}, bf16[4,24,2592]{2,1,0:T(8,128)(2,1)S(1)}, u32[]{:S(2)}, u32[]{:S(2)}) collective-permute-start(bf16[4,24,2592]{2,1,0:T(8,128)(2,1)} %get-tuple-element.41), channel_id=1, source_target_pairs={{0,8},{1,9},{2,10},{3,11},{4,12},{5,13},{6,14},{7,15},{8,0},{9,1},... | collective-permute-start | bytes 1493000 | tf_op jit(solution)/shard_map/ppermute | solution.py:258
  109.9 25.7 %copy-start.7 = (bf16[24,10368]{1,0:T(8,128)(2,1)}, bf16[24,10368]{1,0:T(8,128)(2,1)S(1)}, u32[]{:S(2)}) copy-start(bf16[24,10368]{1,0:T(8,128)(2,1)S(1)} %collective-permute-done.7.refs_5_) | copy-start | bytes 1492996
  109.9 25.7 %collective-permute-start.6 = (bf16[4,24,2592]{2,1,0:T(8,128)(2,1)S(1)}, bf16[4,24,2592]{2,1,0:T(8,128)(2,1)S(1)}, u32[]{:S(2)}, u32[]{:S(2)}) collective-permute-start(bf16[4,24,2592]{2,1,0:T(8,128)(2,1)S(1)} %copy-done.22), channel_id=1, source_target_pairs={{0,12},{1,13},{2,14},{3,15},{4,0},{5,1},{6,2},{7,3},{8,4},{9,5},{1... | collective-permute-start | bytes 1493000 | tf_op jit(solution)/shard_map/ppermute | solution.py:258
  130.6 42.6 %collective-permute-start.1 = (bf16[2,384,384]{2,1,0:T(8,128)(2,1)S(1)}, bf16[2,384,384]{2,1,0:T(8,128)(2,1)S(1)}, u32[]{:S(2)}, u32[]{:S(2)}) collective-permute-start(bf16[2,384,384]{2,1,0:T(8,128)(2,1)S(1)} %copy-done.3), channel_id=1, source_target_pairs={{16,0},{32,16},{48,32},{64,48},{80,64},{96,80},{112,96},{17,1},{33... | collective-permute-start | bytes 1769480 | tf_op jit(solution)/shard_map/ppermute | solution.py:40
  140.7 14.2 %copy-start.26 = (bf16[24,2592]{1,0:T(8,128)(2,1)S(1)}, bf16[24,2592]{1,0:T(8,128)(2,1)}, u32[]{:S(2)}) copy-start(bf16[24,2592]{1,0:T(8,128)(2,1)} %get-tuple-element.52) | copy-start | bytes 373252
  140.8 16.2 %copy-start.25 = (bf16[24,2592]{1,0:T(8,128)(2,1)S(1)}, bf16[24,2592]{1,0:T(8,128)(2,1)}, u32[]{:S(2)}) copy-start(bf16[24,2592]{1,0:T(8,128)(2,1)} %get-tuple-element.53) | copy-start | bytes 373252
  140.8 18.9 %copy-start.24 = (bf16[24,2592]{1,0:T(8,128)(2,1)S(1)}, bf16[24,2592]{1,0:T(8,128)(2,1)}, u32[]{:S(2)}) copy-start(bf16[24,2592]{1,0:T(8,128)(2,1)} %get-tuple-element.54) | copy-start | bytes 373252
  140.8 16.1 %collective-permute-start.10 = (bf16[24,2592]{1,0:T(8,128)(2,1)}, bf16[24,2592]{1,0:T(8,128)(2,1)S(1)}, u32[]{:S(2)}, u32[]{:S(2)}) collective-permute-start(bf16[24,2592]{1,0:T(8,128)(2,1)} %get-tuple-element.48), channel_id=1, source_target_pairs={{0,32},{1,33},{2,34},{3,35},{4,36},{5,37},{6,38},{7,39},{8,40},{9,... | collective-permute-start | bytes 373256 | tf_op jit(solution)/shard_map/ppermute | solution.py:258
  142.3 17.4 %collective-permute-start.11 = (bf16[24,2592]{1,0:T(8,128)(2,1)}, bf16[24,2592]{1,0:T(8,128)(2,1)S(1)}, u32[]{:S(2)}, u32[]{:S(2)}) collective-permute-start(bf16[24,2592]{1,0:T(8,128)(2,1)} %get-tuple-element.49), channel_id=1, source_target_pairs={{0,64},{1,65},{2,66},{3,67},{4,68},{5,69},{6,70},{7,71},{8,72},{9,... | collective-permute-start | bytes 373256 | tf_op jit(solution)/shard_map/ppermute | solution.py:258
  144.7 16.5 %all-to-all-start.1 = ((bf16[8,48,144]{2,1,0:T(8,128)(2,1)}), bf16[8,48,144]{2,1,0:T(8,128)(2,1)S(1)}, u32[]{:S(2)}, u32[]{:S(2)}) async-start(bf16[8,48,144]{2,1,0:T(8,128)(2,1)} %copy.8), calls=%async_computation.1 | async-start | bytes 393216 | tf_op jit(solution)/shard_map/all_to_all | solution.py:387
  152.4 9.1 %collective-permute-start.12 = (bf16[24,2592]{1,0:T(8,128)(2,1)S(1)}, bf16[24,2592]{1,0:T(8,128)(2,1)S(1)}, u32[]{:S(2)}, u32[]{:S(2)}) collective-permute-start(bf16[24,2592]{1,0:T(8,128)(2,1)S(1)} %copy-done.27), channel_id=1, source_target_pairs={{0,96},{1,97},{2,98},{3,99},{4,100},{5,101},{6,102},{7,103},{8,104... | collective-permute-start | bytes 373256 | tf_op jit(solution)/shard_map/ppermute | solution.py:258
  155.0 7.2 %collective-permute-start.13 = (bf16[24,2592]{1,0:T(8,128)(2,1)S(1)}, bf16[24,2592]{1,0:T(8,128)(2,1)S(1)}, u32[]{:S(2)}, u32[]{:S(2)}) collective-permute-start(bf16[24,2592]{1,0:T(8,128)(2,1)S(1)} %copy-done.26), channel_id=1, source_target_pairs={{0,4},{1,5},{2,6},{3,7},{4,8},{5,9},{6,10},{7,11},{8,12},{9,13},{1... | collective-permute-start | bytes 373256 | tf_op jit(solution)/shard_map/ppermute | solution.py:258
  156.9 7.0 %collective-permute-start.14 = (bf16[24,2592]{1,0:T(8,128)(2,1)S(1)}, bf16[24,2592]{1,0:T(8,128)(2,1)S(1)}, u32[]{:S(2)}, u32[]{:S(2)}) collective-permute-start(bf16[24,2592]{1,0:T(8,128)(2,1)S(1)} %copy-done.25), channel_id=1, source_target_pairs={{0,8},{1,9},{2,10},{3,11},{4,12},{5,13},{6,14},{7,15},{8,0},{9,1},... | collective-permute-start | bytes 373256 | tf_op jit(solution)/shard_map/ppermute | solution.py:258
  159.7 5.0 %collective-permute-start.15 = (bf16[24,2592]{1,0:T(8,128)(2,1)S(1)}, bf16[24,2592]{1,0:T(8,128)(2,1)S(1)}, u32[]{:S(2)}, u32[]{:S(2)}) collective-permute-start(bf16[24,2592]{1,0:T(8,128)(2,1)S(1)} %copy-done.24), channel_id=1, source_target_pairs={{0,12},{1,13},{2,14},{3,15},{4,0},{5,1},{6,2},{7,3},{8,4},{9,5},{1... | collective-permute-start | bytes 373256 | tf_op jit(solution)/shard_map/ppermute | solution.py:258
  161.5 32.7 %collective-permute-start.22 = (f32[48,72]{0,1:T(8,128)S(1)}, f32[48,72]{0,1:T(8,128)S(1)}, u32[]{:S(2)}, u32[]{:S(2)}) collective-permute-start(f32[48,72]{0,1:T(8,128)S(1)} %bitcast.28), channel_id=1, source_target_pairs={{0,1},{1,0},{2,3},{3,2},{4,5},{5,4},{6,7},{7,6},{8,9},{9,8},{10,11... | collective-permute-start | bytes 41480 | tf_op jit(solution)/shard_map/ppermute | solution.py:238
  167.6 24.1 %collective-permute-start.16 = (bf16[24,1296]{1,0:T(8,128)(2,1)}, bf16[24,1296]{1,0:T(8,128)(2,1)S(1)}, u32[]{:S(2)}, u32[]{:S(2)}) collective-permute-start(bf16[24,1296]{1,0:T(8,128)(2,1)} %get-tuple-element.56), channel_id=1, source_target_pairs={{0,16},{1,17},{2,18},{3,19},{4,20},{5,21},{6,22},{7,23},{8,24},{9,... | collective-permute-start | bytes 186632 | tf_op jit(solution)/shard_map/ppermute | solution.py:258
  167.6 24.1 %collective-permute-start.17 = (bf16[24,1296]{1,0:T(8,128)(2,1)}, bf16[24,1296]{1,0:T(8,128)(2,1)S(1)}, u32[]{:S(2)}, u32[]{:S(2)}) collective-permute-start(bf16[24,1296]{1,0:T(8,128)(2,1)} %get-tuple-element.57), channel_id=1, source_target_pairs={{0,2},{1,3},{2,0},{3,1},{4,6},{5,7},{6,4},{7,5},{8,10},{9,11},{10,... | collective-permute-start | bytes 186632 | tf_op jit(solution)/shard_map/ppermute | solution.py:258
  171.0 20.7 %collective-permute-start.18 = (bf16[24,1296]{1,0:T(8,128)(2,1)}, bf16[24,1296]{1,0:T(8,128)(2,1)S(1)}, u32[]{:S(2)}, u32[]{:S(2)}) collective-permute-start(bf16[24,1296]{1,0:T(8,128)(2,1)} %get-tuple-element.58), channel_id=1, source_target_pairs={{0,18},{1,19},{2,16},{3,17},{4,22},{5,23},{6,20},{7,21},{8,26},{9,... | collective-permute-start | bytes 186632 | tf_op jit(solution)/shard_map/ppermute | solution.py:258
  194.2 1.5 collective-permute-start.19
  (21 other events, 73.7 us)

commit v3 on v2

--- a/solution.py
+++ b/solution.py
@@ -40,26 +40,32 @@
     return lax.ppermute(value, axis, [(source, source + steps) for source in range(first, last)])
 
 
-def group_mean(value):
-    rows, channels = value.shape
+def group_means(values):
+    rows, channels = values[0].shape
     width = channels // G
-    sums = jnp.broadcast_to(jnp.sum(value, axis=0, keepdims=True), (8, channels))
-    left = lax.broadcasted_iota(jnp.int32, (channels, channels), 0) // width
-    right = lax.broadcasted_iota(jnp.int32, (channels, channels), 1) // width
+    slot = lax.broadcasted_iota(jnp.int32, (8, channels), 0)
+    sums = jnp.zeros((8, channels), F32)
+    for at, value in enumerate(values):
+        sums = jnp.where(slot == at, jnp.sum(value, axis=0, keepdims=True), sums)
+    left = lax.broadcasted_iota(jnp.int32, (channels, 1), 0) // width
+    right = lax.broadcasted_iota(jnp.int32, (1, channels), 1) // width
     mix = jnp.where(left == right, 1.0, 0.0).astype(F32)
     total = jnp.dot(sums, mix, precision=lax.Precision.HIGHEST, preferred_element_type=F32)
-    return total[0:1] * (1.0 / (rows * width))
-
-
-def normalize(value):
-    center = value - group_mean(value)
-    scale = lax.rsqrt(group_mean(center * center) + EPSILON)
-    return center * scale, scale
+    total = total * (1.0 / (rows * width))
+    return [total[at : at + 1] for at in range(len(values))]
+
+
+def normalize(values):
+    centers = [value - mean for value, mean in zip(values, group_means(values))]
+    spreads = group_means([center * center for center in centers])
+    scales = [lax.rsqrt(spread + EPSILON) for spread in spreads]
+    return [center * scale for center, scale in zip(centers, scales)], scales
 
 
 def act_body(field_ref, act_ref):
-    normed, _ = normalize(field_ref[0].astype(F32))
-    act_ref[0] = (normed / (1.0 + jnp.exp(-normed))).astype(BF16)
+    normed, _ = normalize([field_ref[frame].astype(F32) for frame in range(2)])
+    for frame in range(2):
+        act_ref[frame] = (normed[frame] / (1.0 + jnp.exp(-normed[frame]))).astype(BF16)
 
 
 def up_body(cot_ref, weight_ref, local_ref, prior_ref):
@@ -84,8 +90,7 @@
 
 def fill_shifts(frames, cols_ref, breadth):
     rows, channels = frames[0].shape
-    place = lax.broadcasted_iota(jnp.int32, (rows, channels), 0)
-    wide = place % breadth
+    wide = lax.broadcasted_iota(jnp.int32, (rows, 1), 0) % breadth
     for at, frame in enumerate(frames):
         value = frame.astype(F32)
         for wide_tap in range(3):
@@ -93,7 +98,7 @@
             if wide_tap != 1:
                 moved = pltpu.roll(value, (1 - wide_tap) % rows, 0)
                 edge = 0 if wide_tap == 0 else breadth - 1
-                moved = jnp.where(wide == edge, 0.0, moved)
+                moved = moved * jnp.where(wide == edge, 0.0, 1.0).astype(F32)
             for high_tap in range(3):
                 shifted = moved
                 if high_tap == 0:
@@ -164,14 +169,17 @@
         @pl.when(step == 2)
         def _():
             rows = acc_ref.shape[0] // 2
+            normed, scales = normalize([field_ref[frame].astype(F32) for frame in range(2)])
+            grads = []
             for frame in range(2):
-                normed, scale = normalize(field_ref[frame].astype(F32))
-                gate = 1.0 / (1.0 + jnp.exp(-normed))
-                slope = gate * (1.0 + normed * (1.0 - gate))
-                grad = acc_ref[frame * rows : (frame + 1) * rows] * slope
-                inner = grad - group_mean(grad) - normed * group_mean(grad * normed)
+                gate = 1.0 / (1.0 + jnp.exp(-normed[frame]))
+                slope = gate * (1.0 + normed[frame] * (1.0 - gate))
+                grads.append(acc_ref[frame * rows : (frame + 1) * rows] * slope)
+            means = group_means(grads + [grads[frame] * normed[frame] for frame in range(2)])
+            for frame in range(2):
+                inner = grads[frame] - means[frame] - normed[frame] * means[2 + frame]
                 hidden_grad = local_ref[frame] + next_ref[frame].astype(F32)
-                out_ref[frame] = (hidden_grad + scale * inner).astype(BF16)
+                out_ref[frame] = (hidden_grad + scales[frame] * inner).astype(BF16)
 
     return body
 
@@ -266,63 +274,97 @@
     return total
 
 
-def join_body(place_ref, got_ref, keep_ref, *refs):
-    row_refs, col_refs, hold_ref = refs[:4], refs[4:8], refs[8]
-    step = pl.program_id(0)
-    quarter = got_ref.shape[-1] // 4
-    total = (got_ref[0].astype(F32) + keep_ref[0].astype(F32)).astype(BF16)
-    for at in range(4):
-        hold_ref[at] = total[0][:, at * quarter : (at + 1) * quarter]
-    for slot in range(4):
-        row_refs[slot][0] = hold_ref[lax.rem(place_ref[0] + slot, 4)]
-
-        @pl.when(lax.rem(step - place_ref[1] + 4, 4) == slot)
-        def _():
-            col_refs[slot][...] = total[1]
-
-
-def mid_body(place_ref, *refs):
-    row_in, col_in, row_out, col_out = refs[:4], refs[4:8], refs[8:12], refs[12:16]
-    row_hold, col_hold = refs[16:]
-    quarter = col_in[0].shape[-1] // 4
-    row_hold[...] = added(row_in).astype(BF16)
-    total = added(col_in).astype(BF16)
-    for at in range(4):
-        col_hold[at] = total[:, at * quarter : (at + 1) * quarter]
-    for slot in range(4):
-        row_out[slot][...] = row_hold[lax.rem(place_ref[1] + slot, 4)]
-        col_out[slot][...] = col_hold[lax.rem(place_ref[0] + slot, 4)]
-
-
-def end_body(place_ref, *refs):
-    outs, hold_ref = refs[8:12], refs[12]
-    width = outs[0].shape[-1]
-    for low in range(2):
-        total = added(refs[4 * low : 4 * low + 4]).astype(BF16)
-        for high in range(2):
-            hold_ref[high * 2 + low] = total[:, high * width : (high + 1) * width]
-    for slot in range(4):
-        outs[slot][...] = hold_ref[lax.rem(place_ref[2] + slot, 4)]
-
-
-def last_body(place_ref, *refs):
-    total = added(refs[:4])
-    width = total.shape[1] // 2
-    low, high = total[:, :width], total[:, width:]
-    refs[4][...] = jnp.where(place_ref[3] == 0, low, high)
-    refs[5][...] = jnp.where(place_ref[3] == 0, high, low)
-
-
-def reduce_blocks(send, keep):
-    times, cols, rows = send.shape
+def pick(value, widths, index, count):
+    parts, start = [], 0
+    for width in widths:
+        part = width // count
+        parts.append(value[:, start + index * part : start + (index + 1) * part])
+        start += width
+    return jnp.concatenate(parts, axis=1)
+
+
+def make_join(conv_rows, up_rows):
+    widths = (conv_rows, up_rows, up_rows)
+
+    def body(place_ref, conv_got, conv_keep, up_got, up_keep, *refs):
+        row_refs, col_refs, hold_ref = refs[:4], refs[4:8], refs[8]
+        step = pl.program_id(0)
+        conv = conv_got[0] + conv_keep[0]
+        up = up_got[0] + up_keep[0]
+        cols = conv.shape[1]
+        full = [
+            jnp.concatenate([conv[low], up[low, :cols], up[low, cols:]], axis=1)
+            for low in range(2)
+        ]
+        for at in range(4):
+            hold_ref[at] = pick(full[0], widths, at, 4)
+        for slot in range(4):
+            row_refs[slot][0] = hold_ref[lax.rem(place_ref[0] + slot, 4)]
+
+            @pl.when(lax.rem(step - place_ref[1] + 4, 4) == slot)
+            def _():
+                col_refs[slot][...] = full[1]
+
+    return body
+
+
+def make_mid(conv_rows, up_rows):
+    widths = (conv_rows, up_rows, up_rows)
+
+    def body(place_ref, *refs):
+        row_in, col_in, row_out, col_out = refs[:4], refs[4:8], refs[8:12], refs[12:16]
+        row_hold, col_hold = refs[16:]
+        row_hold[...] = added(row_in)
+        total = added(col_in)
+        for at in range(4):
+            col_hold[at] = pick(total, widths, at, 4)
+        for slot in range(4):
+            kind = row_out[slot].dtype
+            row_out[slot][...] = row_hold[lax.rem(place_ref[1] + slot, 4)].astype(kind)
+            col_out[slot][...] = col_hold[lax.rem(place_ref[0] + slot, 4)].astype(kind)
+
+    return body
+
+
+def make_end(conv_rows, up_rows):
+    widths = (conv_rows // 4, up_rows // 4, up_rows // 4)
+
+    def body(place_ref, *refs):
+        outs, hold_ref = refs[8:12], refs[12]
+        for low in range(2):
+            total = added(refs[4 * low : 4 * low + 4])
+            for high in range(2):
+                hold_ref[high * 2 + low] = pick(total, widths, high, 2)
+        for slot in range(4):
+            outs[slot][...] = hold_ref[lax.rem(place_ref[2] + slot, 4)].astype(outs[slot].dtype)
+
+    return body
+
+
+def make_last(conv_rows, up_rows):
+    widths = (conv_rows // 8, up_rows // 8, up_rows // 8)
+
+    def body(place_ref, *refs):
+        total = added(refs[:4])
+        low, high = pick(total, widths, 0, 2), pick(total, widths, 1, 2)
+        refs[4][...] = jnp.where(place_ref[3] == 0, low, high)
+        refs[5][...] = jnp.where(place_ref[3] == 0, high, low)
+
+    return body
+
+
+def reduce_blocks(conv_send, conv_keep, up_send, up_keep):
+    times, cols, conv_rows = conv_send.shape
+    up_rows = up_send.shape[2]
+    rows = conv_rows + 2 * up_rows
     data, time = lax.axis_index("dp"), lax.axis_index("tm")
     place = jnp.stack([data // 4, time // 2, (data // 2 % 2) * 2 + time % 2, data % 2])
     place = place.astype(jnp.int32)
     scalars = pl.BlockSpec(memory_space=pltpu.SMEM)
 
-    def small(body, arrays, shapes, scratch):
+    def small(make, arrays, shapes, scratch):
         return call(
-            body,
+            make(conv_rows, up_rows),
             (1,),
             [scalars] + [whole(*array.shape) for array in arrays],
             [whole(*shape.shape) for shape in shapes],
@@ -335,64 +377,57 @@
     def shape(*dims):
         return jax.ShapeDtypeStruct(dims, BF16)
 
-    got = swap_sides(send)
-    blocks = (4, 2, cols, rows)
-    pair_spec = pl.BlockSpec((1, 2, cols, rows), lambda k: (k, 0, 0, 0))
+    def slots(*dims):
+        return [jax.ShapeDtypeStruct(dims, F32)] + [jax.ShapeDtypeStruct(dims, BF16)] * 3
+
+    conv_got = swap_sides(conv_send)
+    up_got = swap_sides(up_send)
+    conv_blocks = (4, 2, cols, conv_rows)
+    up_blocks = (4, 2, 2 * cols, up_rows)
+    conv_spec = pl.BlockSpec((1,) + conv_blocks[1:], lambda k: (k, 0, 0, 0))
+    up_spec = pl.BlockSpec((1,) + up_blocks[1:], lambda k: (k, 0, 0, 0))
     row_spec = pl.BlockSpec((1, cols, rows // 4), lambda k: (k, 0, 0))
     out = call(
-        join_body,
+        make_join(conv_rows, up_rows),
         (4,),
-        [scalars, pair_spec, pair_spec],
+        [scalars, conv_spec, conv_spec, up_spec, up_spec],
         [row_spec] * 4 + [whole(cols, rows)] * 4,
         [shape(4, cols, rows // 4)] * 4 + [shape(cols, rows)] * 4,
         [pltpu.VMEM((4, cols, rows // 4), BF16)],
         flops=1000,
         nbytes=6 * times * cols * rows,
-    )(place, got.reshape(blocks), keep.reshape(blocks))
+    )(
+        place,
+        conv_got.reshape(conv_blocks),
+        conv_keep.reshape(conv_blocks),
+        up_got.reshape(up_blocks),
+        up_keep.reshape(up_blocks),
+    )
     first = exchange(out[4:], 1)
     second = exchange(out[:4], 0)
-    hold = pltpu.VMEM((4, cols, rows // 4), BF16)
-    out = small(mid_body, second + first, [shape(cols, rows // 4)] * 8, [hold, hold])
+    hold = pltpu.VMEM((4, cols, rows // 4), F32)
+    out = small(make_mid, second + first, slots(cols, rows // 4) * 2, [hold, hold])
     first = exchange(out[:4], 1)
     second = exchange(out[4:], 0)
-    hold = pltpu.VMEM((4, cols, rows // 8), BF16)
-    out = small(end_body, first + second, [shape(cols, rows // 8)] * 4, [hold])
+    hold = pltpu.VMEM((4, cols, rows // 8), F32)
+    out = small(make_end, first + second, slots(cols, rows // 8), [hold])
     out = exchange(out, 2)
     half = jax.ShapeDtypeStruct((cols, rows // 16), F32)
-    mine, other = small(last_body, out, [half, half], [])
+    mine, other = small(make_last, out, [half, half], [])
     got = swap_sides(other)
-    side = data % 2
-    full = jnp.where(
-        side == 0, jnp.concatenate([mine, got], axis=0), jnp.concatenate([got, mine], axis=0)
-    )
-    return full.T
-
-
-def join_pair(send, keep):
-    swapped = swap_sides(send)
-    return (keep.astype(F32) + swapped.astype(F32)).astype(BF16)
-
-
-def over_times(pair):
-    spread = lax.all_to_all(pair, "tm", 0, 0, tiled=True)
-    return jnp.sum(spread.astype(F32), axis=0).astype(BF16)
-
-
-def over_data(rowsum):
-    cols, rows = rowsum.shape
-    chips = lax.axis_size("dp") // 2
-    side = lax.axis_index("dp") % 2
-    blocks = rowsum.reshape(cols, chips, rows // chips).transpose(1, 0, 2)
-    groups = [[2 * chip + own for chip in range(chips)] for own in range(2)]
-    spread = lax.all_to_all(blocks, "dp", 0, 0, axis_index_groups=groups, tiled=True)
-    total = jnp.sum(spread.astype(F32), axis=0).reshape(cols, 2, rows // chips // 2)
-    mine = lax.dynamic_index_in_dim(total, side, 1, keepdims=False)
-    other = lax.dynamic_index_in_dim(total, 1 - side, 1, keepdims=False)
-    got = swap_sides(other)
-    both = jnp.where(
-        side == 0, jnp.concatenate([mine, got], axis=0), jnp.concatenate([got, mine], axis=0)
-    )
-    return both.T
+    even = data % 2 == 0
+    low, high = jnp.where(even, mine, got), jnp.where(even, got, mine)
+    cut, part = conv_rows // 16, up_rows // 16
+    grad_conv = jnp.concatenate([low[:, :cut], high[:, :cut]], axis=0).T
+    grad_up = jnp.concatenate(
+        [
+            side[:, cut + at * part : cut + (at + 1) * part]
+            for side in (low, high)
+            for at in range(2)
+        ],
+        axis=0,
+    ).T
+    return grad_conv, grad_up
 
 
 def step(features, conv_weight, up_weight, cotangent):
@@ -408,9 +443,9 @@
     square = 2 * channels * channels
     act = call(
         act_body,
-        (frames,),
-        [pl.BlockSpec((1, rows, channels), lambda f: (f, 0, 0))],
-        pl.BlockSpec((1, rows, channels), lambda f: (f, 0, 0)),
+        (1,),
+        [whole(*block)],
+        whole(*block),
         jax.ShapeDtypeStruct(block, BF16),
         flops=20 * frames * rows * channels,
         nbytes=4 * frames * rows * channels,
@@ -467,7 +502,6 @@
         flops=27 * frames * rows * square,
         nbytes=4 * 27 * channels * channels,
     )(side, act_prior, act, conv_grad)
-    grad_conv = reduce_blocks(send, keep) * scale
     up_half = jax.ShapeDtypeStruct((times, channels // times, 3 * channels), BF16)
     up_send, up_keep = call(
         make_up_grad(times),
@@ -482,7 +516,8 @@
         flops=6 * frames * rows * square,
         nbytes=12 * channels * channels,
     )(side, hidden_prior, hidden, cot)
-    grad_up = over_data(over_times(join_pair(up_send, up_keep))) * scale
+    grad_conv, grad_up = reduce_blocks(send, keep, up_send, up_keep)
+    grad_conv, grad_up = grad_conv * scale, grad_up * scale
     features_grad = call(
         make_back(breadth),
         (3,),

time: 199 us -> 193 us (0.970)
  starting transfers between devices: 55.2 us -> 47.6 us
  waiting for transfers between devices: 47.9 us -> 52.9 us
  other arithmetic: 5.37 us -> 2.44 us
    all_to_all x2 -> x0, starting transfers between devices: 11.9 us -> none  [the longest x1 7.61 us: over_data(): lax.all_to_all(blocks, 'dp', 0, 0, axis_index_groups=groups, tiled=True)]
    ppermute x15, starting transfers between devices: 32.2 us -> 36.6 us  [exchange(): got.append(lax.ppermute(pieces[step], ('tm', 'dp'), pairs))]
    ppermute x15, waiting for transfers between devices: 25.3 us -> 29.1 us  [exchange(): got.append(lax.ppermute(pieces[step], ('tm', 'dp'), pairs))]
    unnamed x56 -> x47, local copies, waits for them, and re-layouts: 4.36 us -> 5.59 us
  transfers between devices with their start and end apart: 25 -> 22, of which waited for: 8 -> 11; matrix products, arithmetic and copies ran while one was open for 2% -> 0% of each run, Pallas kernels for 33% -> 31%
where the time goes in v3:
time: 193 us; the launch traced here: 190 us
  Pallas kernels  81 us (42%)
  waiting for transfers between devices  52.9 us (27%)
  starting transfers between devices  47.6 us (25%)
  local copies, waits for them, and re-layouts  5.68 us (3%)
  other arithmetic  2.44 us (1%)
    ppermute x15, starting transfers between devices, exchange(): got.append(lax.ppermute(pieces[step], ('tm', 'dp'), pairs))  36.6 us
    ppermute x15, waiting for transfers between devices, exchange(): got.append(lax.ppermute(pieces[step], ('tm', 'dp'), pairs))  29.1 us
    ppermute x4, waiting for transfers between devices, from_behind(): lax.ppermute(value, axis, [(source, source + steps) for source in range(f...  21.8 us
    pallas_call x1, Pallas kernels, step(): call(make_back(breadth), (3,), [whole(*block), whole(*block), kernel_spec...  16.1 us
    pallas_call x1, Pallas kernels, step(): call(make_conv(breadth), (3,), [whole(*block), whole(*block), kernel_spec...  13.4 us
    pallas_call x1, Pallas kernels, step(): call(make_weight_grad(breadth, times), (3,), [pl.BlockSpec(memory_space=p...  12.2 us
    pallas_call x1, Pallas kernels, step(): call(turn_body, (9,), [pl.BlockSpec((3, channels, channels), lambda n: (8...  11.1 us
    ppermute x4, starting transfers between devices, from_behind(): lax.ppermute(value, axis, [(source, source + steps) for source in range(f...  11 us
  transfers between devices with their start and end apart: 22, of which 11 were waited for; matrix products, arithmetic and copies ran while one was open for 0% of the time, Pallas kernels for 31%

profile of v3, /device:TPU:0, one launch (start us, length us, event | category | flops | bytes accessed | tf_op | source)
XLA Modules:
  0.0 190.5 jit_solution(17036732614062900754)
XLA Ops:
  0.6 3.3 %shard_map.68.late_ref = bf16[2,384,384]{2,1,0:T(8,128)(2,1)} custom-call(bf16[2,384,384]{2,1,0:T(8,128)(2,1)} %bitcast.24), custom_call_target="tpu_custom_call" | custom-call | flops 5898240 | bytes 1179648 | tf_op jit(solution)/shard_map/pallas_call | solution.py:444
  3.9 4.0 %collective-permute-start.2 = (bf16[2,384,384]{2,1,0:T(8,128)(2,1)}, bf16[2,384,384]{2,1,0:T(8,128)(2,1)S(1)}, u32[]{:S(2)}, u32[]{:S(2)}) collective-permute-start(bf16[2,384,384]{2,1,0:T(8,128)(2,1)} %shard_map.68.late_ref), channel_id=1, source_target_pairs={{0,16},{16,32},{32,48},{48,64},{64,80},{80,96},{96,112},{1,17},{17... | collective-permute-start | bytes 1769480 | tf_op jit(solution)/shard_map/ppermute | solution.py:40
  7.8 4.6 %shard_map.67 = (f32[2,384,384]{2,1,0:T(8,128)}, bf16[2,384,384]{2,1,0:T(8,128)(2,1)}) custom-call(bf16[4,384,384]{2,1,0:T(8,128)(2,1)} %bitcast.27, bf16[1152,768]{1,0:T(8,128)(2,1)} %weight_ref.1), custom_call_target="tpu_custom_call" | custom-call | flops 1358954496 | bytes 2949120 | tf_op jit(solution)/shard_map/pallas_call | solution.py:454
  13.8 11.1 %shard_map.69 = bf16[27,384,384]{2,1,0:T(8,128)(2,1)} custom-call(bf16[27,384,384]{2,1,0:T(8,128)(2,1)} %bitcast.18), custom_call_target="tpu_custom_call" | custom-call | flops 7962624 | bytes 15925248 | tf_op jit(solution)/shard_map/pallas_call | solution.py:465
  24.9 8.5 %collective-permute-done.2.early_ref = bf16[2,384,384]{2,1,0:T(8,128)(2,1)S(1)} collective-permute-done((bf16[2,384,384]{2,1,0:T(8,128)(2,1)}, bf16[2,384,384]{2,1,0:T(8,128)(2,1)S(1)}, u32[]{:S(2)}, u32[]{:S(2)}) %collective-permute-start.2) | collective-permute-done | bytes 589856 | tf_op jit(solution)/shard_map/ppermute | solution.py:40
  34.5 12.2 %shard_map.71 = (bf16[8,24,10368]{2,1,0:T(8,128)(2,1)}, bf16[8,24,10368]{2,1,0:T(8,128)(2,1)}) custom-call(s32[1]{0:T(128)} %bitcast.8.side_ref, bf16[2,384,384]{2,1,0:T(8,128)(2,1)} %copy-done.21, bf16[2,384,384]{2,1,0:T(8,128)(2,1)} %shard_map.68.late_ref, bf16[2,384,384]{2,1,0:T(8,128)(2,1)} %add_convert_fusion.early_ref.grad_ref), custom_call_target="tpu_custom_call" | custom-call | flops 6115295232 | bytes 15925248 | tf_op jit(solution)/shard_map/pallas_call | solution.py:495
  46.7 13.4 %shard_map.72.late_ref = bf16[2,384,384]{2,1,0:T(8,128)(2,1)} custom-call(bf16[2,384,384]{2,1,0:T(8,128)(2,1)} %copy-done.21, bf16[2,384,384]{2,1,0:T(8,128)(2,1)} %shard_map.68.late_ref, bf16[3,3456,384]{2,1,0:T(8,128)(2,1)} %bitcast.19, bf16[2,384,384]{2,1,0:T(8,128)(2,1)} %bitcast.25), custom_call_target="tpu_custom_call" | custom-call | flops 6115295232 | bytes 7962624 | tf_op jit(solution)/shard_map/pallas_call | solution.py:481
  60.1 4.5 %collective-permute-start.4 = (bf16[2,384,384]{2,1,0:T(8,128)(2,1)}, bf16[2,384,384]{2,1,0:T(8,128)(2,1)S(1)}, u32[]{:S(2)}, u32[]{:S(2)}) collective-permute-start(bf16[2,384,384]{2,1,0:T(8,128)(2,1)} %shard_map.72.late_ref), channel_id=1, source_target_pairs={{0,16},{16,32},{32,48},{48,64},{64,80},{80,96},{96,112},{1,17},{17... | collective-permute-start | bytes 1769480 | tf_op jit(solution)/shard_map/ppermute | solution.py:40
  64.6 13.3 %collective-permute-done.4.early_ref = bf16[2,384,384]{2,1,0:T(8,128)(2,1)S(1)} collective-permute-done((bf16[2,384,384]{2,1,0:T(8,128)(2,1)}, bf16[2,384,384]{2,1,0:T(8,128)(2,1)S(1)}, u32[]{:S(2)}, u32[]{:S(2)}) %collective-permute-start.4) | collective-permute-done | bytes 589856 | tf_op jit(solution)/shard_map/ppermute | solution.py:40
  78.7 4.8 %shard_map.73 = (bf16[8,48,1152]{2,1,0:T(8,128)(2,1)}, bf16[8,48,1152]{2,1,0:T(8,128)(2,1)}) custom-call(s32[1]{0:T(128)} %bitcast.8.side_ref, bf16[2,384,384]{2,1,0:T(8,128)(2,1)} %copy-done.22, bf16[2,384,384]{2,1,0:T(8,128)(2,1)} %shard_map.72.late_ref, bf16[4,384,384]{2,1,0:T(8,128)(2,1)} %bitcast.28), custom_call_target="tpu_custom_call" | custom-call | flops 1358954496 | bytes 1769472 | tf_op jit(solution)/shard_map/pallas_call | solution.py:506
  84.1 2.0 %collective-permute-done.5 = bf16[8,48,1152]{2,1,0:T(8,128)(2,1)S(1)} collective-permute-done((bf16[8,48,1152]{2,1,0:T(8,128)(2,1)}, bf16[8,48,1152]{2,1,0:T(8,128)(2,1)S(1)}, u32[]{:S(2)}, u32[]{:S(2)}) %collective-permute-start.5) | collective-permute-done | bytes 884768 | tf_op jit(solution)/shard_map/ppermute | solution.py:246
  87.0 7.0 %shard_map.74 = (bf16[4,24,3168]{2,1,0:T(8,128)(2,1)}, bf16[4,24,3168]{2,1,0:T(8,128)(2,1)}, bf16[4,24,3168]{2,1,0:T(8,128)(2,1)}, bf16[4,24,3168]{2,1,0:T(8,128...) custom-call(s32[4]{0:T(128)} %pad_add_fusion.place_ref, ...), custom_call_target="tpu_custom_call" | custom-call | flops 1000 | bytes 14598144 | tf_op jit(solution)/shard_map/pallas_call | solution.py:390
  94.0 3.9 %collective-permute-start.9 = (bf16[24,12672]{1,0:T(8,128)(2,1)}, bf16[24,12672]{1,0:T(8,128)(2,1)S(1)}, u32[]{:S(2)}, u32[]{:S(2)}) collective-permute-start(bf16[24,12672]{1,0:T(8,128)(2,1)} %get-tuple-element.46), channel_id=1, source_target_pairs={{0,32},{1,33},{2,34},{3,35},{4,36},{5,37},{6,38},{7,39},{8,40},{9,... | collective-permute-start | bytes 1824776 | tf_op jit(solution)/shard_map/ppermute | solution.py:266
  97.9 2.9 %collective-permute-start.10 = (bf16[24,12672]{1,0:T(8,128)(2,1)}, bf16[24,12672]{1,0:T(8,128)(2,1)S(1)}, u32[]{:S(2)}, u32[]{:S(2)}) collective-permute-start(bf16[24,12672]{1,0:T(8,128)(2,1)} %get-tuple-element.47), channel_id=1, source_target_pairs={{0,64},{1,65},{2,66},{3,67},{4,68},{5,69},{6,70},{7,71},{8,72},{9,... | collective-permute-start | bytes 1824776 | tf_op jit(solution)/shard_map/ppermute | solution.py:266
  100.7 1.4 collective-permute-start.11
  102.1 1.5 collective-permute-start.6
  103.6 2.7 %collective-permute-start.7 = (bf16[4,24,3168]{2,1,0:T(8,128)(2,1)}, bf16[4,24,3168]{2,1,0:T(8,128)(2,1)S(1)}, u32[]{:S(2)}, u32[]{:S(2)}) collective-permute-start(bf16[4,24,3168]{2,1,0:T(8,128)(2,1)} %get-tuple-element.43), channel_id=1, source_target_pairs={{0,8},{1,9},{2,10},{3,11},{4,12},{5,13},{6,14},{7,15},{8,0},{9,1},... | collective-permute-start | bytes 1824776 | tf_op jit(solution)/shard_map/ppermute | solution.py:266
  106.3 7.2 %collective-permute-done.9.refs_5_ = bf16[24,12672]{1,0:T(8,128)(2,1)S(1)} collective-permute-done((bf16[24,12672]{1,0:T(8,128)(2,1)}, bf16[24,12672]{1,0:T(8,128)(2,1)S(1)}, u32[]{:S(2)}, u32[]{:S(2)}) %collective-permute-start.9) | collective-permute-done | bytes 608288 | tf_op jit(solution)/shard_map/ppermute | solution.py:266
  113.5 2.8 %collective-permute-start.8 = (bf16[4,24,3168]{2,1,0:T(8,128)(2,1)}, bf16[4,24,3168]{2,1,0:T(8,128)(2,1)S(1)}, u32[]{:S(2)}, u32[]{:S(2)}) collective-permute-start(bf16[4,24,3168]{2,1,0:T(8,128)(2,1)} %get-tuple-element.44), channel_id=1, source_target_pairs={{0,12},{1,13},{2,14},{3,15},{4,0},{5,1},{6,2},{7,3},{8,4},{9,5},{1... | collective-permute-start | bytes 1824776 | tf_op jit(solution)/shard_map/ppermute | solution.py:266
  116.3 11.4 %collective-permute-done.10.refs_6_ = bf16[24,12672]{1,0:T(8,128)(2,1)S(1)} collective-permute-done((bf16[24,12672]{1,0:T(8,128)(2,1)}, bf16[24,12672]{1,0:T(8,128)(2,1)S(1)}, u32[]{:S(2)}, u32[]{:S(2)}) %collective-permute-start.10) | collective-permute-done | bytes 608288 | tf_op jit(solution)/shard_map/ppermute | solution.py:266
  129.1 3.7 %collective-permute-done.7.refs_2_ = bf16[4,24,3168]{2,1,0:T(8,128)(2,1)S(1)} collective-permute-done((bf16[4,24,3168]{2,1,0:T(8,128)(2,1)}, bf16[4,24,3168]{2,1,0:T(8,128)(2,1)S(1)}, u32[]{:S(2)}, u32[]{:S(2)}) %collective-permute-start.7) | collective-permute-done | bytes 608288 | tf_op jit(solution)/shard_map/ppermute | solution.py:266
  133.8 4.4 %shard_map.75 = (f32[24,3168]{1,0:T(8,128)}, bf16[24,3168]{1,0:T(8,128)(2,1)}, bf16[24,3168]{1,0:T(8,128)(2,1)}, bf16[24,3168]{1,0:T(8,128)(2,1)}, f32[24,3168]{...) custom-call(s32[4]{0:T(128)} %pad_add_fusion.place_ref, ...), custom_call_target="tpu_custom_call" | custom-call | flops 1000 | bytes 4866048 | tf_op jit(solution)/shard_map/pallas_call | solution.py:366
  138.9 5.7 %collective-permute-start.13 = (bf16[24,3168]{1,0:T(8,128)(2,1)}, bf16[24,3168]{1,0:T(8,128)(2,1)S(1)}, u32[]{:S(2)}, u32[]{:S(2)}) collective-permute-start(bf16[24,3168]{1,0:T(8,128)(2,1)} %get-tuple-element.51), channel_id=1, source_target_pairs={{0,64},{1,65},{2,66},{3,67},{4,68},{5,69},{6,70},{7,71},{8,72},{9,... | collective-permute-start | bytes 456200 | tf_op jit(solution)/shard_map/ppermute | solution.py:266
  144.6 2.5 %collective-permute-start.14 = (bf16[24,3168]{1,0:T(8,128)(2,1)}, bf16[24,3168]{1,0:T(8,128)(2,1)S(1)}, u32[]{:S(2)}, u32[]{:S(2)}) collective-permute-start(bf16[24,3168]{1,0:T(8,128)(2,1)} %get-tuple-element.52), channel_id=1, source_target_pairs={{0,96},{1,97},{2,98},{3,99},{4,100},{5,101},{6,102},{7,103},{8,104... | collective-permute-start | bytes 456200 | tf_op jit(solution)/shard_map/ppermute | solution.py:266
  148.2 3.9 %collective-permute-start.16 = (bf16[24,3168]{1,0:T(8,128)(2,1)}, bf16[24,3168]{1,0:T(8,128)(2,1)S(1)}, u32[]{:S(2)}, u32[]{:S(2)}) collective-permute-start(bf16[24,3168]{1,0:T(8,128)(2,1)} %get-tuple-element.55), channel_id=1, source_target_pairs={{0,8},{1,9},{2,10},{3,11},{4,12},{5,13},{6,14},{7,15},{8,0},{9,1},... | collective-permute-start | bytes 456200 | tf_op jit(solution)/shard_map/ppermute | solution.py:266
  154.1 3.1 %collective-permute-done.16.refs_6_ = bf16[24,3168]{1,0:T(8,128)(2,1)S(1)} collective-permute-done((bf16[24,3168]{1,0:T(8,128)(2,1)}, bf16[24,3168]{1,0:T(8,128)(2,1)S(1)}, u32[]{:S(2)}, u32[]{:S(2)}) %collective-permute-start.16) | collective-permute-done | bytes 152096 | tf_op jit(solution)/shard_map/ppermute | solution.py:266
  158.3 2.4 %shard_map.76 = (f32[24,1584]{1,0:T(8,128)}, bf16[24,1584]{1,0:T(8,128)(2,1)}, bf16[24,1584]{1,0:T(8,128)(2,1)}, bf16[24,1584]{1,0:T(8,128)(2,1)}) custom-call(s32[4]{0:T(128)} %pad_add_fusion.place_ref, f32[24,3168]{1,0:T(8,128)} %get-tuple-element.49.refs_0_, bf16[24,3168]{1,0:T(8,128)(2,1)} %copy-done.10, bf16[24,3168]{1,0:T(8,128)(2,1)} %copy-done.11, ...), custom_call_target="tpu_custom_call" | custom-call | flops 1000 | bytes 4866048 | tf_op jit(solution)/shard_map/pallas_call | solution.py:366
  160.8 3.8 %collective-permute-start.19 = (bf16[24,1584]{1,0:T(8,128)(2,1)}, bf16[24,1584]{1,0:T(8,128)(2,1)S(1)}, u32[]{:S(2)}, u32[]{:S(2)}) collective-permute-start(bf16[24,1584]{1,0:T(8,128)(2,1)} %get-tuple-element.59), channel_id=1, source_target_pairs={{0,2},{1,3},{2,0},{3,1},{4,6},{5,7},{6,4},{7,5},{8,10},{9,11},{10,... | collective-permute-start | bytes 228104 | tf_op jit(solution)/shard_map/ppermute | solution.py:266
  164.6 2.6 %collective-permute-start.20 = (bf16[24,1584]{1,0:T(8,128)(2,1)}, bf16[24,1584]{1,0:T(8,128)(2,1)S(1)}, u32[]{:S(2)}, u32[]{:S(2)}) collective-permute-start(bf16[24,1584]{1,0:T(8,128)(2,1)} %get-tuple-element.60), channel_id=1, source_target_pairs={{0,18},{1,19},{2,16},{3,17},{4,22},{5,23},{6,20},{7,21},{8,26},{9,... | collective-permute-start | bytes 228104 | tf_op jit(solution)/shard_map/ppermute | solution.py:266
  168.0 1.5 collective-permute-done.20.refs_3_
  170.2 1.8 shard_map.77
  172.8 16.1 %shard_map.70 = bf16[2,384,384]{2,1,0:T(8,128)(2,1)} custom-call(bf16[2,384,384]{2,1,0:T(8,128)(2,1)} %add_convert_fusion.early_ref.grad_ref, bf16[2,384,384]{2,1,0:T(8,128)(2,1)} %copy-done.20, bf16[3,3456,384]{2,1,0:T(8,128)(2,1)} %bitcast.20, bf16[2,384,384]{2,1,0:T(8,128)(2,1)} %bitcast.26, f32[2,384,384]{2,1,0:T(8,128)} %get-tuple-element.33.local_ref, ...), custom_call_target="tpu_custom_call" | custom-call | flops 6115295232 | bytes 7962624 | tf_op jit(solution)/shard_map/pallas_call | solution.py:521
  (78 shorter events, 15.9 us)
Async XLA Ops:
  3.9 29.5 %collective-permute-start.2 = (bf16[2,384,384]{2,1,0:T(8,128)(2,1)}, bf16[2,384,384]{2,1,0:T(8,128)(2,1)S(1)}, u32[]{:S(2)}, u32[]{:S(2)}) collective-permute-start(bf16[2,384,384]{2,1,0:T(8,128)(2,1)} %shard_map.68.late_ref), channel_id=1, source_target_pairs={{0,16},{16,32},{32,48},{48,64},{64,80},{80,96},{96,112},{1,17},{17... | collective-permute-start | bytes 1769480 | tf_op jit(solution)/shard_map/ppermute | solution.py:40
  12.4 20.9 %collective-permute-start = (bf16[2,384,384]{2,1,0:T(8,128)(2,1)}, bf16[2,384,384]{2,1,0:T(8,128)(2,1)S(1)}, u32[]{:S(2)}, u32[]{:S(2)}) collective-permute-start(bf16[2,384,384]{2,1,0:T(8,128)(2,1)} %get-tuple-element.34), channel_id=1, source_target_pairs={{16,0},{32,16},{48,32},{64,48},{80,64},{96,80},{112,96},{17,1},{33... | collective-permute-start | bytes 1769480 | tf_op jit(solution)/shard_map/ppermute | solution.py:40
  13.7 19.6 %copy-start = (f32[2,384,384]{2,1,0:T(8,128)S(1)}, f32[2,384,384]{2,1,0:T(8,128)}, u32[]{:S(2)}) copy-start(f32[2,384,384]{2,1,0:T(8,128)} %get-tuple-element.33.local_ref) | copy-start | bytes 3538948
  33.3 13.3 %copy-start.8 = (bf16[2,384,384]{2,1,0:T(8,128)(2,1)}, bf16[2,384,384]{2,1,0:T(8,128)(2,1)S(1)}, u32[]{:S(2)}) copy-start(bf16[2,384,384]{2,1,0:T(8,128)(2,1)S(1)} %collective-permute-done.next_ref) | copy-start | bytes 1769476
  46.7 39.4 %collective-permute-start.3 = (bf16[8,24,10368]{2,1,0:T(8,128)(2,1)}, bf16[8,24,10368]{2,1,0:T(8,128)(2,1)}, u32[]{:S(2)}, u32[]{:S(2)}) collective-permute-start(bf16[8,24,10368]{2,1,0:T(8,128)(2,1)} %get-tuple-element.37), channel_id=1, source_target_pairs={{0,1},{1,0},{2,3},{3,2},{4,5},{5,4},{6,7},{7,6},{8,9},{9,8},{10,11... | collective-permute-start | bytes 11943944 | tf_op jit(solution)/shard_map/ppermute | solution.py:246
  60.1 17.8 %collective-permute-start.4 = (bf16[2,384,384]{2,1,0:T(8,128)(2,1)}, bf16[2,384,384]{2,1,0:T(8,128)(2,1)S(1)}, u32[]{:S(2)}, u32[]{:S(2)}) collective-permute-start(bf16[2,384,384]{2,1,0:T(8,128)(2,1)} %shard_map.72.late_ref), channel_id=1, source_target_pairs={{0,16},{16,32},{32,48},{48,64},{64,80},{80,96},{96,112},{1,17},{17... | collective-permute-start | bytes 1769480 | tf_op jit(solution)/shard_map/ppermute | solution.py:40
  83.5 2.6 %collective-permute-start.5 = (bf16[8,48,1152]{2,1,0:T(8,128)(2,1)}, bf16[8,48,1152]{2,1,0:T(8,128)(2,1)S(1)}, u32[]{:S(2)}, u32[]{:S(2)}) collective-permute-start(bf16[8,48,1152]{2,1,0:T(8,128)(2,1)} %get-tuple-element.39), channel_id=1, source_target_pairs={{0,1},{1,0},{2,3},{3,2},{4,5},{5,4},{6,7},{7,6},{8,9},{9,8},{10,11... | collective-permute-start | bytes 2654216 | tf_op jit(solution)/shard_map/ppermute | solution.py:246
  87.0 40.7 %copy-start.9 = (bf16[2,384,384]{2,1,0:T(8,128)(2,1)S(1)}, bf16[2,384,384]{2,1,0:T(8,128)(2,1)}, u32[]{:S(2)}) copy-start(bf16[2,384,384]{2,1,0:T(8,128)(2,1)} %add_convert_fusion.early_ref.grad_ref) | copy-start | bytes 1769476
  94.0 19.5 %collective-permute-start.9 = (bf16[24,12672]{1,0:T(8,128)(2,1)}, bf16[24,12672]{1,0:T(8,128)(2,1)S(1)}, u32[]{:S(2)}, u32[]{:S(2)}) collective-permute-start(bf16[24,12672]{1,0:T(8,128)(2,1)} %get-tuple-element.46), channel_id=1, source_target_pairs={{0,32},{1,33},{2,34},{3,35},{4,36},{5,37},{6,38},{7,39},{8,40},{9,... | collective-permute-start | bytes 1824776 | tf_op jit(solution)/shard_map/ppermute | solution.py:266
  97.9 29.9 %collective-permute-start.10 = (bf16[24,12672]{1,0:T(8,128)(2,1)}, bf16[24,12672]{1,0:T(8,128)(2,1)S(1)}, u32[]{:S(2)}, u32[]{:S(2)}) collective-permute-start(bf16[24,12672]{1,0:T(8,128)(2,1)} %get-tuple-element.47), channel_id=1, source_target_pairs={{0,64},{1,65},{2,66},{3,67},{4,68},{5,69},{6,70},{7,71},{8,72},{9,... | collective-permute-start | bytes 1824776 | tf_op jit(solution)/shard_map/ppermute | solution.py:266
  100.7 28.3 %collective-permute-start.11 = (bf16[24,12672]{1,0:T(8,128)(2,1)}, bf16[24,12672]{1,0:T(8,128)(2,1)S(1)}, u32[]{:S(2)}, u32[]{:S(2)}) collective-permute-start(bf16[24,12672]{1,0:T(8,128)(2,1)} %get-tuple-element.48), channel_id=1, source_target_pairs={{0,96},{1,97},{2,98},{3,99},{4,100},{5,101},{6,102},{7,103},{8,104... | collective-permute-start | bytes 1824776 | tf_op jit(solution)/shard_map/ppermute | solution.py:266
  102.1 26.9 %collective-permute-start.6 = (bf16[4,24,3168]{2,1,0:T(8,128)(2,1)}, bf16[4,24,3168]{2,1,0:T(8,128)(2,1)S(1)}, u32[]{:S(2)}, u32[]{:S(2)}) collective-permute-start(bf16[4,24,3168]{2,1,0:T(8,128)(2,1)} %get-tuple-element.42), channel_id=1, source_target_pairs={{0,4},{1,5},{2,6},{3,7},{4,8},{5,9},{6,10},{7,11},{8,12},{9,13},{1... | collective-permute-start | bytes 1824776 | tf_op jit(solution)/shard_map/ppermute | solution.py:266
  103.6 29.1 %collective-permute-start.7 = (bf16[4,24,3168]{2,1,0:T(8,128)(2,1)}, bf16[4,24,3168]{2,1,0:T(8,128)(2,1)S(1)}, u32[]{:S(2)}, u32[]{:S(2)}) collective-permute-start(bf16[4,24,3168]{2,1,0:T(8,128)(2,1)} %get-tuple-element.43), channel_id=1, source_target_pairs={{0,8},{1,9},{2,10},{3,11},{4,12},{5,13},{6,14},{7,15},{8,0},{9,1},... | collective-permute-start | bytes 1824776 | tf_op jit(solution)/shard_map/ppermute | solution.py:266
  113.5 19.2 %copy-start.5 = (bf16[24,12672]{1,0:T(8,128)(2,1)}, bf16[24,12672]{1,0:T(8,128)(2,1)S(1)}, u32[]{:S(2)}) copy-start(bf16[24,12672]{1,0:T(8,128)(2,1)S(1)} %collective-permute-done.9.refs_5_) | copy-start | bytes 1824772
  113.5 19.2 %collective-permute-start.8 = (bf16[4,24,3168]{2,1,0:T(8,128)(2,1)}, bf16[4,24,3168]{2,1,0:T(8,128)(2,1)S(1)}, u32[]{:S(2)}, u32[]{:S(2)}) collective-permute-start(bf16[4,24,3168]{2,1,0:T(8,128)(2,1)} %get-tuple-element.44), channel_id=1, source_target_pairs={{0,12},{1,13},{2,14},{3,15},{4,0},{5,1},{6,2},{7,3},{8,4},{9,5},{1... | collective-permute-start | bytes 1824776 | tf_op jit(solution)/shard_map/ppermute | solution.py:266
  127.7 5.0 %copy-start.6 = (bf16[24,12672]{1,0:T(8,128)(2,1)}, bf16[24,12672]{1,0:T(8,128)(2,1)S(1)}, u32[]{:S(2)}) copy-start(bf16[24,12672]{1,0:T(8,128)(2,1)S(1)} %collective-permute-done.10.refs_6_) | copy-start | bytes 1824772
  127.7 44.3 %collective-permute-start.1 = (bf16[2,384,384]{2,1,0:T(8,128)(2,1)S(1)}, bf16[2,384,384]{2,1,0:T(8,128)(2,1)S(1)}, u32[]{:S(2)}, u32[]{:S(2)}) collective-permute-start(bf16[2,384,384]{2,1,0:T(8,128)(2,1)S(1)} %copy-done.9), channel_id=1, source_target_pairs={{16,0},{32,16},{48,32},{64,48},{80,64},{96,80},{112,96},{17,1},{33... | collective-permute-start | bytes 1769480 | tf_op jit(solution)/shard_map/ppermute | solution.py:40
  129.0 3.7 %copy-start.7 = (bf16[24,12672]{1,0:T(8,128)(2,1)}, bf16[24,12672]{1,0:T(8,128)(2,1)S(1)}, u32[]{:S(2)}) copy-start(bf16[24,12672]{1,0:T(8,128)(2,1)S(1)} %collective-permute-done.11.refs_7_) | copy-start | bytes 1824772
  138.1 10.1 %collective-permute-start.12 = (bf16[24,3168]{1,0:T(8,128)(2,1)}, bf16[24,3168]{1,0:T(8,128)(2,1)S(1)}, u32[]{:S(2)}, u32[]{:S(2)}) collective-permute-start(bf16[24,3168]{1,0:T(8,128)(2,1)} %get-tuple-element.50), channel_id=1, source_target_pairs={{0,32},{1,33},{2,34},{3,35},{4,36},{5,37},{6,38},{7,39},{8,40},{9,... | collective-permute-start | bytes 456200 | tf_op jit(solution)/shard_map/ppermute | solution.py:266
  138.9 13.3 %collective-permute-start.13 = (bf16[24,3168]{1,0:T(8,128)(2,1)}, bf16[24,3168]{1,0:T(8,128)(2,1)S(1)}, u32[]{:S(2)}, u32[]{:S(2)}) collective-permute-start(bf16[24,3168]{1,0:T(8,128)(2,1)} %get-tuple-element.51), channel_id=1, source_target_pairs={{0,64},{1,65},{2,66},{3,67},{4,68},{5,69},{6,70},{7,71},{8,72},{9,... | collective-permute-start | bytes 456200 | tf_op jit(solution)/shard_map/ppermute | solution.py:266
  144.6 8.5 %collective-permute-start.14 = (bf16[24,3168]{1,0:T(8,128)(2,1)}, bf16[24,3168]{1,0:T(8,128)(2,1)S(1)}, u32[]{:S(2)}, u32[]{:S(2)}) collective-permute-start(bf16[24,3168]{1,0:T(8,128)(2,1)} %get-tuple-element.52), channel_id=1, source_target_pairs={{0,96},{1,97},{2,98},{3,99},{4,100},{5,101},{6,102},{7,103},{8,104... | collective-permute-start | bytes 456200 | tf_op jit(solution)/shard_map/ppermute | solution.py:266
  147.1 7.0 %collective-permute-start.15 = (bf16[24,3168]{1,0:T(8,128)(2,1)}, bf16[24,3168]{1,0:T(8,128)(2,1)S(1)}, u32[]{:S(2)}, u32[]{:S(2)}) collective-permute-start(bf16[24,3168]{1,0:T(8,128)(2,1)} %get-tuple-element.54), channel_id=1, source_target_pairs={{0,4},{1,5},{2,6},{3,7},{4,8},{5,9},{6,10},{7,11},{8,12},{9,13},{1... | collective-permute-start | bytes 456200 | tf_op jit(solution)/shard_map/ppermute | solution.py:266
  148.2 9.4 %copy-start.10 = (bf16[24,3168]{1,0:T(8,128)(2,1)}, bf16[24,3168]{1,0:T(8,128)(2,1)S(1)}, u32[]{:S(2)}) copy-start(bf16[24,3168]{1,0:T(8,128)(2,1)S(1)} %collective-permute-done.12.refs_1_) | copy-start | bytes 456196
  148.2 9.0 %collective-permute-start.16 = (bf16[24,3168]{1,0:T(8,128)(2,1)}, bf16[24,3168]{1,0:T(8,128)(2,1)S(1)}, u32[]{:S(2)}, u32[]{:S(2)}) collective-permute-start(bf16[24,3168]{1,0:T(8,128)(2,1)} %get-tuple-element.55), channel_id=1, source_target_pairs={{0,8},{1,9},{2,10},{3,11},{4,12},{5,13},{6,14},{7,15},{8,0},{9,1},... | collective-permute-start | bytes 456200 | tf_op jit(solution)/shard_map/ppermute | solution.py:266
  152.2 5.4 %copy-start.11 = (bf16[24,3168]{1,0:T(8,128)(2,1)}, bf16[24,3168]{1,0:T(8,128)(2,1)S(1)}, u32[]{:S(2)}) copy-start(bf16[24,3168]{1,0:T(8,128)(2,1)S(1)} %collective-permute-done.13.refs_2_) | copy-start | bytes 456196
  152.2 5.4 %collective-permute-start.17 = (bf16[24,3168]{1,0:T(8,128)(2,1)}, bf16[24,3168]{1,0:T(8,128)(2,1)S(1)}, u32[]{:S(2)}, u32[]{:S(2)}) collective-permute-start(bf16[24,3168]{1,0:T(8,128)(2,1)} %get-tuple-element.56), channel_id=1, source_target_pairs={{0,12},{1,13},{2,14},{3,15},{4,0},{5,1},{6,2},{7,3},{8,4},{9,5},{1... | collective-permute-start | bytes 456200 | tf_op jit(solution)/shard_map/ppermute | solution.py:266
  153.1 4.5 %copy-start.12 = (bf16[24,3168]{1,0:T(8,128)(2,1)}, bf16[24,3168]{1,0:T(8,128)(2,1)S(1)}, u32[]{:S(2)}) copy-start(bf16[24,3168]{1,0:T(8,128)(2,1)S(1)} %collective-permute-done.14.refs_3_) | copy-start | bytes 456196
  160.7 6.5 %collective-permute-start.18 = (bf16[24,1584]{1,0:T(8,128)(2,1)}, bf16[24,1584]{1,0:T(8,128)(2,1)S(1)}, u32[]{:S(2)}, u32[]{:S(2)}) collective-permute-start(bf16[24,1584]{1,0:T(8,128)(2,1)} %get-tuple-element.58), channel_id=1, source_target_pairs={{0,16},{1,17},{2,18},{3,19},{4,20},{5,21},{6,22},{7,23},{8,24},{9,... | collective-permute-start | bytes 228104 | tf_op jit(solution)/shard_map/ppermute | solution.py:266
  160.8 7.2 %collective-permute-start.19 = (bf16[24,1584]{1,0:T(8,128)(2,1)}, bf16[24,1584]{1,0:T(8,128)(2,1)S(1)}, u32[]{:S(2)}, u32[]{:S(2)}) collective-permute-start(bf16[24,1584]{1,0:T(8,128)(2,1)} %get-tuple-element.59), channel_id=1, source_target_pairs={{0,2},{1,3},{2,0},{3,1},{4,6},{5,7},{6,4},{7,5},{8,10},{9,11},{10,... | collective-permute-start | bytes 228104 | tf_op jit(solution)/shard_map/ppermute | solution.py:266
  164.6 4.9 %collective-permute-start.20 = (bf16[24,1584]{1,0:T(8,128)(2,1)}, bf16[24,1584]{1,0:T(8,128)(2,1)S(1)}, u32[]{:S(2)}, u32[]{:S(2)}) collective-permute-start(bf16[24,1584]{1,0:T(8,128)(2,1)} %get-tuple-element.60), channel_id=1, source_target_pairs={{0,18},{1,19},{2,16},{3,17},{4,22},{5,23},{6,20},{7,21},{8,26},{9,... | collective-permute-start | bytes 228104 | tf_op jit(solution)/shard_map/ppermute | solution.py:266
  172.0 17.0 %copy-start.16 = (f32[24,792]{1,0:T(8,128)S(1)}, f32[24,792]{1,0:T(8,128)}, u32[]{:S(2)}) copy-start(f32[24,792]{1,0:T(8,128)} %get-tuple-element.61) | copy-start | bytes 228100
  172.0 17.0 %collective-permute-start.21 = (f32[24,792]{1,0:T(8,128)}, f32[24,792]{1,0:T(8,128)S(1)}, u32[]{:S(2)}, u32[]{:S(2)}) collective-permute-start(f32[24,792]{1,0:T(8,128)} %get-tuple-element.62), channel_id=1, source_target_pairs={{0,1},{1,0},{2,3},{3,2},{4,5},{5,4},{6,7},{7,6},{8,9},{9,8},{10,11... | collective-permute-start | bytes 228104 | tf_op jit(solution)/shard_map/ppermute | solution.py:246
  (13 other events, 18.7 us)

commit v4 on v3

--- a/solution.py
+++ b/solution.py
@@ -13,6 +13,8 @@
 F32 = jnp.float32
 BF16 = jnp.bfloat16
 ROW_ROW = (((1,), (1,)), ((), ()))
+
+LIMIT = 23 * 2**20
 
 
 def call(body, grid, ins, outs, shapes, scratch=(), flops=0, nbytes=0):
@@ -25,19 +27,29 @@
         scratch_shapes=list(scratch),
         cost_estimate=pl.CostEstimate(flops=flops, bytes_accessed=nbytes, transcendentals=0),
         compiler_params=pltpu.CompilerParams(
-            dimension_semantics=("arbitrary",) * len(grid), vmem_limit_bytes=56 * 2**20
+            dimension_semantics=("arbitrary",) * len(grid), vmem_limit_bytes=LIMIT
         ),
     )
 
 
 def whole(*shape):
-    return pl.BlockSpec(shape, lambda *at: (0,) * len(shape))
+    return pl.BlockSpec(shape, lambda *at: (0,) * len(shape), pipeline_mode=pl.Buffered(1))
+
+
+RESIDENT = pl.BlockSpec(memory_space=pltpu.VMEM)
 
 
 def from_behind(value, axis, steps):
     count = lax.axis_size(axis)
     first, last = (max(0, -steps), min(count, count - steps))
     return lax.ppermute(value, axis, [(source, source + steps) for source in range(first, last)])
+
+
+def own_place():
+    data, time = lax.axis_index("dp"), lax.axis_index("tm")
+    core = lax.rem(data, 2)
+    high = lax.rem(lax.div(data, 2), 2)
+    return lax.div(data, 4), lax.div(time, 2), high * 2 + lax.rem(time, 2), core
 
 
 def group_means(values):
@@ -68,7 +80,7 @@
         act_ref[frame] = (normed[frame] / (1.0 + jnp.exp(-normed[frame]))).astype(BF16)
 
 
-def up_body(cot_ref, weight_ref, local_ref, prior_ref):
+def up_body(cot_ref, weight_ref, ahead_ref, local_ref, prior_ref):
     channels = cot_ref.shape[-1]
     weight = weight_ref[...]
     parts = []
@@ -84,8 +96,10 @@
 
 
 def turn_body(weight_ref, out_ref):
+    step = pl.program_id(0)
     for tap in range(3):
-        out_ref[tap] = weight_ref[2 - tap].astype(F32).T.astype(BF16)
+        at = step * 3 + tap
+        out_ref[at] = weight_ref[26 - at].astype(F32).T.astype(BF16)
 
 
 def fill_shifts(frames, cols_ref, breadth):
@@ -119,7 +133,7 @@
     rows = acc_ref.shape[0]
     part = jnp.dot(
         cols_ref[pl.ds(pl.multiple_of(step * (rows // 2), rows // 2), rows), :],
-        weight_ref[0],
+        weight_ref[step],
         preferred_element_type=F32,
     )
 
@@ -194,7 +208,7 @@
 
 
 def make_weight_grad(breadth, times):
-    def body(side_ref, early_ref, late_ref, grad_ref, send_ref, keep_ref, cols_ref, turned_ref):
+    def body(early_ref, late_ref, grad_ref, send_ref, keep_ref, cols_ref, turned_ref):
         step = pl.program_id(0)
         rows, channels = early_ref.shape[1:]
 
@@ -217,13 +231,13 @@
                 cols_ref[pl.ds(start, 2 * rows), at : at + width],
                 preferred_element_type=F32,
             )
-            split_store(part, side_ref[0], send_ref, keep_ref, times, at)
+            split_store(part, own_place()[3], send_ref, keep_ref, times, at)
 
     return body
 
 
 def make_up_grad(times):
-    def body(side_ref, early_ref, late_ref, cot_ref, send_ref, keep_ref, cols_ref, turned_ref):
+    def body(early_ref, late_ref, cot_ref, send_ref, keep_ref, cols_ref, turned_ref):
         rows, channels = early_ref.shape[1:]
         frames = [early_ref[0], early_ref[1], late_ref[0], late_ref[1]]
         for tap in range(3):
@@ -237,7 +251,7 @@
                     half * channels : (half + 1) * channels, frame * rows : (frame + 1) * rows
                 ] = cot_ref[2 * frame + half].astype(F32).T.astype(BF16)
         part = jnp.dot(turned_ref[...], cols_ref[...], preferred_element_type=F32)
-        split_store(part, side_ref[0], send_ref, keep_ref, times, 0)
+        split_store(part, own_place()[3], send_ref, keep_ref, times, 0)
 
     return body
 
@@ -286,7 +300,7 @@
 def make_join(conv_rows, up_rows):
     widths = (conv_rows, up_rows, up_rows)
 
-    def body(place_ref, conv_got, conv_keep, up_got, up_keep, *refs):
+    def body(conv_got, conv_keep, up_got, up_keep, *refs):
         row_refs, col_refs, hold_ref = refs[:4], refs[4:8], refs[8]
         step = pl.program_id(0)
         conv = conv_got[0] + conv_keep[0]
@@ -299,9 +313,9 @@
         for at in range(4):
             hold_ref[at] = pick(full[0], widths, at, 4)
         for slot in range(4):
-            row_refs[slot][0] = hold_ref[lax.rem(place_ref[0] + slot, 4)]
-
-            @pl.when(lax.rem(step - place_ref[1] + 4, 4) == slot)
+            row_refs[slot][0] = hold_ref[lax.rem(own_place()[0] + slot, 4)]
+
+            @pl.when(lax.rem(step - own_place()[1] + 4, 4) == slot)
             def _():
                 col_refs[slot][...] = full[1]
 
@@ -311,7 +325,7 @@
 def make_mid(conv_rows, up_rows):
     widths = (conv_rows, up_rows, up_rows)
 
-    def body(place_ref, *refs):
+    def body(*refs):
         row_in, col_in, row_out, col_out = refs[:4], refs[4:8], refs[8:12], refs[12:16]
         row_hold, col_hold = refs[16:]
         row_hold[...] = added(row_in)
@@ -320,8 +334,8 @@
             col_hold[at] = pick(total, widths, at, 4)
         for slot in range(4):
             kind = row_out[slot].dtype
-            row_out[slot][...] = row_hold[lax.rem(place_ref[1] + slot, 4)].astype(kind)
-            col_out[slot][...] = col_hold[lax.rem(place_ref[0] + slot, 4)].astype(kind)
+            row_out[slot][...] = row_hold[lax.rem(own_place()[1] + slot, 4)].astype(kind)
+            col_out[slot][...] = col_hold[lax.rem(own_place()[0] + slot, 4)].astype(kind)
 
     return body
 
@@ -329,14 +343,14 @@
 def make_end(conv_rows, up_rows):
     widths = (conv_rows // 4, up_rows // 4, up_rows // 4)
 
-    def body(place_ref, *refs):
+    def body(*refs):
         outs, hold_ref = refs[8:12], refs[12]
         for low in range(2):
             total = added(refs[4 * low : 4 * low + 4])
             for high in range(2):
                 hold_ref[high * 2 + low] = pick(total, widths, high, 2)
         for slot in range(4):
-            outs[slot][...] = hold_ref[lax.rem(place_ref[2] + slot, 4)].astype(outs[slot].dtype)
+            outs[slot][...] = hold_ref[lax.rem(own_place()[2] + slot, 4)].astype(outs[slot].dtype)
 
     return body
 
@@ -344,35 +358,47 @@
 def make_last(conv_rows, up_rows):
     widths = (conv_rows // 8, up_rows // 8, up_rows // 8)
 
-    def body(place_ref, *refs):
+    def body(*refs):
         total = added(refs[:4])
         low, high = pick(total, widths, 0, 2), pick(total, widths, 1, 2)
-        refs[4][...] = jnp.where(place_ref[3] == 0, low, high)
-        refs[5][...] = jnp.where(place_ref[3] == 0, high, low)
-
-    return body
-
-
-def reduce_blocks(conv_send, conv_keep, up_send, up_keep):
+        refs[4][...] = jnp.where(own_place()[3] == 0, low, high)
+        refs[5][...] = jnp.where(own_place()[3] == 0, high, low)
+
+    return body
+
+
+def make_spread(conv_rows, up_rows, scale):
+    cut, part = conv_rows // 16, up_rows // 16
+
+    def body(mine_ref, got_ref, conv_ref, up_ref):
+        even = own_place()[3] == 0
+        mine, got = mine_ref[...], got_ref[...]
+        sides = jnp.where(even, mine, got), jnp.where(even, got, mine)
+        conv_ref[...] = jnp.concatenate([side[:, :cut] for side in sides], axis=0).T * scale
+        pieces = [
+            side[:, cut + at * part : cut + (at + 1) * part] for side in sides for at in range(2)
+        ]
+        up_ref[...] = jnp.concatenate(pieces, axis=0).T * scale
+
+    return body
+
+
+def reduce_blocks(conv_send, conv_keep, up_send, up_keep, scale):
     times, cols, conv_rows = conv_send.shape
     up_rows = up_send.shape[2]
     rows = conv_rows + 2 * up_rows
-    data, time = lax.axis_index("dp"), lax.axis_index("tm")
-    place = jnp.stack([data // 4, time // 2, (data // 2 % 2) * 2 + time % 2, data % 2])
-    place = place.astype(jnp.int32)
-    scalars = pl.BlockSpec(memory_space=pltpu.SMEM)
 
     def small(make, arrays, shapes, scratch):
         return call(
             make(conv_rows, up_rows),
             (1,),
-            [scalars] + [whole(*array.shape) for array in arrays],
+            [whole(*array.shape) for array in arrays],
             [whole(*shape.shape) for shape in shapes],
             shapes,
             scratch,
             flops=1000,
             nbytes=2 * times * cols * rows,
-        )(place, *arrays)
+        )(*arrays)
 
     def shape(*dims):
         return jax.ShapeDtypeStruct(dims, BF16)
@@ -390,14 +416,13 @@
     out = call(
         make_join(conv_rows, up_rows),
         (4,),
-        [scalars, conv_spec, conv_spec, up_spec, up_spec],
+        [conv_spec, conv_spec, up_spec, up_spec],
         [row_spec] * 4 + [whole(cols, rows)] * 4,
         [shape(4, cols, rows // 4)] * 4 + [shape(cols, rows)] * 4,
         [pltpu.VMEM((4, cols, rows // 4), BF16)],
         flops=1000,
         nbytes=6 * times * cols * rows,
     )(
-        place,
         conv_got.reshape(conv_blocks),
         conv_keep.reshape(conv_blocks),
         up_got.reshape(up_blocks),
@@ -415,19 +440,16 @@
     half = jax.ShapeDtypeStruct((cols, rows // 16), F32)
     mine, other = small(make_last, out, [half, half], [])
     got = swap_sides(other)
-    even = data % 2 == 0
-    low, high = jnp.where(even, mine, got), jnp.where(even, got, mine)
     cut, part = conv_rows // 16, up_rows // 16
-    grad_conv = jnp.concatenate([low[:, :cut], high[:, :cut]], axis=0).T
-    grad_up = jnp.concatenate(
+    return small(
+        lambda *sizes: make_spread(*sizes, scale),
+        [mine, got],
         [
-            side[:, cut + at * part : cut + (at + 1) * part]
-            for side in (low, high)
-            for at in range(2)
+            jax.ShapeDtypeStruct((cut, 2 * cols), F32),
+            jax.ShapeDtypeStruct((part, 4 * cols), F32),
         ],
-        axis=0,
-    ).T
-    return grad_conv, grad_up
+        [],
+    )
 
 
 def step(features, conv_weight, up_weight, cotangent):
@@ -438,7 +460,6 @@
     scale = 1.0 / math.sqrt(crops * frames * rows * times * data)
     field = features.reshape(frames, rows, channels)
     cot = cotangent.reshape(2 * frames, rows, channels)
-    side = (lax.axis_index("dp") % 2).astype(jnp.int32).reshape(1)
     block = (frames, rows, channels)
     square = 2 * channels * channels
     act = call(
@@ -454,19 +475,19 @@
     local, prior_part = call(
         up_body,
         (1,),
-        [whole(*cot.shape), whole(*up_weight.shape)],
+        [whole(*cot.shape), whole(*up_weight.shape), RESIDENT],
         [whole(*block), whole(*block)],
         [jax.ShapeDtypeStruct(block, F32), jax.ShapeDtypeStruct(block, BF16)],
         flops=6 * frames * rows * square,
         nbytes=10 * frames * rows * channels,
-    )(cot, up_weight)
+    )(cot, up_weight, conv_weight)
     next_part = from_behind(prior_part, "tm", -1)
     taps = conv_weight.reshape(27, channels, channels)
     turned = call(
         turn_body,
         (9,),
-        [pl.BlockSpec((3, channels, channels), lambda n: (8 - n, 0, 0))],
-        pl.BlockSpec((3, channels, channels), lambda n: (n, 0, 0)),
+        [RESIDENT],
+        RESIDENT,
         jax.ShapeDtypeStruct(taps.shape, BF16),
         flops=27 * square,
         nbytes=4 * 27 * channels * channels,
@@ -476,12 +497,10 @@
     conv_next = from_behind(conv_grad, "tm", -1)
     columns = pltpu.VMEM((4 * rows, 9 * channels), BF16)
     sums = pltpu.VMEM((frames * rows, channels), F32)
-    kernel_spec = pl.BlockSpec((1, 9 * channels, channels), lambda k: (k, 0, 0))
-    act_prior, turned = lax.optimization_barrier((act_prior, turned))
     hidden = call(
         make_conv(breadth),
         (3,),
-        [whole(*block), whole(*block), kernel_spec, whole(*block)],
+        [whole(*block), whole(*block), RESIDENT, whole(*block)],
         whole(*block),
         jax.ShapeDtypeStruct(block, BF16),
         [columns, sums],
@@ -495,18 +514,18 @@
     send, keep = call(
         make_weight_grad(breadth, times),
         (3,),
-        [pl.BlockSpec(memory_space=pltpu.SMEM), whole(*block), whole(*block), whole(*block)],
+        [whole(*block), whole(*block), whole(*block)],
         [half_spec, half_spec],
         [half, half],
         [columns, pltpu.VMEM((channels, frames * rows), BF16)],
         flops=27 * frames * rows * square,
         nbytes=4 * 27 * channels * channels,
-    )(side, act_prior, act, conv_grad)
+    )(act_prior, act, conv_grad)
     up_half = jax.ShapeDtypeStruct((times, channels // times, 3 * channels), BF16)
     up_send, up_keep = call(
         make_up_grad(times),
         (1,),
-        [pl.BlockSpec(memory_space=pltpu.SMEM), whole(*block), whole(*block), whole(*cot.shape)],
+        [whole(*block), whole(*block), whole(*cot.shape)],
         [whole(*up_half.shape), whole(*up_half.shape)],
         [up_half, up_half],
         [
@@ -515,13 +534,12 @@
         ],
         flops=6 * frames * rows * square,
         nbytes=12 * channels * channels,
-    )(side, hidden_prior, hidden, cot)
-    grad_conv, grad_up = reduce_blocks(send, keep, up_send, up_keep)
-    grad_conv, grad_up = grad_conv * scale, grad_up * scale
+    )(hidden_prior, hidden, cot)
+    grad_conv, grad_up = reduce_blocks(send, keep, up_send, up_keep, scale)
     features_grad = call(
         make_back(breadth),
         (3,),
-        [whole(*block), whole(*block), kernel_spec] + [whole(*block)] * 3,
+        [whole(*block), whole(*block), RESIDENT] + [whole(*block)] * 3,
         whole(*block),
         jax.ShapeDtypeStruct(block, BF16),
         [columns, sums],

time: 193 us -> 169 us (0.88)
  the two profiles are of different devices: /device:TPU:0 before, /device:TPU:9 now
where the time goes in v4:
time: 169 us
  waiting for transfers between devices  80.8 us (48%)
  Pallas kernels  45.1 us (27%)
  starting transfers between devices  34.9 us (21%)
  local copies, waits for them, and re-layouts  6.83 us (4%)
    ppermute x15, waiting for transfers between devices, exchange(): got.append(lax.ppermute(pieces[step], ('tm', 'dp'), pairs))  42.2 us
    ppermute x4, waiting for transfers between devices, from_behind(): lax.ppermute(value, axis, [(source, source + steps) for source in range(f...  36.5 us
    ppermute x15, starting transfers between devices, exchange(): got.append(lax.ppermute(pieces[step], ('tm', 'dp'), pairs))  14.7 us
    pallas_call x1, Pallas kernels, step(): call(make_back(breadth), (3,), [whole(*block), whole(*block), RESIDENT] +...  13.4 us
    ppermute x4, starting transfers between devices, from_behind(): lax.ppermute(value, axis, [(source, source + steps) for source in range(f...  12.8 us
    pallas_call x1, Pallas kernels, step(): call(make_conv(breadth), (3,), [whole(*block), whole(*block), RESIDENT, w...  10.4 us
    pallas_call x1, Pallas kernels, step(): call(make_weight_grad(breadth, times), (3,), [whole(*block), whole(*block...  9.7 us
    ppermute x3, starting transfers between devices, swap_sides(): lax.ppermute(value, 'dp', [(d, d ^ 1) for d in range(lax.axis_size('dp'))])  7.4 us
  transfers between devices with their start and end apart: 22, of which 11 were waited for; matrix products, arithmetic and copies ran while one was open for 0% of the time, Pallas kernels for 19%

profile of v4, /device:TPU:9, one launch (start us, length us, event | category | flops | bytes accessed | tf_op | source)
XLA Modules:
  0.0 168.6 jit_solution(15410587891864854672)
XLA Ops:
  0.6 3.3 %copy-done = bf16[10368,384]{1,0:T(8,128)(2,1)S(1)} copy-done((bf16[10368,384]{1,0:T(8,128)(2,1)S(1)}, bf16[10368,384]{1,0:T(8,128)(2,1)}, u32[]{:S(2)}) %copy-start) | copy-done | bytes 7962648
  3.9 1.5 copy-done.1
  5.4 1.3 copy-done.2
  6.6 1.7 %shard_map.67 = (f32[2,384,384]{2,1,0:T(8,128)S(1)}, bf16[2,384,384]{2,1,0:T(8,128)(2,1)S(1)}) custom-call(bf16[4,384,384]{2,1,0:T(8,128)(2,1)S(1)} %bitcast.17, bf16[1152,768]{1,0:T(8,128)(2,1)S(1)} %copy-done.1, bf16[10368,384]{1,0:T(8,128)(2,1)S(1)} %copy-done), custom_call_target="tpu_custom_call" | custom-call | flops 1358954496 | bytes 2949120 | tf_op jit(solution)/shard_map/pallas_call | solution.py:475
  8.4 3.4 %collective-permute-start = (bf16[2,384,384]{2,1,0:T(8,128)(2,1)S(1)}, bf16[2,384,384]{2,1,0:T(8,128)(2,1)S(1)}, u32[]{:S(2)}, u32[]{:S(2)}) collective-permute-start(bf16[2,384,384]{2,1,0:T(8,128)(2,1)S(1)} %get-tuple-element.34), channel_id=1, source_target_pairs={{16,0},{32,16},{48,32},{64,48},{80,64},{96,80},{112,96},{17,1},{33... | collective-permute-start | bytes 1769480 | tf_op jit(solution)/shard_map/ppermute | solution.py:45
  11.8 1.3 shard_map.70.late_ref
  13.2 2.0 %collective-permute-start.2 = (bf16[2,384,384]{2,1,0:T(8,128)(2,1)S(1)}, bf16[2,384,384]{2,1,0:T(8,128)(2,1)S(1)}, u32[]{:S(2)}, u32[]{:S(2)}) collective-permute-start(bf16[2,384,384]{2,1,0:T(8,128)(2,1)S(1)} %shard_map.70.late_ref), channel_id=1, source_target_pairs={{0,16},{16,32},{32,48},{48,64},{64,80},{80,96},{96,112},{1,17},{17... | collective-permute-start | bytes 1769480 | tf_op jit(solution)/shard_map/ppermute | solution.py:45
  15.2 22.3 %collective-permute-done.next_ref = bf16[2,384,384]{2,1,0:T(8,128)(2,1)S(1)} collective-permute-done((bf16[2,384,384]{2,1,0:T(8,128)(2,1)S(1)}, bf16[2,384,384]{2,1,0:T(8,128)(2,1)S(1)}, u32[]{:S(2)}, u32[]{:S(2)}) %collective-permute-start) | collective-permute-done | bytes 589856 | tf_op jit(solution)/shard_map/ppermute | solution.py:45
  38.5 9.7 %shard_map.71 = (bf16[8,24,10368]{2,1,0:T(8,128)(2,1)S(1)}, bf16[8,24,10368]{2,1,0:T(8,128)(2,1)S(1)}) custom-call(bf16[2,384,384]{2,1,0:T(8,128)(2,1)S(1)} %collective-permute-done.2.early_ref, bf16[2,384,384]{2,1,0:T(8,128)(2,1)S(1)} %shard_map.70.late_ref, bf16[2,384,384]{2,1,0:T(8,128)(2,1)S(1)} %add_convert_fusion.early_ref.grad_ref), custom_call_target="tpu_custom_call" | custom-call | flops 6115295232 | bytes 15925248 | tf_op jit(solution)/shard_map/pallas_call | solution.py:514
  48.8 10.4 %shard_map.72.late_ref = bf16[2,384,384]{2,1,0:T(8,128)(2,1)S(1)} custom-call(bf16[2,384,384]{2,1,0:T(8,128)(2,1)S(1)} %collective-permute-done.2.early_ref, bf16[2,384,384]{2,1,0:T(8,128)(2,1)S(1)} %shard_map.70.late_ref, bf16[3,3456,384]{2,1,0:T(8,128)(2,1)S(1)} %bitcast.12, bf16[2,384,384]{2,1,0:T(8,128)(2,1)S(1)} %bitcast.22), custom_call_target="tpu_custom_call" | custom-call | flops 6115295232 | bytes 7962624 | tf_op jit(solution)/shard_map/pallas_call | solution.py:500
  59.2 4.3 %collective-permute-start.4 = (bf16[2,384,384]{2,1,0:T(8,128)(2,1)S(1)}, bf16[2,384,384]{2,1,0:T(8,128)(2,1)S(1)}, u32[]{:S(2)}, u32[]{:S(2)}) collective-permute-start(bf16[2,384,384]{2,1,0:T(8,128)(2,1)S(1)} %shard_map.72.late_ref), channel_id=1, source_target_pairs={{0,16},{16,32},{32,48},{48,64},{64,80},{80,96},{96,112},{1,17},{17... | collective-permute-start | bytes 1769480 | tf_op jit(solution)/shard_map/ppermute | solution.py:45
  63.4 13.3 %collective-permute-done.4.early_ref = bf16[2,384,384]{2,1,0:T(8,128)(2,1)S(1)} collective-permute-done((bf16[2,384,384]{2,1,0:T(8,128)(2,1)S(1)}, bf16[2,384,384]{2,1,0:T(8,128)(2,1)S(1)}, u32[]{:S(2)}, u32[]{:S(2)}) %collective-permute-start.4) | collective-permute-done | bytes 589856 | tf_op jit(solution)/shard_map/ppermute | solution.py:45
  76.8 1.9 %shard_map.73 = (bf16[8,48,1152]{2,1,0:T(8,128)(2,1)S(1)}, bf16[8,48,1152]{2,1,0:T(8,128)(2,1)S(1)}) custom-call(bf16[2,384,384]{2,1,0:T(8,128)(2,1)S(1)} %collective-permute-done.4.early_ref, bf16[2,384,384]{2,1,0:T(8,128)(2,1)S(1)} %shard_map.72.late_ref, bf16[4,384,384]{2,1,0:T(8,128)(2,1)S(1)} %bitcast.18), custom_call_target="tpu_custom_call" | custom-call | flops 1358954496 | bytes 1769472 | tf_op jit(solution)/shard_map/pallas_call | solution.py:525
  79.7 2.1 %collective-permute-done.5 = bf16[8,48,1152]{2,1,0:T(8,128)(2,1)S(1)} collective-permute-done((bf16[8,48,1152]{2,1,0:T(8,128)(2,1)S(1)}, bf16[8,48,1152]{2,1,0:T(8,128)(2,1)S(1)}, u32[]{:S(2)}, u32[]{:S(2)}) %collective-permute-start.5) | collective-permute-done | bytes 884768 | tf_op jit(solution)/shard_map/ppermute | solution.py:260
  81.7 1.6 shard_map.74
  83.3 1.3 collective-permute-start.6
  84.6 2.5 %collective-permute-start.7 = (bf16[4,24,3168]{2,1,0:T(8,128)(2,1)S(1)}, bf16[4,24,3168]{2,1,0:T(8,128)(2,1)S(1)}, u32[]{:S(2)}, u32[]{:S(2)}) collective-permute-start(bf16[4,24,3168]{2,1,0:T(8,128)(2,1)S(1)} %get-tuple-element.41), channel_id=1, source_target_pairs={{0,8},{1,9},{2,10},{3,11},{4,12},{5,13},{6,14},{7,15},{8,0},{9,1},... | collective-permute-start | bytes 1824776 | tf_op jit(solution)/shard_map/ppermute | solution.py:280
  88.2 1.3 collective-permute-start.9
  90.3 9.4 %collective-permute-done.6.refs_1_ = bf16[4,24,3168]{2,1,0:T(8,128)(2,1)S(1)} collective-permute-done((bf16[4,24,3168]{2,1,0:T(8,128)(2,1)S(1)}, bf16[4,24,3168]{2,1,0:T(8,128)(2,1)S(1)}, u32[]{:S(2)}, u32[]{:S(2)}) %collective-permute-start.6) | collective-permute-done | bytes 608288 | tf_op jit(solution)/shard_map/ppermute | solution.py:280
  99.7 14.2 %collective-permute-done.7.refs_2_ = bf16[4,24,3168]{2,1,0:T(8,128)(2,1)S(1)} collective-permute-done((bf16[4,24,3168]{2,1,0:T(8,128)(2,1)S(1)}, bf16[4,24,3168]{2,1,0:T(8,128)(2,1)S(1)}, u32[]{:S(2)}, u32[]{:S(2)}) %collective-permute-start.7) | collective-permute-done | bytes 608288 | tf_op jit(solution)/shard_map/ppermute | solution.py:280
  113.8 3.1 %collective-permute-start.1 = (bf16[2,384,384]{2,1,0:T(8,128)(2,1)S(1)}, bf16[2,384,384]{2,1,0:T(8,128)(2,1)S(1)}, u32[]{:S(2)}, u32[]{:S(2)}) collective-permute-start(bf16[2,384,384]{2,1,0:T(8,128)(2,1)S(1)} %add_convert_fusion.early_ref.grad_ref), channel_id=1, source_target_pairs={{16,0},{32,16},{48,32},{64,48},{80,64},{96,80},{112,96},{17,1},{33... | collective-permute-start | bytes 1769480 | tf_op jit(solution)/shard_map/ppermute | solution.py:45
  116.9 2.8 %collective-permute-done.11.refs_7_ = bf16[24,12672]{1,0:T(8,128)(2,1)S(1)} collective-permute-done((bf16[24,12672]{1,0:T(8,128)(2,1)S(1)}, bf16[24,12672]{1,0:T(8,128)(2,1)S(1)}, u32[]{:S(2)}, u32[]{:S(2)}) %collective-permute-start.11) | collective-permute-done | bytes 608288 | tf_op jit(solution)/shard_map/ppermute | solution.py:280
  121.1 2.0 %collective-permute-start.14 = (bf16[24,3168]{1,0:T(8,128)(2,1)S(1)}, bf16[24,3168]{1,0:T(8,128)(2,1)S(1)}, u32[]{:S(2)}, u32[]{:S(2)}) collective-permute-start(bf16[24,3168]{1,0:T(8,128)(2,1)S(1)} %get-tuple-element.50), channel_id=1, source_target_pairs={{0,96},{1,97},{2,98},{3,99},{4,100},{5,101},{6,102},{7,103},{8,104... | collective-permute-start | bytes 456200 | tf_op jit(solution)/shard_map/ppermute | solution.py:280
  123.1 2.7 %collective-permute-done.12.refs_1_ = bf16[24,3168]{1,0:T(8,128)(2,1)S(1)} collective-permute-done((bf16[24,3168]{1,0:T(8,128)(2,1)S(1)}, bf16[24,3168]{1,0:T(8,128)(2,1)S(1)}, u32[]{:S(2)}, u32[]{:S(2)}) %collective-permute-start.12) | collective-permute-done | bytes 152096 | tf_op jit(solution)/shard_map/ppermute | solution.py:280
  125.8 8.8 %collective-permute-done.13.refs_2_ = bf16[24,3168]{1,0:T(8,128)(2,1)S(1)} collective-permute-done((bf16[24,3168]{1,0:T(8,128)(2,1)S(1)}, bf16[24,3168]{1,0:T(8,128)(2,1)S(1)}, u32[]{:S(2)}, u32[]{:S(2)}) %collective-permute-start.13) | collective-permute-done | bytes 152096 | tf_op jit(solution)/shard_map/ppermute | solution.py:280
  134.6 2.8 %collective-permute-done.14.refs_3_ = bf16[24,3168]{1,0:T(8,128)(2,1)S(1)} collective-permute-done((bf16[24,3168]{1,0:T(8,128)(2,1)S(1)}, bf16[24,3168]{1,0:T(8,128)(2,1)S(1)}, u32[]{:S(2)}, u32[]{:S(2)}) %collective-permute-start.14) | collective-permute-done | bytes 152096 | tf_op jit(solution)/shard_map/ppermute | solution.py:280
  137.4 1.6 collective-permute-done.17.refs_7_
  139.3 3.4 %collective-permute-start.19 = (bf16[24,1584]{1,0:T(8,128)(2,1)S(1)}, bf16[24,1584]{1,0:T(8,128)(2,1)S(1)}, u32[]{:S(2)}, u32[]{:S(2)}) collective-permute-start(bf16[24,1584]{1,0:T(8,128)(2,1)S(1)} %get-tuple-element.57), channel_id=1, source_target_pairs={{0,2},{1,3},{2,0},{3,1},{4,6},{5,7},{6,4},{7,5},{8,10},{9,11},{10,... | collective-permute-start | bytes 228104 | tf_op jit(solution)/shard_map/ppermute | solution.py:280
  142.7 2.0 %collective-permute-start.20 = (bf16[24,1584]{1,0:T(8,128)(2,1)S(1)}, bf16[24,1584]{1,0:T(8,128)(2,1)S(1)}, u32[]{:S(2)}, u32[]{:S(2)}) collective-permute-start(bf16[24,1584]{1,0:T(8,128)(2,1)S(1)} %get-tuple-element.58), channel_id=1, source_target_pairs={{0,18},{1,19},{2,16},{3,17},{4,22},{5,23},{6,20},{7,21},{8,26},{9,... | collective-permute-start | bytes 228104 | tf_op jit(solution)/shard_map/ppermute | solution.py:280
  144.7 2.8 %shard_map.68 = bf16[27,384,384]{2,1,0:T(8,128)(2,1)S(1)} custom-call(bf16[27,384,384]{2,1,0:T(8,128)(2,1)S(1)} %bitcast.13), custom_call_target="tpu_custom_call" | custom-call | flops 7962624 | bytes 15925248 | tf_op jit(solution)/shard_map/pallas_call | solution.py:486
  147.7 5.8 %collective-permute-start.21 = (f32[24,792]{1,0:T(8,128)S(1)}, f32[24,792]{1,0:T(8,128)S(1)}, u32[]{:S(2)}, u32[]{:S(2)}) collective-permute-start(f32[24,792]{1,0:T(8,128)S(1)} %get-tuple-element.60), channel_id=1, source_target_pairs={{0,1},{1,0},{2,3},{3,2},{4,5},{5,4},{6,7},{7,6},{8,9},{9,8},{10,11... | collective-permute-start | bytes 228104 | tf_op jit(solution)/shard_map/ppermute | solution.py:260
  153.5 13.4 %shard_map.69 = bf16[2,384,384]{2,1,0:T(8,128)(2,1)} custom-call(bf16[2,384,384]{2,1,0:T(8,128)(2,1)S(1)} %add_convert_fusion.early_ref.grad_ref, bf16[2,384,384]{2,1,0:T(8,128)(2,1)S(1)} %collective-permute-done.1.late_ref, bf16[3,3456,384]{2,1,0:T(8,128)(2,1)S(1)} %bitcast.14, bf16[2,384,384]{2,1,0:T(8,128)(2,1)S(1)} %bitcast.23, ...), custom_call_target="tpu_custom_call" | custom-call | flops 6115295232 | bytes 7962624 | tf_op jit(solution)/shard_map/pallas_call | solution.py:539
  (41 shorter events, 8.1 us)
Async XLA Ops:
  0.6 3.3 %copy-start = (bf16[10368,384]{1,0:T(8,128)(2,1)S(1)}, bf16[10368,384]{1,0:T(8,128)(2,1)}, u32[]{:S(2)}) copy-start(bf16[10368,384]{1,0:T(8,128)(2,1)} %ahead_ref.1) | copy-start | bytes 23887876
  3.9 1.5 copy-start.1
  5.4 1.3 copy-start.2
  6.6 5.2 %copy-start.4 = (bf16[1,2,16,24,384]{4,3,2,1,0:T(8,128)(2,1)S(1)}, bf16[1,2,16,24,384]{4,3,2,1,0:T(8,128)(2,1)}, u32[]{:S(2)}) copy-start(bf16[1,2,16,24,384]{4,3,2,1,0:T(8,128)(2,1)} %param.4) | copy-start | bytes 1769476
  8.4 29.1 %collective-permute-start = (bf16[2,384,384]{2,1,0:T(8,128)(2,1)S(1)}, bf16[2,384,384]{2,1,0:T(8,128)(2,1)S(1)}, u32[]{:S(2)}, u32[]{:S(2)}) collective-permute-start(bf16[2,384,384]{2,1,0:T(8,128)(2,1)S(1)} %get-tuple-element.34), channel_id=1, source_target_pairs={{16,0},{32,16},{48,32},{64,48},{80,64},{96,80},{112,96},{17,1},{33... | collective-permute-start | bytes 1769480 | tf_op jit(solution)/shard_map/ppermute | solution.py:45
  13.2 25.3 %collective-permute-start.2 = (bf16[2,384,384]{2,1,0:T(8,128)(2,1)S(1)}, bf16[2,384,384]{2,1,0:T(8,128)(2,1)S(1)}, u32[]{:S(2)}, u32[]{:S(2)}) collective-permute-start(bf16[2,384,384]{2,1,0:T(8,128)(2,1)S(1)} %shard_map.70.late_ref), channel_id=1, source_target_pairs={{0,16},{16,32},{32,48},{48,64},{64,80},{80,96},{96,112},{1,17},{17... | collective-permute-start | bytes 1769480 | tf_op jit(solution)/shard_map/ppermute | solution.py:45
  37.5 11.3 %slice-start = ((s8[7962624]{0:T(1024)(128)(4,1)}), s8[4194304]{0:T(1024)(128)(4,1)S(1)}, s32[]{:S(2)}) async-start(s8[7962624]{0:T(1024)(128)(4,1)} %bitcast.10), calls=%async_computation | async-start | bytes 8388608
  37.6 11.2 %slice-start.1 = ((s8[7962624]{0:T(1024)(128)(4,1)}), s8[3768320]{0:T(1024)(128)(4,1)S(1)}, s32[]{:S(2)}) async-start(s8[7962624]{0:T(1024)(128)(4,1)} %bitcast.10), calls=%async_computation.1 | async-start | bytes 7536640
  48.2 33.5 %collective-permute-start.3 = (bf16[8,24,10368]{2,1,0:T(8,128)(2,1)S(1)}, bf16[8,24,10368]{2,1,0:T(8,128)(2,1)S(1)}, u32[]{:S(2)}, u32[]{:S(2)}) collective-permute-start(bf16[8,24,10368]{2,1,0:T(8,128)(2,1)S(1)} %get-tuple-element.35), channel_id=1, source_target_pairs={{0,1},{1,0},{2,3},{3,2},{4,5},{5,4},{6,7},{7,6},{8,9},{9,8},{10,11... | collective-permute-start | bytes 11943944 | tf_op jit(solution)/shard_map/ppermute | solution.py:260
  48.8 28.0 %copy-start.3 = (bf16[1,4,16,24,384]{4,3,2,1,0:T(8,128)(2,1)S(1)}, bf16[1,4,16,24,384]{4,3,2,1,0:T(8,128)(2,1)}, u32[]{:S(2)}) copy-start(bf16[1,4,16,24,384]{4,3,2,1,0:T(8,128)(2,1)} %param.7) | copy-start | bytes 3538948
  59.2 17.6 %collective-permute-start.4 = (bf16[2,384,384]{2,1,0:T(8,128)(2,1)S(1)}, bf16[2,384,384]{2,1,0:T(8,128)(2,1)S(1)}, u32[]{:S(2)}, u32[]{:S(2)}) collective-permute-start(bf16[2,384,384]{2,1,0:T(8,128)(2,1)S(1)} %shard_map.72.late_ref), channel_id=1, source_target_pairs={{0,16},{16,32},{32,48},{48,64},{64,80},{80,96},{96,112},{1,17},{17... | collective-permute-start | bytes 1769480 | tf_op jit(solution)/shard_map/ppermute | solution.py:45
  78.7 3.0 %collective-permute-start.5 = (bf16[8,48,1152]{2,1,0:T(8,128)(2,1)S(1)}, bf16[8,48,1152]{2,1,0:T(8,128)(2,1)S(1)}, u32[]{:S(2)}, u32[]{:S(2)}) collective-permute-start(bf16[8,48,1152]{2,1,0:T(8,128)(2,1)S(1)} %get-tuple-element.37), channel_id=1, source_target_pairs={{0,1},{1,0},{2,3},{3,2},{4,5},{5,4},{6,7},{7,6},{8,9},{9,8},{10,11... | collective-permute-start | bytes 2654216 | tf_op jit(solution)/shard_map/ppermute | solution.py:260
  83.3 16.3 %collective-permute-start.6 = (bf16[4,24,3168]{2,1,0:T(8,128)(2,1)S(1)}, bf16[4,24,3168]{2,1,0:T(8,128)(2,1)S(1)}, u32[]{:S(2)}, u32[]{:S(2)}) collective-permute-start(bf16[4,24,3168]{2,1,0:T(8,128)(2,1)S(1)} %get-tuple-element.40), channel_id=1, source_target_pairs={{0,4},{1,5},{2,6},{3,7},{4,8},{5,9},{6,10},{7,11},{8,12},{9,13},{1... | collective-permute-start | bytes 1824776 | tf_op jit(solution)/shard_map/ppermute | solution.py:280
  84.6 29.2 %collective-permute-start.7 = (bf16[4,24,3168]{2,1,0:T(8,128)(2,1)S(1)}, bf16[4,24,3168]{2,1,0:T(8,128)(2,1)S(1)}, u32[]{:S(2)}, u32[]{:S(2)}) collective-permute-start(bf16[4,24,3168]{2,1,0:T(8,128)(2,1)S(1)} %get-tuple-element.41), channel_id=1, source_target_pairs={{0,8},{1,9},{2,10},{3,11},{4,12},{5,13},{6,14},{7,15},{8,0},{9,1},... | collective-permute-start | bytes 1824776 | tf_op jit(solution)/shard_map/ppermute | solution.py:280
  87.1 29.8 %collective-permute-start.8 = (bf16[4,24,3168]{2,1,0:T(8,128)(2,1)S(1)}, bf16[4,24,3168]{2,1,0:T(8,128)(2,1)S(1)}, u32[]{:S(2)}, u32[]{:S(2)}) collective-permute-start(bf16[4,24,3168]{2,1,0:T(8,128)(2,1)S(1)} %get-tuple-element.42), channel_id=1, source_target_pairs={{0,12},{1,13},{2,14},{3,15},{4,0},{5,1},{6,2},{7,3},{8,4},{9,5},{1... | collective-permute-start | bytes 1824776 | tf_op jit(solution)/shard_map/ppermute | solution.py:280
  88.2 28.7 %collective-permute-start.9 = (bf16[24,12672]{1,0:T(8,128)(2,1)S(1)}, bf16[24,12672]{1,0:T(8,128)(2,1)S(1)}, u32[]{:S(2)}, u32[]{:S(2)}) collective-permute-start(bf16[24,12672]{1,0:T(8,128)(2,1)S(1)} %get-tuple-element.44), channel_id=1, source_target_pairs={{0,32},{1,33},{2,34},{3,35},{4,36},{5,37},{6,38},{7,39},{8,40},{9,... | collective-permute-start | bytes 1824776 | tf_op jit(solution)/shard_map/ppermute | solution.py:280
  89.5 27.4 %collective-permute-start.10 = (bf16[24,12672]{1,0:T(8,128)(2,1)S(1)}, bf16[24,12672]{1,0:T(8,128)(2,1)S(1)}, u32[]{:S(2)}, u32[]{:S(2)}) collective-permute-start(bf16[24,12672]{1,0:T(8,128)(2,1)S(1)} %get-tuple-element.45), channel_id=1, source_target_pairs={{0,64},{1,65},{2,66},{3,67},{4,68},{5,69},{6,70},{7,71},{8,72},{9,... | collective-permute-start | bytes 1824776 | tf_op jit(solution)/shard_map/ppermute | solution.py:280
  99.7 20.0 %collective-permute-start.11 = (bf16[24,12672]{1,0:T(8,128)(2,1)S(1)}, bf16[24,12672]{1,0:T(8,128)(2,1)S(1)}, u32[]{:S(2)}, u32[]{:S(2)}) collective-permute-start(bf16[24,12672]{1,0:T(8,128)(2,1)S(1)} %get-tuple-element.46), channel_id=1, source_target_pairs={{0,96},{1,97},{2,98},{3,99},{4,100},{5,101},{6,102},{7,103},{8,104... | collective-permute-start | bytes 1824776 | tf_op jit(solution)/shard_map/ppermute | solution.py:280
  113.8 39.7 %collective-permute-start.1 = (bf16[2,384,384]{2,1,0:T(8,128)(2,1)S(1)}, bf16[2,384,384]{2,1,0:T(8,128)(2,1)S(1)}, u32[]{:S(2)}, u32[]{:S(2)}) collective-permute-start(bf16[2,384,384]{2,1,0:T(8,128)(2,1)S(1)} %add_convert_fusion.early_ref.grad_ref), channel_id=1, source_target_pairs={{16,0},{32,16},{48,32},{64,48},{80,64},{96,80},{112,96},{17,1},{33... | collective-permute-start | bytes 1769480 | tf_op jit(solution)/shard_map/ppermute | solution.py:45
  120.8 5.0 %collective-permute-start.12 = (bf16[24,3168]{1,0:T(8,128)(2,1)S(1)}, bf16[24,3168]{1,0:T(8,128)(2,1)S(1)}, u32[]{:S(2)}, u32[]{:S(2)}) collective-permute-start(bf16[24,3168]{1,0:T(8,128)(2,1)S(1)} %get-tuple-element.48), channel_id=1, source_target_pairs={{0,32},{1,33},{2,34},{3,35},{4,36},{5,37},{6,38},{7,39},{8,40},{9,... | collective-permute-start | bytes 456200 | tf_op jit(solution)/shard_map/ppermute | solution.py:280
  120.9 13.7 %collective-permute-start.13 = (bf16[24,3168]{1,0:T(8,128)(2,1)S(1)}, bf16[24,3168]{1,0:T(8,128)(2,1)S(1)}, u32[]{:S(2)}, u32[]{:S(2)}) collective-permute-start(bf16[24,3168]{1,0:T(8,128)(2,1)S(1)} %get-tuple-element.49), channel_id=1, source_target_pairs={{0,64},{1,65},{2,66},{3,67},{4,68},{5,69},{6,70},{7,71},{8,72},{9,... | collective-permute-start | bytes 456200 | tf_op jit(solution)/shard_map/ppermute | solution.py:280
  121.1 16.3 %collective-permute-start.14 = (bf16[24,3168]{1,0:T(8,128)(2,1)S(1)}, bf16[24,3168]{1,0:T(8,128)(2,1)S(1)}, u32[]{:S(2)}, u32[]{:S(2)}) collective-permute-start(bf16[24,3168]{1,0:T(8,128)(2,1)S(1)} %get-tuple-element.50), channel_id=1, source_target_pairs={{0,96},{1,97},{2,98},{3,99},{4,100},{5,101},{6,102},{7,103},{8,104... | collective-permute-start | bytes 456200 | tf_op jit(solution)/shard_map/ppermute | solution.py:280
  123.0 14.4 %collective-permute-start.15 = (bf16[24,3168]{1,0:T(8,128)(2,1)S(1)}, bf16[24,3168]{1,0:T(8,128)(2,1)S(1)}, u32[]{:S(2)}, u32[]{:S(2)}) collective-permute-start(bf16[24,3168]{1,0:T(8,128)(2,1)S(1)} %get-tuple-element.52), channel_id=1, source_target_pairs={{0,4},{1,5},{2,6},{3,7},{4,8},{5,9},{6,10},{7,11},{8,12},{9,13},{1... | collective-permute-start | bytes 456200 | tf_op jit(solution)/shard_map/ppermute | solution.py:280
  125.8 11.6 %collective-permute-start.16 = (bf16[24,3168]{1,0:T(8,128)(2,1)S(1)}, bf16[24,3168]{1,0:T(8,128)(2,1)S(1)}, u32[]{:S(2)}, u32[]{:S(2)}) collective-permute-start(bf16[24,3168]{1,0:T(8,128)(2,1)S(1)} %get-tuple-element.53), channel_id=1, source_target_pairs={{0,8},{1,9},{2,10},{3,11},{4,12},{5,13},{6,14},{7,15},{8,0},{9,1},... | collective-permute-start | bytes 456200 | tf_op jit(solution)/shard_map/ppermute | solution.py:280
  134.6 4.4 %collective-permute-start.17 = (bf16[24,3168]{1,0:T(8,128)(2,1)S(1)}, bf16[24,3168]{1,0:T(8,128)(2,1)S(1)}, u32[]{:S(2)}, u32[]{:S(2)}) collective-permute-start(bf16[24,3168]{1,0:T(8,128)(2,1)S(1)} %get-tuple-element.54), channel_id=1, source_target_pairs={{0,12},{1,13},{2,14},{3,15},{4,0},{5,1},{6,2},{7,3},{8,4},{9,5},{1... | collective-permute-start | bytes 456200 | tf_op jit(solution)/shard_map/ppermute | solution.py:280
  139.2 8.3 %collective-permute-start.18 = (bf16[24,1584]{1,0:T(8,128)(2,1)S(1)}, bf16[24,1584]{1,0:T(8,128)(2,1)S(1)}, u32[]{:S(2)}, u32[]{:S(2)}) collective-permute-start(bf16[24,1584]{1,0:T(8,128)(2,1)S(1)} %get-tuple-element.56), channel_id=1, source_target_pairs={{0,16},{1,17},{2,18},{3,19},{4,20},{5,21},{6,22},{7,23},{8,24},{9,... | collective-permute-start | bytes 228104 | tf_op jit(solution)/shard_map/ppermute | solution.py:280
  139.3 8.3 %collective-permute-start.19 = (bf16[24,1584]{1,0:T(8,128)(2,1)S(1)}, bf16[24,1584]{1,0:T(8,128)(2,1)S(1)}, u32[]{:S(2)}, u32[]{:S(2)}) collective-permute-start(bf16[24,1584]{1,0:T(8,128)(2,1)S(1)} %get-tuple-element.57), channel_id=1, source_target_pairs={{0,2},{1,3},{2,0},{3,1},{4,6},{5,7},{6,4},{7,5},{8,10},{9,11},{10,... | collective-permute-start | bytes 228104 | tf_op jit(solution)/shard_map/ppermute | solution.py:280
  142.7 4.8 %collective-permute-start.20 = (bf16[24,1584]{1,0:T(8,128)(2,1)S(1)}, bf16[24,1584]{1,0:T(8,128)(2,1)S(1)}, u32[]{:S(2)}, u32[]{:S(2)}) collective-permute-start(bf16[24,1584]{1,0:T(8,128)(2,1)S(1)} %get-tuple-element.58), channel_id=1, source_target_pairs={{0,18},{1,19},{2,16},{3,17},{4,22},{5,23},{6,20},{7,21},{8,26},{9,... | collective-permute-start | bytes 228104 | tf_op jit(solution)/shard_map/ppermute | solution.py:280
  147.7 19.2 %collective-permute-start.21 = (f32[24,792]{1,0:T(8,128)S(1)}, f32[24,792]{1,0:T(8,128)S(1)}, u32[]{:S(2)}, u32[]{:S(2)}) collective-permute-start(f32[24,792]{1,0:T(8,128)S(1)} %get-tuple-element.60), channel_id=1, source_target_pairs={{0,1},{1,0},{2,3},{3,2},{4,5},{5,4},{6,7},{7,6},{8,9},{9,8},{10,11... | collective-permute-start | bytes 228104 | tf_op jit(solution)/shard_map/ppermute | solution.py:260
